TPU v7x, 256 devices: a whole 4x4x8 slice. The times are simulated.
256 devices in a mesh: pipe: 8 (over x, y_lo), seq: 32 (over z, y_hi, core).
Axes of the slice: x: 4, y: 4 (y_hi: 2, y_lo: 2; y = y_hi * 2 + y_lo), z: 8, core: 2. Of those that a mesh axis runs over, the one named last changes fastest.
Arguments:
- latents: bfloat16 [2, 256, 1536], P(None, 'seq', 'pipe'), may hold values from -6 to 6
- timesteps: int32 [2, 2], replicated, may hold values from 0 to 15
- step_sizes: float32 [16], replicated, may hold values from 0.2 to 0.8
- mod_table: float32 [8, 16, 4608], P('pipe'), may hold values from -4 to 4
- qk_gain: float32 [8, 2, 128], P('pipe'), may hold values from 0.5 to 2
- w_query: bfloat16 [8, 1536, 1536], P('pipe'), may hold values from -0.15625 to 0.15625
- w_kv: bfloat16 [8, 1536, 3072], P('pipe', 'seq'), may hold values from -0.15625 to 0.15625
- w_out: bfloat16 [8, 1536, 1536], P('pipe'), may hold values from -0.15625 to 0.15625
Outputs:
- final_latents: bfloat16 [2, 256, 1536], P(None, 'seq', 'pipe')
All inputs are finite; a program needn't handle non-finite values.
Results may differ from a plain program's by a relative error of at most 0.025.
Values may be sent and summed in bfloat16 or wider, within the bound.
No kernel may reach another device: no remote copies, remote signals or barrier semaphores. Data moves between devices by JAX's collectives and lax.ppermute only.
A program may use at most 64 MiB of HBM per device.

v0:
```python
import math

import jax
import jax.numpy as jnp
from jax import lax
from jax.sharding import PartitionSpec as P

norm_eps = 1e-06


def passed_along(value, axis, steps):
    count = lax.axis_size(axis)
    pairs = [(source, (source + steps) % count) for source in range(count)]
    return lax.ppermute(value, axis, pairs)


def from_root(value, axis, source):
    kept = jnp.where(lax.axis_index(axis) == source, value, 0).astype(value.dtype)
    return lax.psum(kept, axis)


def rms_heads(values, gain_row):
    mean_square = jnp.mean(values * values, axis=-1, keepdims=True)
    return values * lax.rsqrt(mean_square + norm_eps) * gain_row


def modulate(hidden, shift_row, scale_row):
    as_float = hidden.astype(jnp.float32)
    center = jnp.mean(as_float, axis=-1, keepdims=True)
    spread = jnp.mean(jnp.square(as_float - center), axis=-1, keepdims=True)
    return (
        (as_float - center) * lax.rsqrt(spread + norm_eps) * (1.0 + scale_row) + shift_row
    ).astype(jnp.bfloat16)


def attend(queries, key_rows, value_rows, score_scale):
    logits = (
        jnp.einsum("qhd,khd->hqk", queries, key_rows, preferred_element_type=jnp.float32)
        * score_scale
    )
    weights_soft = jnp.exp(logits)
    running_sum = jnp.sum(weights_soft, axis=-1)
    weighted = jnp.einsum(
        "hqk,khd->hqd",
        weights_soft.astype(jnp.bfloat16),
        value_rows,
        preferred_element_type=jnp.float32,
    )
    return (running_sum, weighted)


def shards(latents, timesteps, step_sizes, mod_table, qk_gain, w_query, w_kv, w_out):
    n_pipe = lax.axis_size("pipe")
    segment_now = lax.axis_index("pipe")
    micro_count = latents.shape[0]
    row_count = latents.shape[1]
    feature_share = latents.shape[2]
    model_width = feature_share * n_pipe
    table_size = step_sizes.shape[0]
    inner_width = w_out.shape[1]
    head_dim = qk_gain.shape[2]
    head_count = inner_width // head_dim
    step_count = timesteps.shape[0]
    score_scale = 1.0 / math.sqrt(head_dim)
    slots = lax.all_gather(latents, "pipe", axis=2, tiled=True)
    kv_weight = lax.all_gather(w_kv, "seq", axis=1, tiled=True)[0]
    query_weight = w_query[0]
    out_weight = w_out[0]
    mod_rows = mod_table[0]
    gain_query = qk_gain[0, 0]
    gain_key = qk_gain[0, 1]

    def key_value(modded):
        projected = jnp.dot(modded, kv_weight, preferred_element_type=jnp.float32)
        projected = projected.reshape(modded.shape[0], 2, head_count, head_dim)
        key_rows = rms_heads(projected[:, 0], gain_key).astype(jnp.bfloat16)
        value_rows = projected[:, 1].astype(jnp.bfloat16)
        return (key_rows, value_rows)

    def apply_layer(hidden, time_index):
        one_hot = (jnp.arange(table_size, dtype=jnp.int32) == time_index).astype(jnp.float32)
        modulation = jnp.dot(one_hot, mod_rows, precision=lax.Precision.HIGHEST)
        shift_row = modulation[:model_width]
        scale_row = modulation[model_width : 2 * model_width]
        gate_row = modulation[2 * model_width :]
        modded = modulate(hidden, shift_row, scale_row)
        queries = jnp.dot(modded, query_weight, preferred_element_type=jnp.float32)
        queries = rms_heads(queries.reshape(row_count, head_count, head_dim), gain_query).astype(
            jnp.bfloat16
        )
        key_rows, value_rows = key_value(modded)
        running_sum, weighted = attend(
            queries,
            lax.all_gather(key_rows, "seq", axis=0, tiled=True),
            lax.all_gather(value_rows, "seq", axis=0, tiled=True),
            score_scale,
        )
        attended = (weighted / running_sum[..., None]).astype(jnp.bfloat16)
        attended = jnp.transpose(attended, (1, 0, 2)).reshape(row_count, inner_width)
        projected_out = jnp.dot(attended, out_weight, preferred_element_type=jnp.float32)
        return (hidden.astype(jnp.float32) + gate_row * projected_out).astype(jnp.bfloat16)

    def advance(tick_now, running):
        moving, latent_state = running
        offset = tick_now - segment_now
        step_now = jnp.floor_divide(offset, n_pipe)
        slot_now = jnp.mod(offset, n_pipe)
        is_live = (offset >= 0) & (slot_now < micro_count) & (step_now < step_count)
        slot_safe = jnp.clip(slot_now, 0, micro_count - 1)
        step_safe = jnp.clip(step_now, 0, step_count - 1)
        time_index = timesteps[step_safe, slot_safe]
        first_pass = (segment_now == 0) & (step_safe == 0)
        incoming = jnp.where(first_pass, slots[slot_safe], moving)
        layer_out = apply_layer(incoming, time_index)
        is_last = segment_now == n_pipe - 1
        one_hot = (jnp.arange(table_size, dtype=jnp.int32) == time_index).astype(jnp.float32)
        step_size = jnp.dot(one_hot, step_sizes, precision=lax.Precision.HIGHEST)
        previous = latent_state[slot_safe]
        update = (previous.astype(jnp.float32) - step_size * layer_out.astype(jnp.float32)).astype(
            jnp.bfloat16
        )
        new_state = jnp.where(
            is_last & is_live, latent_state.at[slot_safe].set(update), latent_state
        )
        outgoing = jnp.where(is_live, jnp.where(is_last, update, layer_out), incoming)
        moving = passed_along(outgoing, "pipe", 1)
        return (moving, new_state)

    tick_count = step_count * n_pipe + micro_count - 1
    moving = jnp.zeros((row_count, model_width), jnp.bfloat16)
    moving, latent_state = lax.fori_loop(0, tick_count, advance, (moving, slots))
    result_all = from_root(latent_state, "pipe", n_pipe - 1)
    return lax.dynamic_slice_in_dim(result_all, segment_now * feature_share, feature_share, 2)


def solution(mesh):
    in_specs = (
        P(None, "seq", "pipe"),
        P(),
        P(),
        P("pipe", None, None),
        P("pipe", None, None),
        P("pipe", None, None),
        P("pipe", "seq", None),
        P("pipe", None, None),
    )
    out_specs = P(None, "seq", "pipe")
    return jax.shard_map(shards, mesh=mesh, in_specs=in_specs, out_specs=out_specs, check_vma=False)
```

profile of v0, /device:TPU:1, one launch (start us, length us, event | category | flops | bytes accessed | tf_op | source)
XLA Modules:
  0.0 1923.2 jit_solution(12389518325979543403)
XLA Ops:
  8.1 25.9 %all_gather.26 = bf16[2,8,1536]{1,0,2:T(2,128)(2,1)S(1)} all-gather(bf16[2,8,192]{1,0,2:T(2,128)(2,1)S(1)} %copy.9), channel_id=1, replica_groups=mesh['pipe'=8,'seq'=32] {'pipe'}, dimensions={2}, use_global_device_ids=true | all-gather | bytes 55296 | tf_op jit(solution)/shard_map/all_gather | solution.py:65
  35.2 87.6 %all-gather.5.cloned.1.call-done = bf16[1,1536,3072]{2,1,0:T(8,128)(2,1)} async-done(((bf16[1,48,3072]{2,1,0:T(8,128)(2,1)}), bf16[1,1536,3072]{2,1,0:T(8,128)(2,1)}) %all-gather.5.cloned.1.call-update) | async-done | bytes 9437200 | tf_op jit(solution)/shard_map/all_gather | solution.py:66
  122.8 1767.8 %while.18 = (s32[]{:T(128)}, bf16[8,1536]{1,0:T(8,128)(2,1)S(1)}, bf16[2,8,1536]{2,1,0:T(8,128)(2,1)S(1)}, s32[]{:T(128)}, pred[]{:T(512)}, /*index=5*/s32[2,2]{...) while((s32[]{:T(128)}, bf16[8,1536]{1,0:T(8,128)(2,1)S(1)}, ...), condition=%wide.region_7.8_spmd, body=%wide.region_0.7_spmd.sunk | while | flops 165140176 | bytes 23390328 | solution.py:131
  126.3 5.0 fusion.70
  131.6 40.4 %all_gather.29 = bf16[256,12,128]{2,0,1:T(8,128)(2,1)S(1)} all-gather(bf16[8,12,128]{2,0,1:T(8,128)(2,1)S(1)} %multiply_convert_fusion.4), channel_id=1, replica_groups=mesh['pipe'=8,'seq'=32] {'seq'}, dimensions={0}, use_global_device_ids=true | all-gather | bytes 811008 | tf_op jit(solution)/shard_map/while/body/eval_jaxpr/all_gather | solution.py:94
  175.2 40.2 %all-gather.2 = bf16[256,1,12,128]{3,0,2,1:T(8,128)(2,1)S(1)} all-gather(bf16[8,1,12,128]{3,0,2,1:T(8,128)(2,1)S(1)} %slice.120), channel_id=2, replica_groups=mesh['pipe'=8,'seq'=32] {'seq'}, dimensions={0}, use_global_device_ids=true | all-gather | bytes 811008 | tf_op jit(solution)/shard_map/while/body/eval_jaxpr/all_gather | solution.py:95
  217.1 3.8 select_select_fusion.3
  229.2 5.0 fusion.70
  234.5 41.7 %all_gather.29 = bf16[256,12,128]{2,0,1:T(8,128)(2,1)S(1)} all-gather(bf16[8,12,128]{2,0,1:T(8,128)(2,1)S(1)} %multiply_convert_fusion.4), channel_id=1, replica_groups=mesh['pipe'=8,'seq'=32] {'seq'}, dimensions={0}, use_global_device_ids=true | all-gather | bytes 811008 | tf_op jit(solution)/shard_map/while/body/eval_jaxpr/all_gather | solution.py:94
  279.4 40.0 %all-gather.2 = bf16[256,1,12,128]{3,0,2,1:T(8,128)(2,1)S(1)} all-gather(bf16[8,1,12,128]{3,0,2,1:T(8,128)(2,1)S(1)} %slice.120), channel_id=2, replica_groups=mesh['pipe'=8,'seq'=32] {'seq'}, dimensions={0}, use_global_device_ids=true | all-gather | bytes 811008 | tf_op jit(solution)/shard_map/while/body/eval_jaxpr/all_gather | solution.py:95
  321.1 3.8 select_select_fusion.3
  333.2 5.0 fusion.70
  338.5 41.7 %all_gather.29 = bf16[256,12,128]{2,0,1:T(8,128)(2,1)S(1)} all-gather(bf16[8,12,128]{2,0,1:T(8,128)(2,1)S(1)} %multiply_convert_fusion.4), channel_id=1, replica_groups=mesh['pipe'=8,'seq'=32] {'seq'}, dimensions={0}, use_global_device_ids=true | all-gather | bytes 811008 | tf_op jit(solution)/shard_map/while/body/eval_jaxpr/all_gather | solution.py:94
  383.4 40.0 %all-gather.2 = bf16[256,1,12,128]{3,0,2,1:T(8,128)(2,1)S(1)} all-gather(bf16[8,1,12,128]{3,0,2,1:T(8,128)(2,1)S(1)} %slice.120), channel_id=2, replica_groups=mesh['pipe'=8,'seq'=32] {'seq'}, dimensions={0}, use_global_device_ids=true | all-gather | bytes 811008 | tf_op jit(solution)/shard_map/while/body/eval_jaxpr/all_gather | solution.py:95
  425.2 3.8 select_select_fusion.3
  437.3 5.0 fusion.70
  442.5 41.7 %all_gather.29 = bf16[256,12,128]{2,0,1:T(8,128)(2,1)S(1)} all-gather(bf16[8,12,128]{2,0,1:T(8,128)(2,1)S(1)} %multiply_convert_fusion.4), channel_id=1, replica_groups=mesh['pipe'=8,'seq'=32] {'seq'}, dimensions={0}, use_global_device_ids=true | all-gather | bytes 811008 | tf_op jit(solution)/shard_map/while/body/eval_jaxpr/all_gather | solution.py:94
  487.5 40.0 %all-gather.2 = bf16[256,1,12,128]{3,0,2,1:T(8,128)(2,1)S(1)} all-gather(bf16[8,1,12,128]{3,0,2,1:T(8,128)(2,1)S(1)} %slice.120), channel_id=2, replica_groups=mesh['pipe'=8,'seq'=32] {'seq'}, dimensions={0}, use_global_device_ids=true | all-gather | bytes 811008 | tf_op jit(solution)/shard_map/while/body/eval_jaxpr/all_gather | solution.py:95
  529.2 3.8 select_select_fusion.3
  541.3 5.0 fusion.70
  546.6 41.7 %all_gather.29 = bf16[256,12,128]{2,0,1:T(8,128)(2,1)S(1)} all-gather(bf16[8,12,128]{2,0,1:T(8,128)(2,1)S(1)} %multiply_convert_fusion.4), channel_id=1, replica_groups=mesh['pipe'=8,'seq'=32] {'seq'}, dimensions={0}, use_global_device_ids=true | all-gather | bytes 811008 | tf_op jit(solution)/shard_map/while/body/eval_jaxpr/all_gather | solution.py:94
  591.5 40.0 %all-gather.2 = bf16[256,1,12,128]{3,0,2,1:T(8,128)(2,1)S(1)} all-gather(bf16[8,1,12,128]{3,0,2,1:T(8,128)(2,1)S(1)} %slice.120), channel_id=2, replica_groups=mesh['pipe'=8,'seq'=32] {'seq'}, dimensions={0}, use_global_device_ids=true | all-gather | bytes 811008 | tf_op jit(solution)/shard_map/while/body/eval_jaxpr/all_gather | solution.py:95
  645.4 5.0 fusion.70
  650.7 41.7 %all_gather.29 = bf16[256,12,128]{2,0,1:T(8,128)(2,1)S(1)} all-gather(bf16[8,12,128]{2,0,1:T(8,128)(2,1)S(1)} %multiply_convert_fusion.4), channel_id=1, replica_groups=mesh['pipe'=8,'seq'=32] {'seq'}, dimensions={0}, use_global_device_ids=true | all-gather | bytes 811008 | tf_op jit(solution)/shard_map/while/body/eval_jaxpr/all_gather | solution.py:94
  695.6 40.0 %all-gather.2 = bf16[256,1,12,128]{3,0,2,1:T(8,128)(2,1)S(1)} all-gather(bf16[8,1,12,128]{3,0,2,1:T(8,128)(2,1)S(1)} %slice.120), channel_id=2, replica_groups=mesh['pipe'=8,'seq'=32] {'seq'}, dimensions={0}, use_global_device_ids=true | all-gather | bytes 811008 | tf_op jit(solution)/shard_map/while/body/eval_jaxpr/all_gather | solution.py:95
  749.4 5.0 fusion.70
  754.7 41.7 %all_gather.29 = bf16[256,12,128]{2,0,1:T(8,128)(2,1)S(1)} all-gather(bf16[8,12,128]{2,0,1:T(8,128)(2,1)S(1)} %multiply_convert_fusion.4), channel_id=1, replica_groups=mesh['pipe'=8,'seq'=32] {'seq'}, dimensions={0}, use_global_device_ids=true | all-gather | bytes 811008 | tf_op jit(solution)/shard_map/while/body/eval_jaxpr/all_gather | solution.py:94
  799.6 40.0 %all-gather.2 = bf16[256,1,12,128]{3,0,2,1:T(8,128)(2,1)S(1)} all-gather(bf16[8,1,12,128]{3,0,2,1:T(8,128)(2,1)S(1)} %slice.120), channel_id=2, replica_groups=mesh['pipe'=8,'seq'=32] {'seq'}, dimensions={0}, use_global_device_ids=true | all-gather | bytes 811008 | tf_op jit(solution)/shard_map/while/body/eval_jaxpr/all_gather | solution.py:95
  841.4 3.8 select_select_fusion.3
  853.5 5.0 fusion.70
  858.8 41.7 %all_gather.29 = bf16[256,12,128]{2,0,1:T(8,128)(2,1)S(1)} all-gather(bf16[8,12,128]{2,0,1:T(8,128)(2,1)S(1)} %multiply_convert_fusion.4), channel_id=1, replica_groups=mesh['pipe'=8,'seq'=32] {'seq'}, dimensions={0}, use_global_device_ids=true | all-gather | bytes 811008 | tf_op jit(solution)/shard_map/while/body/eval_jaxpr/all_gather | solution.py:94
  903.7 40.0 %all-gather.2 = bf16[256,1,12,128]{3,0,2,1:T(8,128)(2,1)S(1)} all-gather(bf16[8,1,12,128]{3,0,2,1:T(8,128)(2,1)S(1)} %slice.120), channel_id=2, replica_groups=mesh['pipe'=8,'seq'=32] {'seq'}, dimensions={0}, use_global_device_ids=true | all-gather | bytes 811008 | tf_op jit(solution)/shard_map/while/body/eval_jaxpr/all_gather | solution.py:95
  945.5 3.8 select_select_fusion.3
  957.6 5.0 fusion.70
  962.8 41.7 %all_gather.29 = bf16[256,12,128]{2,0,1:T(8,128)(2,1)S(1)} all-gather(bf16[8,12,128]{2,0,1:T(8,128)(2,1)S(1)} %multiply_convert_fusion.4), channel_id=1, replica_groups=mesh['pipe'=8,'seq'=32] {'seq'}, dimensions={0}, use_global_device_ids=true | all-gather | bytes 811008 | tf_op jit(solution)/shard_map/while/body/eval_jaxpr/all_gather | solution.py:94
  1007.8 40.0 %all-gather.2 = bf16[256,1,12,128]{3,0,2,1:T(8,128)(2,1)S(1)} all-gather(bf16[8,1,12,128]{3,0,2,1:T(8,128)(2,1)S(1)} %slice.120), channel_id=2, replica_groups=mesh['pipe'=8,'seq'=32] {'seq'}, dimensions={0}, use_global_device_ids=true | all-gather | bytes 811008 | tf_op jit(solution)/shard_map/while/body/eval_jaxpr/all_gather | solution.py:95
  1061.6 5.0 fusion.70
  1066.9 41.7 %all_gather.29 = bf16[256,12,128]{2,0,1:T(8,128)(2,1)S(1)} all-gather(bf16[8,12,128]{2,0,1:T(8,128)(2,1)S(1)} %multiply_convert_fusion.4), channel_id=1, replica_groups=mesh['pipe'=8,'seq'=32] {'seq'}, dimensions={0}, use_global_device_ids=true | all-gather | bytes 811008 | tf_op jit(solution)/shard_map/while/body/eval_jaxpr/all_gather | solution.py:94
  1111.8 40.0 %all-gather.2 = bf16[256,1,12,128]{3,0,2,1:T(8,128)(2,1)S(1)} all-gather(bf16[8,1,12,128]{3,0,2,1:T(8,128)(2,1)S(1)} %slice.120), channel_id=2, replica_groups=mesh['pipe'=8,'seq'=32] {'seq'}, dimensions={0}, use_global_device_ids=true | all-gather | bytes 811008 | tf_op jit(solution)/shard_map/while/body/eval_jaxpr/all_gather | solution.py:95
  1165.7 5.0 fusion.70
  1170.9 41.7 %all_gather.29 = bf16[256,12,128]{2,0,1:T(8,128)(2,1)S(1)} all-gather(bf16[8,12,128]{2,0,1:T(8,128)(2,1)S(1)} %multiply_convert_fusion.4), channel_id=1, replica_groups=mesh['pipe'=8,'seq'=32] {'seq'}, dimensions={0}, use_global_device_ids=true | all-gather | bytes 811008 | tf_op jit(solution)/shard_map/while/body/eval_jaxpr/all_gather | solution.py:94
  1215.9 40.0 %all-gather.2 = bf16[256,1,12,128]{3,0,2,1:T(8,128)(2,1)S(1)} all-gather(bf16[8,1,12,128]{3,0,2,1:T(8,128)(2,1)S(1)} %slice.120), channel_id=2, replica_groups=mesh['pipe'=8,'seq'=32] {'seq'}, dimensions={0}, use_global_device_ids=true | all-gather | bytes 811008 | tf_op jit(solution)/shard_map/while/body/eval_jaxpr/all_gather | solution.py:95
  1269.7 5.0 fusion.70
  1275.0 41.7 %all_gather.29 = bf16[256,12,128]{2,0,1:T(8,128)(2,1)S(1)} all-gather(bf16[8,12,128]{2,0,1:T(8,128)(2,1)S(1)} %multiply_convert_fusion.4), channel_id=1, replica_groups=mesh['pipe'=8,'seq'=32] {'seq'}, dimensions={0}, use_global_device_ids=true | all-gather | bytes 811008 | tf_op jit(solution)/shard_map/while/body/eval_jaxpr/all_gather | solution.py:94
  1319.9 40.0 %all-gather.2 = bf16[256,1,12,128]{3,0,2,1:T(8,128)(2,1)S(1)} all-gather(bf16[8,1,12,128]{3,0,2,1:T(8,128)(2,1)S(1)} %slice.120), channel_id=2, replica_groups=mesh['pipe'=8,'seq'=32] {'seq'}, dimensions={0}, use_global_device_ids=true | all-gather | bytes 811008 | tf_op jit(solution)/shard_map/while/body/eval_jaxpr/all_gather | solution.py:95
  1361.7 3.8 select_select_fusion.3
  1373.8 5.0 fusion.70
  1379.1 41.7 %all_gather.29 = bf16[256,12,128]{2,0,1:T(8,128)(2,1)S(1)} all-gather(bf16[8,12,128]{2,0,1:T(8,128)(2,1)S(1)} %multiply_convert_fusion.4), channel_id=1, replica_groups=mesh['pipe'=8,'seq'=32] {'seq'}, dimensions={0}, use_global_device_ids=true | all-gather | bytes 811008 | tf_op jit(solution)/shard_map/while/body/eval_jaxpr/all_gather | solution.py:94
  1424.0 40.0 %all-gather.2 = bf16[256,1,12,128]{3,0,2,1:T(8,128)(2,1)S(1)} all-gather(bf16[8,1,12,128]{3,0,2,1:T(8,128)(2,1)S(1)} %slice.120), channel_id=2, replica_groups=mesh['pipe'=8,'seq'=32] {'seq'}, dimensions={0}, use_global_device_ids=true | all-gather | bytes 811008 | tf_op jit(solution)/shard_map/while/body/eval_jaxpr/all_gather | solution.py:95
  1477.9 5.0 fusion.70
  1483.1 41.7 %all_gather.29 = bf16[256,12,128]{2,0,1:T(8,128)(2,1)S(1)} all-gather(bf16[8,12,128]{2,0,1:T(8,128)(2,1)S(1)} %multiply_convert_fusion.4), channel_id=1, replica_groups=mesh['pipe'=8,'seq'=32] {'seq'}, dimensions={0}, use_global_device_ids=true | all-gather | bytes 811008 | tf_op jit(solution)/shard_map/while/body/eval_jaxpr/all_gather | solution.py:94
  1528.0 40.0 %all-gather.2 = bf16[256,1,12,128]{3,0,2,1:T(8,128)(2,1)S(1)} all-gather(bf16[8,1,12,128]{3,0,2,1:T(8,128)(2,1)S(1)} %slice.120), channel_id=2, replica_groups=mesh['pipe'=8,'seq'=32] {'seq'}, dimensions={0}, use_global_device_ids=true | all-gather | bytes 811008 | tf_op jit(solution)/shard_map/while/body/eval_jaxpr/all_gather | solution.py:95
  1581.9 5.0 fusion.70
  1587.2 41.7 %all_gather.29 = bf16[256,12,128]{2,0,1:T(8,128)(2,1)S(1)} all-gather(bf16[8,12,128]{2,0,1:T(8,128)(2,1)S(1)} %multiply_convert_fusion.4), channel_id=1, replica_groups=mesh['pipe'=8,'seq'=32] {'seq'}, dimensions={0}, use_global_device_ids=true | all-gather | bytes 811008 | tf_op jit(solution)/shard_map/while/body/eval_jaxpr/all_gather | solution.py:94
  1632.1 40.0 %all-gather.2 = bf16[256,1,12,128]{3,0,2,1:T(8,128)(2,1)S(1)} all-gather(bf16[8,1,12,128]{3,0,2,1:T(8,128)(2,1)S(1)} %slice.120), channel_id=2, replica_groups=mesh['pipe'=8,'seq'=32] {'seq'}, dimensions={0}, use_global_device_ids=true | all-gather | bytes 811008 | tf_op jit(solution)/shard_map/while/body/eval_jaxpr/all_gather | solution.py:95
  1686.0 5.0 fusion.70
  1691.2 41.7 %all_gather.29 = bf16[256,12,128]{2,0,1:T(8,128)(2,1)S(1)} all-gather(bf16[8,12,128]{2,0,1:T(8,128)(2,1)S(1)} %multiply_convert_fusion.4), channel_id=1, replica_groups=mesh['pipe'=8,'seq'=32] {'seq'}, dimensions={0}, use_global_device_ids=true | all-gather | bytes 811008 | tf_op jit(solution)/shard_map/while/body/eval_jaxpr/all_gather | solution.py:94
  1736.2 40.0 %all-gather.2 = bf16[256,1,12,128]{3,0,2,1:T(8,128)(2,1)S(1)} all-gather(bf16[8,1,12,128]{3,0,2,1:T(8,128)(2,1)S(1)} %slice.120), channel_id=2, replica_groups=mesh['pipe'=8,'seq'=32] {'seq'}, dimensions={0}, use_global_device_ids=true | all-gather | bytes 811008 | tf_op jit(solution)/shard_map/while/body/eval_jaxpr/all_gather | solution.py:95
  1777.9 3.8 select_select_fusion.3
  1790.0 5.0 fusion.70
  1795.3 41.7 %all_gather.29 = bf16[256,12,128]{2,0,1:T(8,128)(2,1)S(1)} all-gather(bf16[8,12,128]{2,0,1:T(8,128)(2,1)S(1)} %multiply_convert_fusion.4), channel_id=1, replica_groups=mesh['pipe'=8,'seq'=32] {'seq'}, dimensions={0}, use_global_device_ids=true | all-gather | bytes 811008 | tf_op jit(solution)/shard_map/while/body/eval_jaxpr/all_gather | solution.py:94
  1840.2 40.0 %all-gather.2 = bf16[256,1,12,128]{3,0,2,1:T(8,128)(2,1)S(1)} all-gather(bf16[8,1,12,128]{3,0,2,1:T(8,128)(2,1)S(1)} %slice.120), channel_id=2, replica_groups=mesh['pipe'=8,'seq'=32] {'seq'}, dimensions={0}, use_global_device_ids=true | all-gather | bytes 811008 | tf_op jit(solution)/shard_map/while/body/eval_jaxpr/all_gather | solution.py:95
  1882.0 3.8 select_select_fusion.3
  1890.6 25.1 %psum.7 = bf16[2,8,1536]{2,1,0:T(8,128)(2,1)S(1)} all-reduce(bf16[2,8,1536]{2,1,0:T(8,128)(2,1)S(1)} %broadcast_select_fusion), channel_id=1, replica_groups=mesh['pipe'=8,'seq'=32] {'pipe'}, use_global_device_ids=true, to_apply=%region_8.9 | all-reduce | flops 24576 | bytes 98304 | tf_op jit(solution)/shard_map/psum | solution.py:19
  (425 shorter events, 260.2 us)
Async XLA Ops:
  6.5 116.3 %all-gather.5.cloned.1.call-start = ((), (), s32[]{:S(2)}) async-start(), calls=%async_computation | async-start | bytes 9732096 | tf_op jit(solution)/shard_map/all_gather | solution.py:66
  131.4 84.0 %copy-start.1 = (f32[16]{0:T(128)S(1)}, f32[16]{0:T(128)}, u32[]{:S(2)}) copy-start(f32[16]{0:T(128)} %get-tuple-element.577) | copy-start | bytes 196 | tf_op jit(solution)/shard_map/while
  175.2 46.2 %copy-start = (s32[3]{0:T(128)S(1)}, s32[3]{0:T(128)}, u32[]{:S(2)}) copy-start(s32[3]{0:T(128)} %get-tuple-element.593) | copy-start | bytes 40 | tf_op jit(solution)/shard_map/while
  220.9 4.8 collective-permute-start
  234.3 85.1 %copy-start.1 = (f32[16]{0:T(128)S(1)}, f32[16]{0:T(128)}, u32[]{:S(2)}) copy-start(f32[16]{0:T(128)} %get-tuple-element.577) | copy-start | bytes 196 | tf_op jit(solution)/shard_map/while
  279.4 45.6 %copy-start = (s32[3]{0:T(128)S(1)}, s32[3]{0:T(128)}, u32[]{:S(2)}) copy-start(s32[3]{0:T(128)} %get-tuple-element.593) | copy-start | bytes 40 | tf_op jit(solution)/shard_map/while
  324.9 4.8 collective-permute-start
  338.3 85.2 %copy-start.1 = (f32[16]{0:T(128)S(1)}, f32[16]{0:T(128)}, u32[]{:S(2)}) copy-start(f32[16]{0:T(128)} %get-tuple-element.577) | copy-start | bytes 196 | tf_op jit(solution)/shard_map/while
  383.4 45.7 %copy-start = (s32[3]{0:T(128)S(1)}, s32[3]{0:T(128)}, u32[]{:S(2)}) copy-start(s32[3]{0:T(128)} %get-tuple-element.593) | copy-start | bytes 40 | tf_op jit(solution)/shard_map/while
  429.0 4.8 collective-permute-start
  442.3 85.2 %copy-start.1 = (f32[16]{0:T(128)S(1)}, f32[16]{0:T(128)}, u32[]{:S(2)}) copy-start(f32[16]{0:T(128)} %get-tuple-element.577) | copy-start | bytes 196 | tf_op jit(solution)/shard_map/while
  487.5 45.7 %copy-start = (s32[3]{0:T(128)S(1)}, s32[3]{0:T(128)}, u32[]{:S(2)}) copy-start(s32[3]{0:T(128)} %get-tuple-element.593) | copy-start | bytes 40 | tf_op jit(solution)/shard_map/while
  533.0 4.8 collective-permute-start
  546.4 85.2 %copy-start.1 = (f32[16]{0:T(128)S(1)}, f32[16]{0:T(128)}, u32[]{:S(2)}) copy-start(f32[16]{0:T(128)} %get-tuple-element.577) | copy-start | bytes 196 | tf_op jit(solution)/shard_map/while
  591.5 45.7 %copy-start = (s32[3]{0:T(128)S(1)}, s32[3]{0:T(128)}, u32[]{:S(2)}) copy-start(s32[3]{0:T(128)} %get-tuple-element.593) | copy-start | bytes 40 | tf_op jit(solution)/shard_map/while
  637.1 4.8 collective-permute-start
  650.4 85.2 %copy-start.1 = (f32[16]{0:T(128)S(1)}, f32[16]{0:T(128)}, u32[]{:S(2)}) copy-start(f32[16]{0:T(128)} %get-tuple-element.577) | copy-start | bytes 196 | tf_op jit(solution)/shard_map/while
  695.6 45.7 %copy-start = (s32[3]{0:T(128)S(1)}, s32[3]{0:T(128)}, u32[]{:S(2)}) copy-start(s32[3]{0:T(128)} %get-tuple-element.593) | copy-start | bytes 40 | tf_op jit(solution)/shard_map/while
  741.1 4.8 collective-permute-start
  754.5 85.2 %copy-start.1 = (f32[16]{0:T(128)S(1)}, f32[16]{0:T(128)}, u32[]{:S(2)}) copy-start(f32[16]{0:T(128)} %get-tuple-element.577) | copy-start | bytes 196 | tf_op jit(solution)/shard_map/while
  799.6 45.7 %copy-start = (s32[3]{0:T(128)S(1)}, s32[3]{0:T(128)}, u32[]{:S(2)}) copy-start(s32[3]{0:T(128)} %get-tuple-element.593) | copy-start | bytes 40 | tf_op jit(solution)/shard_map/while
  845.2 4.8 collective-permute-start
  858.6 85.2 %copy-start.1 = (f32[16]{0:T(128)S(1)}, f32[16]{0:T(128)}, u32[]{:S(2)}) copy-start(f32[16]{0:T(128)} %get-tuple-element.577) | copy-start | bytes 196 | tf_op jit(solution)/shard_map/while
  903.7 45.7 %copy-start = (s32[3]{0:T(128)S(1)}, s32[3]{0:T(128)}, u32[]{:S(2)}) copy-start(s32[3]{0:T(128)} %get-tuple-element.593) | copy-start | bytes 40 | tf_op jit(solution)/shard_map/while
  949.3 4.8 collective-permute-start
  962.6 85.2 %copy-start.1 = (f32[16]{0:T(128)S(1)}, f32[16]{0:T(128)}, u32[]{:S(2)}) copy-start(f32[16]{0:T(128)} %get-tuple-element.577) | copy-start | bytes 196 | tf_op jit(solution)/shard_map/while
  1007.7 45.7 %copy-start = (s32[3]{0:T(128)S(1)}, s32[3]{0:T(128)}, u32[]{:S(2)}) copy-start(s32[3]{0:T(128)} %get-tuple-element.593) | copy-start | bytes 40 | tf_op jit(solution)/shard_map/while
  1053.3 4.8 collective-permute-start
  1066.7 85.2 %copy-start.1 = (f32[16]{0:T(128)S(1)}, f32[16]{0:T(128)}, u32[]{:S(2)}) copy-start(f32[16]{0:T(128)} %get-tuple-element.577) | copy-start | bytes 196 | tf_op jit(solution)/shard_map/while
  1111.8 45.7 %copy-start = (s32[3]{0:T(128)S(1)}, s32[3]{0:T(128)}, u32[]{:S(2)}) copy-start(s32[3]{0:T(128)} %get-tuple-element.593) | copy-start | bytes 40 | tf_op jit(solution)/shard_map/while
  1157.4 4.8 collective-permute-start
  1170.7 85.2 %copy-start.1 = (f32[16]{0:T(128)S(1)}, f32[16]{0:T(128)}, u32[]{:S(2)}) copy-start(f32[16]{0:T(128)} %get-tuple-element.577) | copy-start | bytes 196 | tf_op jit(solution)/shard_map/while
  1215.9 45.7 %copy-start = (s32[3]{0:T(128)S(1)}, s32[3]{0:T(128)}, u32[]{:S(2)}) copy-start(s32[3]{0:T(128)} %get-tuple-element.593) | copy-start | bytes 40 | tf_op jit(solution)/shard_map/while
  1261.4 4.8 collective-permute-start
  1274.8 85.2 %copy-start.1 = (f32[16]{0:T(128)S(1)}, f32[16]{0:T(128)}, u32[]{:S(2)}) copy-start(f32[16]{0:T(128)} %get-tuple-element.577) | copy-start | bytes 196 | tf_op jit(solution)/shard_map/while
  1319.9 45.7 %copy-start = (s32[3]{0:T(128)S(1)}, s32[3]{0:T(128)}, u32[]{:S(2)}) copy-start(s32[3]{0:T(128)} %get-tuple-element.593) | copy-start | bytes 40 | tf_op jit(solution)/shard_map/while
  1365.5 4.8 collective-permute-start
  1378.8 85.2 %copy-start.1 = (f32[16]{0:T(128)S(1)}, f32[16]{0:T(128)}, u32[]{:S(2)}) copy-start(f32[16]{0:T(128)} %get-tuple-element.577) | copy-start | bytes 196 | tf_op jit(solution)/shard_map/while
  1424.0 45.7 %copy-start = (s32[3]{0:T(128)S(1)}, s32[3]{0:T(128)}, u32[]{:S(2)}) copy-start(s32[3]{0:T(128)} %get-tuple-element.593) | copy-start | bytes 40 | tf_op jit(solution)/shard_map/while
  1469.5 4.8 collective-permute-start
  1482.9 85.2 %copy-start.1 = (f32[16]{0:T(128)S(1)}, f32[16]{0:T(128)}, u32[]{:S(2)}) copy-start(f32[16]{0:T(128)} %get-tuple-element.577) | copy-start | bytes 196 | tf_op jit(solution)/shard_map/while
  1528.0 45.7 %copy-start = (s32[3]{0:T(128)S(1)}, s32[3]{0:T(128)}, u32[]{:S(2)}) copy-start(s32[3]{0:T(128)} %get-tuple-element.593) | copy-start | bytes 40 | tf_op jit(solution)/shard_map/while
  1573.6 4.8 collective-permute-start
  1587.0 85.2 %copy-start.1 = (f32[16]{0:T(128)S(1)}, f32[16]{0:T(128)}, u32[]{:S(2)}) copy-start(f32[16]{0:T(128)} %get-tuple-element.577) | copy-start | bytes 196 | tf_op jit(solution)/shard_map/while
  1632.1 45.7 %copy-start = (s32[3]{0:T(128)S(1)}, s32[3]{0:T(128)}, u32[]{:S(2)}) copy-start(s32[3]{0:T(128)} %get-tuple-element.593) | copy-start | bytes 40 | tf_op jit(solution)/shard_map/while
  1677.7 4.8 collective-permute-start
  1691.0 85.2 %copy-start.1 = (f32[16]{0:T(128)S(1)}, f32[16]{0:T(128)}, u32[]{:S(2)}) copy-start(f32[16]{0:T(128)} %get-tuple-element.577) | copy-start | bytes 196 | tf_op jit(solution)/shard_map/while
  1736.1 45.7 %copy-start = (s32[3]{0:T(128)S(1)}, s32[3]{0:T(128)}, u32[]{:S(2)}) copy-start(s32[3]{0:T(128)} %get-tuple-element.593) | copy-start | bytes 40 | tf_op jit(solution)/shard_map/while
  1781.7 4.8 collective-permute-start
  1795.1 85.2 %copy-start.1 = (f32[16]{0:T(128)S(1)}, f32[16]{0:T(128)}, u32[]{:S(2)}) copy-start(f32[16]{0:T(128)} %get-tuple-element.577) | copy-start | bytes 196 | tf_op jit(solution)/shard_map/while
  1840.2 45.7 %copy-start = (s32[3]{0:T(128)S(1)}, s32[3]{0:T(128)}, u32[]{:S(2)}) copy-start(s32[3]{0:T(128)} %get-tuple-element.593) | copy-start | bytes 40 | tf_op jit(solution)/shard_map/while
  1885.8 4.8 collective-permute-start
Sparse Core Ops, SparseCore 0:
  10.1 112.6 all-gather.4
where the time goes:
time: 1930 us; the launch traced here: 1920 us
  blocking collectives  1440 us (75%)
  matrix products  243 us (13%)
  waiting for transfers between devices  135 us (7%)
  other arithmetic  64.2 us (3%)
  local copies, waits for them, and re-layouts  24.9 us (1%)
    all_gather x17, blocking collectives, apply_layer(): lax.all_gather(key_rows, 'seq', axis=0, tiled=True)  708 us
    all_gather x17, blocking collectives, apply_layer(): lax.all_gather(value_rows, 'seq', axis=0, tiled=True)  681 us
    all_gather x1, waiting for transfers between devices, shards(): kv_weight = lax.all_gather(w_kv, 'seq', axis=1, tiled=True)[0]  87.6 us
    dot_general x17, matrix products, key_value(): projected = jnp.dot(modded, kv_weight, preferred_element_type=jnp.float32)  85.8 us
    dot_general x17, matrix products, apply_layer(): jnp.dot(attended, out_weight, preferred_element_type=jnp.float32)  64.6 us
    dot_general x17, matrix products, apply_layer(): queries = jnp.dot(modded, query_weight, preferred_element_type=jnp.float32)  53.9 us
    ppermute x17, waiting for transfers between devices, passed_along(): return lax.ppermute(value, axis, pairs)  46.4 us
  transfers between devices with their start and end apart: 18, of which 18 were waited for; matrix products, arithmetic and copies ran while one was open for 2% of the time, Pallas kernels for 0%

commit v1 on v0

v1 whole, which is shorter than its diff:
```python
import math

import jax
import jax.numpy as jnp
from jax import lax
from jax.experimental import pallas as pl
from jax.experimental.pallas import tpu as pltpu
from jax.sharding import PartitionSpec as P

norm_eps = 1e-06


def layer_front(head_dim):
    score_scale = 1.0 / math.sqrt(head_dim)

    def body(core_ref, own_ref, other_ref, mod_ref, gain_ref, wq_ref, wkv_ref, out_ref):
        core = core_ref[0]
        half = own_ref.shape[1]
        width = 2 * half
        near = pl.multiple_of(core * half, half)
        far = pl.multiple_of((1 - core) * half, half)
        own = own_ref[...].astype(jnp.float32)
        other = other_ref[...].astype(jnp.float32)
        center = (
            jnp.sum(own, axis=-1, keepdims=True) + jnp.sum(other, axis=-1, keepdims=True)
        ) / width
        own = own - center
        other = other - center
        spread = (
            jnp.sum(own * own, axis=-1, keepdims=True)
            + jnp.sum(other * other, axis=-1, keepdims=True)
        ) / width
        inverse = lax.rsqrt(spread + norm_eps)

        def modulated(values, at):
            shift_row = mod_ref[pl.ds(at, 1), :]
            scale_row = mod_ref[pl.ds(2 + at, 1), :]
            return (values * inverse * (1.0 + scale_row) + shift_row).astype(jnp.bfloat16)

        own = modulated(own, core)
        other = modulated(other, 1 - core)

        def project(weight_ref, start, size):
            cols = pl.ds(start, size)
            return jnp.dot(
                own, weight_ref[pl.ds(near, half), cols], preferred_element_type=jnp.float32
            ) + jnp.dot(
                other, weight_ref[pl.ds(far, half), cols], preferred_element_type=jnp.float32
            )

        def rms(values, gain_row):
            mean_square = jnp.mean(values * values, axis=-1, keepdims=True)
            return (values * lax.rsqrt(mean_square + norm_eps) * gain_row).astype(jnp.bfloat16)

        gain_query = gain_ref[0:1, :]
        gain_key = gain_ref[1:2, :]
        group = 2 * head_dim
        for start in range(0, half, group):
            queries = project(wq_ref, start, group)
            keys = project(wkv_ref, start, group)
            values = project(wkv_ref, half + start, group).astype(jnp.bfloat16)
            for at in range(0, group, head_dim):
                query_head = rms(queries[:, at : at + head_dim], gain_query)
                key_head = rms(keys[:, at : at + head_dim], gain_key)
                logits = (
                    lax.dot_general(
                        query_head,
                        key_head,
                        (((1,), (1,)), ((), ())),
                        preferred_element_type=jnp.float32,
                    )
                    * score_scale
                )
                weights = jnp.exp(logits)
                total = jnp.sum(weights, axis=-1, keepdims=True)
                mixed = jnp.dot(
                    weights.astype(jnp.bfloat16),
                    values[:, at : at + head_dim],
                    preferred_element_type=jnp.float32,
                )
                out_ref[:, start + at : start + at + head_dim] = (mixed / total).astype(
                    jnp.bfloat16
                )

    return body


def layer_back(core_ref, own_ref, other_ref, hidden_ref, mod_ref, wo_ref, out_ref):
    core = core_ref[0]
    half = own_ref.shape[1]
    near = pl.multiple_of(core * half, half)
    far = pl.multiple_of((1 - core) * half, half)
    projected = jnp.dot(
        own_ref[...], wo_ref[pl.ds(near, half), :], preferred_element_type=jnp.float32
    ) + jnp.dot(other_ref[...], wo_ref[pl.ds(far, half), :], preferred_element_type=jnp.float32)
    gate_row = mod_ref[pl.ds(4 + core, 1), :]
    out_ref[...] = (hidden_ref[...].astype(jnp.float32) + gate_row * projected).astype(jnp.bfloat16)


def shards(latents, timesteps, step_sizes, mod_table, qk_gain, w_query, w_kv, w_out):
    n_pipe = lax.axis_size("pipe")
    n_seq = lax.axis_size("seq")
    pipe_at = lax.axis_index("pipe")
    seq_at = lax.axis_index("seq")
    core = seq_at % 2
    micro = (seq_at // 2) % 2
    micro_count, row_share, feature_share = latents.shape
    step_count = timesteps.shape[0]
    tokens = row_share * n_seq
    width = feature_share * n_pipe
    half = width // 2
    head_dim = qk_gain.shape[2]
    core_pairs = [(at, at ^ 1) for at in range(n_seq)]
    quads = [[4 * at + j for j in range(4)] for at in range(n_seq // 4)]

    def swapped(value):
        return lax.ppermute(value, "seq", core_pairs)

    def columns(value, side, axis):
        return lax.dynamic_slice_in_dim(value, side * half, half, axis)

    pair = w_kv[0].reshape(w_kv.shape[1], 2, half * 2)
    mine = columns(pair, core, 2)
    theirs = swapped(columns(pair, 1 - core, 2))
    mine = mine.reshape(mine.shape[0], width)
    theirs = theirs.reshape(mine.shape)
    low = jnp.where(core == 0, mine, theirs)
    high = jnp.where(core == 0, theirs, mine)
    block = jnp.concatenate([low, high], axis=0)
    theirs = lax.ppermute(block, "seq", [(at, at ^ 2) for at in range(n_seq)])
    low = jnp.where(micro == 0, block, theirs)
    high = jnp.where(micro == 0, theirs, block)
    block = jnp.concatenate([low, high], axis=0)
    block_rows = block.shape[0]
    ring = n_seq // 4
    place = seq_at // 4
    rings = [[(at, (at + turn) % n_seq) for at in range(n_seq)] for turn in (4, -4)]
    kv_half = jnp.zeros((ring * block_rows, width), jnp.bfloat16)

    def placed(whole, part, at):
        return lax.dynamic_update_slice_in_dim(whole, part, ((place + at) % ring) * block_rows, 0)

    kv_half = placed(kv_half, block, 0)
    rising = falling = block
    for turn in range(1, ring // 2 + 1):
        rising = lax.ppermute(rising, "seq", rings[0])
        kv_half = placed(kv_half, rising, ring - turn)
        if turn < ring - turn:
            falling = lax.ppermute(falling, "seq", rings[1])
            kv_half = placed(kv_half, falling, turn)
    query_half = columns(w_query[0], core, 1)
    out_half = columns(w_out[0], core, 1)
    core_word = core.astype(jnp.int32).reshape(1)

    taus = lax.dynamic_index_in_dim(timesteps, micro, 1, keepdims=False)
    mods = [
        lax.dynamic_index_in_dim(mod_table[0], taus[at], 0, keepdims=False).reshape(6, half)
        for at in range(step_count)
    ]
    first_size = lax.dynamic_index_in_dim(step_sizes, taus[0], 0, keepdims=False)
    last_sizes = jnp.stack([step_sizes[timesteps[step_count - 1, at]] for at in range(micro_count)])

    sent = jnp.broadcast_to(latents[None], (n_pipe,) + latents.shape)
    rows = lax.all_to_all(sent, "pipe", 0, 0, tiled=True)
    rows = jnp.transpose(rows, (1, 2, 0, 3)).reshape(micro_count, row_share, 2, half)
    sent = jnp.transpose(rows, (0, 2, 1, 3)).reshape(1, 4, row_share, half)
    sent = jnp.broadcast_to(sent, (n_seq // 4, 4, row_share, half)).reshape(
        n_seq, row_share, half
    )
    slot = lax.all_to_all(sent, "seq", 0, 0, tiled=True).reshape(tokens, half)

    smem = pl.BlockSpec(memory_space=pltpu.SMEM)
    vmem = pl.BlockSpec(memory_space=pltpu.VMEM)
    front = pl.pallas_call(
        layer_front(head_dim),
        out_shape=jax.ShapeDtypeStruct((tokens, half), jnp.bfloat16),
        in_specs=[smem] + [vmem] * 6,
        out_specs=vmem,
        compiler_params=pltpu.CompilerParams(vmem_limit_bytes=32 << 20),
        name="front",
    )
    back = pl.pallas_call(
        layer_back,
        out_shape=jax.ShapeDtypeStruct((tokens, half), jnp.bfloat16),
        in_specs=[smem] + [vmem] * 5,
        out_specs=vmem,
        compiler_params=pltpu.CompilerParams(vmem_limit_bytes=16 << 20),
        name="back",
    )

    hidden = slot
    for tick in range(step_count * n_pipe):
        step = tick // n_pipe
        if tick > 0:
            hidden = lax.ppermute(hidden, "pipe", [((tick - 1) % n_pipe, tick % n_pipe)])
        if tick > 0 and tick % n_pipe == 0:
            slot = (
                slot.astype(jnp.float32) - first_size * hidden.astype(jnp.float32)
            ).astype(jnp.bfloat16)
            hidden = slot
        attended = front(
            core_word, hidden, swapped(hidden), mods[step], qk_gain[0], query_half, kv_half
        )
        hidden = back(core_word, attended, swapped(attended), hidden, mods[step], out_half)

    kept = jnp.where(pipe_at == 0, slot, hidden)
    kept = lax.dynamic_slice_in_dim(kept, (seq_at // 4) * 4 * row_share, 4 * row_share, 0)
    kept = kept.reshape(4, row_share, half)
    kept = lax.all_to_all(kept, "seq", 0, 0, tiled=True, axis_index_groups=quads)
    kept = kept.reshape(micro_count, 2, row_share, n_pipe // 2, feature_share)
    sent = jnp.transpose(kept, (1, 3, 0, 2, 4)).reshape(
        n_pipe, micro_count, row_share, feature_share
    )
    got = lax.all_to_all(sent, "pipe", 0, 0, tiled=True).astype(jnp.float32)
    return (got[0] - last_sizes[:, None, None] * got[n_pipe - 1]).astype(jnp.bfloat16)


def solution(mesh):
    in_specs = (
        P(None, "seq", "pipe"),
        P(),
        P(),
        P("pipe", None, None),
        P("pipe", None, None),
        P("pipe", None, None),
        P("pipe", "seq", None),
        P("pipe", None, None),
    )
    out_specs = P(None, "seq", "pipe")
    return jax.shard_map(shards, mesh=mesh, in_specs=in_specs, out_specs=out_specs, check_vma=False)
```

time: 1930 us -> 494 us (0.26)
  blocking collectives: 1440 us -> 19.8 us
  matrix products: 243 us -> 0 us
  starting transfers between devices: 1.35 us -> 128 us
  Pallas kernels: 0 us -> 117 us
  other arithmetic: 64.2 us -> 5.04 us
  waiting for transfers between devices: 135 us -> 185 us
    all_gather x35 -> x0, blocking collectives: 1420 us -> none  [the longest x17 708 us: apply_layer(): lax.all_gather(key_rows, 'seq', axis=0, tiled=True)]
    dot_general x85 -> x0, matrix products: 243 us -> none  [the longest x17 85.8 us: key_value(): projected = jnp.dot(modded, kv_weight, preferred_element_type=jnp.float32)]
    ppermute x17 -> x56, waiting for transfers between devices: 46.4 us -> 181 us  [the longest x15 91 us: shards(): lax.ppermute(hidden, 'pipe', [((tick - 1) % n_pipe, tick % n_pipe)])]
    pallas_call x0 -> x32, Pallas kernels: none -> 117 us  [the longest x16 103 us: shards(): front(core_word, hidden, swapped(hidden), mods[step], qk_gain[0], query_h...]
    all_gather x1 -> x0, waiting for transfers between devices: 87.6 us -> none  [shards(): kv_weight = lax.all_gather(w_kv, 'seq', axis=1, tiled=True)[0]]
    all_to_all x0 -> x2, starting transfers between devices: none -> 83.7 us  [the longest x1 70.7 us: shards(): got = lax.all_to_all(sent, 'pipe', 0, 0, tiled=True).astype(jnp.float32)]
    ppermute x17 -> x56, starting transfers between devices: 1.35 us -> 44.6 us  [the longest x33 23.2 us: swapped(): return lax.ppermute(value, 'seq', core_pairs)]
    psum x1 -> x0, blocking collectives: 25.1 us -> none  [from_root(): return lax.psum(kept, axis)]
  transfers between devices with their start and end apart: 18 -> 58, of which waited for: 18 -> 42; matrix products, arithmetic and copies ran while one was open for 2% -> 4% of each run, Pallas kernels for 0% -> 0%
where the time goes in v1:
time: 494 us; the launch traced here: 486 us
  waiting for transfers between devices  185 us (37%)
  starting transfers between devices  128 us (26%)
  Pallas kernels  117 us (24%)
  local copies, waits for them, and re-layouts  22.7 us (5%)
  blocking collectives  19.8 us (4%)
  between operations  8.32 us (2%)
  other arithmetic  5.04 us (1%)
    pallas_call x16, Pallas kernels, shards(): front(core_word, hidden, swapped(hidden), mods[step], qk_gain[0], query_h...  103 us
    ppermute x15, waiting for transfers between devices, shards(): lax.ppermute(hidden, 'pipe', [((tick - 1) % n_pipe, tick % n_pipe)])  91 us
    all_to_all x1, starting transfers between devices, shards(): got = lax.all_to_all(sent, 'pipe', 0, 0, tiled=True).astype(jnp.float32)  70.7 us
    ppermute x33, waiting for transfers between devices, swapped(): return lax.ppermute(value, 'seq', core_pairs)  42.6 us
    ppermute x33, starting transfers between devices, swapped(): return lax.ppermute(value, 'seq', core_pairs)  23.2 us
    ppermute x3, waiting for transfers between devices, shards(): falling = lax.ppermute(falling, 'seq', rings[1])  22.3 us
    ppermute x4, waiting for transfers between devices, shards(): rising = lax.ppermute(rising, 'seq', rings[0])  16.5 us
    pallas_call x16, Pallas kernels, shards(): back(core_word, attended, swapped(attended), hidden, mods[step], out_half)  13.7 us
  transfers between devices with their start and end apart: 58, of which 42 were waited for; matrix products, arithmetic and copies ran while one was open for 4% of the time, Pallas kernels for 0%

profile of v1, /device:TPU:1, one launch (start us, length us, event | category | flops | bytes accessed | tf_op | source)
XLA Modules:
  0.0 486.1 jit_solution(6128306356537074063)
XLA Ops:
  1.3 3.3 collective-permute-start.1
  7.2 8.6 %collective-permute-done.2 = bf16[96,1536]{1,0:T(8,128)(2,1)S(1)} collective-permute-done((bf16[96,1536]{1,0:T(8,128)(2,1)S(1)}, bf16[96,1536]{1,0:T(8,128)(2,1)S(1)}, u32[]{:S(2)}, u32[]{:S(2)}) %collective-permute-start.2) | collective-permute-done | bytes 294944 | tf_op jit(solution)/shard_map/ppermute | solution.py:130
  15.9 2.5 broadcast_in_dim.20
  19.5 9.9 %all_to_all.20 = bf16[8,2,8,192]{3,2,1,0:T(8,128)(2,1)S(1)} all-to-all(bf16[8,2,8,192]{3,2,1,0:T(8,128)(2,1)S(1)} %broadcast_in_dim.8), channel_id=1, replica_groups=mesh['pipe'=8,'seq'=32] {'pipe'}, dimensions={0} | all-to-all | bytes 98304 | tf_op jit(solution)/shard_map/all_to_all | solution.py:164
  30.3 13.0 %all-to-all-start.1 = ((bf16[32,8,768]{2,1,0:T(8,128)(2,1)}), bf16[32,8,768]{2,1,0:T(8,128)(2,1)S(1)}, u32[]{:S(2)}, u32[]{:S(2)}) async-start(bf16[32,8,768]{2,1,0:T(8,128)(2,1)} %bitcast.3), calls=%async_computation.1 | async-start | bytes 786432 | tf_op jit(solution)/shard_map/all_to_all | solution.py:170
  43.3 2.7 collective-permute-start.4
  46.1 1.8 dynamic-slice_bitcast_fusion.1.wq_ref
  47.9 18.7 %collective-permute-done.4 = bf16[192,1536]{1,0:T(8,128)(2,1)} collective-permute-done((bf16[192,1536]{1,0:T(8,128)(2,1)}, bf16[192,1536]{1,0:T(8,128)(2,1)}, u32[]{:S(2)}, u32[]{:S(2)}) %collective-permute-start.4) | collective-permute-done | bytes 589856 | tf_op jit(solution)/shard_map/ppermute | solution.py:149
  66.7 1.5 collective-permute-start.6
  72.4 1.7 dynamic-slice_reduce_fusion
  76.3 1.9 constant_dynamic-update-slice_fusion.7
  78.2 2.7 collective-permute-done.6
  81.0 2.9 collective-permute-start.8
  83.9 1.9 constant_dynamic-update-slice_fusion.6
  85.8 5.7 %collective-permute-done.7 = bf16[192,1536]{1,0:T(8,128)(2,1)S(1)} collective-permute-done((bf16[192,1536]{1,0:T(8,128)(2,1)}, bf16[192,1536]{1,0:T(8,128)(2,1)S(1)}, u32[]{:S(2)}, u32[]{:S(2)}) %collective-permute-start.7) | collective-permute-done | bytes 589856 | tf_op jit(solution)/shard_map/ppermute | solution.py:146
  91.7 1.9 constant_dynamic-update-slice_fusion.5
  96.1 10.8 %collective-permute-done.9 = bf16[192,1536]{1,0:T(8,128)(2,1)S(1)} collective-permute-done((bf16[192,1536]{1,0:T(8,128)(2,1)S(1)}, bf16[192,1536]{1,0:T(8,128)(2,1)S(1)}, u32[]{:S(2)}, u32[]{:S(2)}) %collective-permute-start.9) | collective-permute-done | bytes 589856 | tf_op jit(solution)/shard_map/ppermute | solution.py:146
  107.8 6.5 %front.16.own_ref = bf16[256,768]{1,0:T(8,128)(2,1)S(1)} custom-call(s32[1]{0:T(128)} %bitcast.7.core_ref, bf16[256,768]{1,0:T(8,128)(2,1)S(1)} %bitcast.40, bf16[256,768]{1,0:T(8,128)(2,1)S(1)} %collective-permute-done.other_ref, f32[6,768]{1,0:T(8,128)S(1)} %reshape.53.mod_ref, f32[2,128]{1,0:T(2,128)S(1)} %bitcast.42, ...), custom_call_target="tpu_custom_call" | custom-call | tf_op jit(solution)/shard_map/front/pallas_call | solution.py:201
  114.3 1.9 collective-permute-start.10
  118.3 1.9 collective-permute-start.11
  120.1 8.1 %collective-permute-done.11.own_ref.hidden_ref = bf16[256,768]{1,0:T(8,128)(2,1)S(1)} collective-permute-done((bf16[256,768]{1,0:T(8,128)(2,1)S(1)}, bf16[256,768]{1,0:T(8,128)(2,1)S(1)}, u32[]{:S(2)}, u32[]{:S(2)}) %collective-permute-start.11) | collective-permute-done | bytes 393248 | tf_op jit(solution)/shard_map/ppermute | solution.py:195
  130.8 6.4 %front.17.own_ref = bf16[256,768]{1,0:T(8,128)(2,1)S(1)} custom-call(s32[1]{0:T(128)} %bitcast.7.core_ref, bf16[256,768]{1,0:T(8,128)(2,1)S(1)} %collective-permute-done.11.own_ref.hidden_ref, bf16[256,768]{1,0:T(8,128)(2,1)S(1)} %collective-permute-done.12.other_ref, f32[6,768]{1,0:T(8,128)S(1)} %reshape.53.mod_ref, f32[2,128]{1,0:T(2,128)S(1)} %bitcast.43, ...), custom_call_target="tpu_custom_call" | custom-call | tf_op jit(solution)/shard_map/front/pallas_call | solution.py:201
  142.7 6.4 %front.18.own_ref = bf16[256,768]{1,0:T(8,128)(2,1)S(1)} custom-call(s32[1]{0:T(128)} %bitcast.7.core_ref, bf16[256,768]{1,0:T(8,128)(2,1)S(1)} %collective-permute-done.14.own_ref.hidden_ref, bf16[256,768]{1,0:T(8,128)(2,1)S(1)} %collective-permute-done.15.other_ref, f32[6,768]{1,0:T(8,128)S(1)} %reshape.53.mod_ref, f32[2,128]{1,0:T(2,128)S(1)} %bitcast.44, ...), custom_call_target="tpu_custom_call" | custom-call | tf_op jit(solution)/shard_map/front/pallas_call | solution.py:201
  154.3 6.4 %front.19.own_ref = bf16[256,768]{1,0:T(8,128)(2,1)S(1)} custom-call(s32[1]{0:T(128)} %bitcast.7.core_ref, bf16[256,768]{1,0:T(8,128)(2,1)S(1)} %collective-permute-done.17.own_ref.hidden_ref, bf16[256,768]{1,0:T(8,128)(2,1)S(1)} %collective-permute-done.18.other_ref, f32[6,768]{1,0:T(8,128)S(1)} %reshape.53.mod_ref, f32[2,128]{1,0:T(2,128)S(1)} %bitcast.45, ...), custom_call_target="tpu_custom_call" | custom-call | tf_op jit(solution)/shard_map/front/pallas_call | solution.py:201
  161.1 1.4 collective-permute-done.19.other_ref
  164.6 1.4 collective-permute-done.21.other_ref
  166.0 6.4 %front.20.own_ref = bf16[256,768]{1,0:T(8,128)(2,1)S(1)} custom-call(s32[1]{0:T(128)} %bitcast.7.core_ref, bf16[256,768]{1,0:T(8,128)(2,1)S(1)} %collective-permute-done.20.own_ref.hidden_ref, bf16[256,768]{1,0:T(8,128)(2,1)S(1)} %collective-permute-done.21.other_ref, f32[6,768]{1,0:T(8,128)S(1)} %reshape.53.mod_ref, f32[2,128]{1,0:T(2,128)S(1)} %bitcast.46, ...), custom_call_target="tpu_custom_call" | custom-call | tf_op jit(solution)/shard_map/front/pallas_call | solution.py:201
  172.8 1.4 collective-permute-done.22.other_ref
  177.5 6.4 %front.21.own_ref = bf16[256,768]{1,0:T(8,128)(2,1)S(1)} custom-call(s32[1]{0:T(128)} %bitcast.7.core_ref, bf16[256,768]{1,0:T(8,128)(2,1)S(1)} %collective-permute-done.23.own_ref.hidden_ref, bf16[256,768]{1,0:T(8,128)(2,1)S(1)} %collective-permute-done.24.other_ref, f32[6,768]{1,0:T(8,128)S(1)} %reshape.53.mod_ref, f32[2,128]{1,0:T(2,128)S(1)} %bitcast.47, ...), custom_call_target="tpu_custom_call" | custom-call | tf_op jit(solution)/shard_map/front/pallas_call | solution.py:201
  184.4 1.4 collective-permute-done.25.other_ref
  187.9 1.4 collective-permute-done.27.other_ref
  189.3 6.4 %front.22.own_ref = bf16[256,768]{1,0:T(8,128)(2,1)S(1)} custom-call(s32[1]{0:T(128)} %bitcast.7.core_ref, bf16[256,768]{1,0:T(8,128)(2,1)S(1)} %collective-permute-done.26.own_ref.hidden_ref, bf16[256,768]{1,0:T(8,128)(2,1)S(1)} %collective-permute-done.27.other_ref, f32[6,768]{1,0:T(8,128)S(1)} %reshape.53.mod_ref, f32[2,128]{1,0:T(2,128)S(1)} %bitcast.48, ...), custom_call_target="tpu_custom_call" | custom-call | tf_op jit(solution)/shard_map/front/pallas_call | solution.py:201
  196.1 1.4 collective-permute-done.28.other_ref
  199.4 1.4 collective-permute-done.30.other_ref
  200.8 6.4 %front.23.own_ref = bf16[256,768]{1,0:T(8,128)(2,1)S(1)} custom-call(s32[1]{0:T(128)} %bitcast.7.core_ref, bf16[256,768]{1,0:T(8,128)(2,1)S(1)} %collective-permute-done.29.own_ref.hidden_ref, bf16[256,768]{1,0:T(8,128)(2,1)S(1)} %collective-permute-done.30.other_ref, f32[6,768]{1,0:T(8,128)S(1)} %reshape.53.mod_ref, f32[2,128]{1,0:T(2,128)S(1)} %bitcast.49, ...), custom_call_target="tpu_custom_call" | custom-call | tf_op jit(solution)/shard_map/front/pallas_call | solution.py:201
  207.7 1.4 collective-permute-done.31.other_ref
  215.9 74.5 %collective-permute-done.32 = bf16[256,768]{1,0:T(8,128)(2,1)} collective-permute-done((bf16[256,768]{1,0:T(8,128)(2,1)S(1)}, bf16[256,768]{1,0:T(8,128)(2,1)}, u32[]{:S(2)}, u32[]{:S(2)}) %collective-permute-start.32) | collective-permute-done | bytes 393248 | tf_op jit(solution)/shard_map/ppermute | solution.py:195
  290.4 1.7 subtract_convert_fusion.own_ref.hidden_ref
  292.1 1.4 collective-permute-start.33
  294.8 1.7 copy-done.2
  296.4 6.4 %front.24.own_ref = bf16[256,768]{1,0:T(8,128)(2,1)S(1)} custom-call(s32[1]{0:T(128)} %bitcast.7.core_ref, bf16[256,768]{1,0:T(8,128)(2,1)S(1)} %subtract_convert_fusion.own_ref.hidden_ref, bf16[256,768]{1,0:T(8,128)(2,1)S(1)} %collective-permute-done.33.other_ref, f32[6,768]{1,0:T(8,128)S(1)} %reshape.54.mod_ref, f32[2,128]{1,0:T(2,128)S(1)} %bitcast.50, ...), custom_call_target="tpu_custom_call" | custom-call | tf_op jit(solution)/shard_map/front/pallas_call | solution.py:201
  306.8 8.4 %collective-permute-done.35.own_ref.hidden_ref = bf16[256,768]{1,0:T(8,128)(2,1)S(1)} collective-permute-done((bf16[256,768]{1,0:T(8,128)(2,1)S(1)}, bf16[256,768]{1,0:T(8,128)(2,1)S(1)}, u32[]{:S(2)}, u32[]{:S(2)}) %collective-permute-start.35) | collective-permute-done | bytes 393248 | tf_op jit(solution)/shard_map/ppermute | solution.py:195
  317.4 6.4 %front.25.own_ref = bf16[256,768]{1,0:T(8,128)(2,1)S(1)} custom-call(s32[1]{0:T(128)} %bitcast.7.core_ref, bf16[256,768]{1,0:T(8,128)(2,1)S(1)} %collective-permute-done.35.own_ref.hidden_ref, bf16[256,768]{1,0:T(8,128)(2,1)S(1)} %collective-permute-done.36.other_ref, f32[6,768]{1,0:T(8,128)S(1)} %reshape.54.mod_ref, f32[2,128]{1,0:T(2,128)S(1)} %bitcast.51, ...), custom_call_target="tpu_custom_call" | custom-call | tf_op jit(solution)/shard_map/front/pallas_call | solution.py:201
  329.1 6.4 %front.26.own_ref = bf16[256,768]{1,0:T(8,128)(2,1)S(1)} custom-call(s32[1]{0:T(128)} %bitcast.7.core_ref, bf16[256,768]{1,0:T(8,128)(2,1)S(1)} %collective-permute-done.38.own_ref.hidden_ref, bf16[256,768]{1,0:T(8,128)(2,1)S(1)} %collective-permute-done.39.other_ref, f32[6,768]{1,0:T(8,128)S(1)} %reshape.54.mod_ref, f32[2,128]{1,0:T(2,128)S(1)} %bitcast.52, ...), custom_call_target="tpu_custom_call" | custom-call | tf_op jit(solution)/shard_map/front/pallas_call | solution.py:201
  336.0 1.4 collective-permute-done.40.other_ref
  339.3 1.4 collective-permute-done.42.other_ref
  340.7 6.4 %front.27.own_ref = bf16[256,768]{1,0:T(8,128)(2,1)S(1)} custom-call(s32[1]{0:T(128)} %bitcast.7.core_ref, bf16[256,768]{1,0:T(8,128)(2,1)S(1)} %collective-permute-done.41.own_ref.hidden_ref, bf16[256,768]{1,0:T(8,128)(2,1)S(1)} %collective-permute-done.42.other_ref, f32[6,768]{1,0:T(8,128)S(1)} %reshape.54.mod_ref, f32[2,128]{1,0:T(2,128)S(1)} %bitcast.53, ...), custom_call_target="tpu_custom_call" | custom-call | tf_op jit(solution)/shard_map/front/pallas_call | solution.py:201
  347.5 1.4 collective-permute-done.43.other_ref
  351.0 1.4 collective-permute-done.45.other_ref
  352.4 6.4 %front.28.own_ref = bf16[256,768]{1,0:T(8,128)(2,1)S(1)} custom-call(s32[1]{0:T(128)} %bitcast.7.core_ref, bf16[256,768]{1,0:T(8,128)(2,1)S(1)} %collective-permute-done.44.own_ref.hidden_ref, bf16[256,768]{1,0:T(8,128)(2,1)S(1)} %collective-permute-done.45.other_ref, f32[6,768]{1,0:T(8,128)S(1)} %reshape.54.mod_ref, f32[2,128]{1,0:T(2,128)S(1)} %bitcast.54, ...), custom_call_target="tpu_custom_call" | custom-call | tf_op jit(solution)/shard_map/front/pallas_call | solution.py:201
  359.3 1.4 collective-permute-done.46.other_ref
  362.6 1.4 collective-permute-done.48.other_ref
  363.9 6.4 %front.29.own_ref = bf16[256,768]{1,0:T(8,128)(2,1)S(1)} custom-call(s32[1]{0:T(128)} %bitcast.7.core_ref, bf16[256,768]{1,0:T(8,128)(2,1)S(1)} %collective-permute-done.47.own_ref.hidden_ref, bf16[256,768]{1,0:T(8,128)(2,1)S(1)} %collective-permute-done.48.other_ref, f32[6,768]{1,0:T(8,128)S(1)} %reshape.54.mod_ref, f32[2,128]{1,0:T(2,128)S(1)} %bitcast.55, ...), custom_call_target="tpu_custom_call" | custom-call | tf_op jit(solution)/shard_map/front/pallas_call | solution.py:201
  370.8 1.4 collective-permute-done.49.other_ref
  374.4 1.4 collective-permute-done.51.other_ref
  375.7 6.4 %front.30.own_ref = bf16[256,768]{1,0:T(8,128)(2,1)S(1)} custom-call(s32[1]{0:T(128)} %bitcast.7.core_ref, bf16[256,768]{1,0:T(8,128)(2,1)S(1)} %collective-permute-done.50.own_ref.hidden_ref, bf16[256,768]{1,0:T(8,128)(2,1)S(1)} %collective-permute-done.51.other_ref, f32[6,768]{1,0:T(8,128)S(1)} %reshape.54.mod_ref, f32[2,128]{1,0:T(2,128)S(1)} %bitcast.56, ...), custom_call_target="tpu_custom_call" | custom-call | tf_op jit(solution)/shard_map/front/pallas_call | solution.py:201
  382.6 1.4 collective-permute-done.52.other_ref
  385.9 1.4 collective-permute-done.54.other_ref
  387.2 7.2 %front.31.own_ref = bf16[256,768]{1,0:T(8,128)(2,1)} custom-call(s32[1]{0:T(128)} %bitcast.7.core_ref, bf16[256,768]{1,0:T(8,128)(2,1)S(1)} %collective-permute-done.53.own_ref.hidden_ref, bf16[256,768]{1,0:T(8,128)(2,1)S(1)} %collective-permute-done.54.other_ref, f32[6,768]{1,0:T(8,128)S(1)} %reshape.54.mod_ref, f32[2,128]{1,0:T(2,128)S(1)} %bitcast.57, ...), custom_call_target="tpu_custom_call" | custom-call | tf_op jit(solution)/shard_map/front/pallas_call | solution.py:201
  394.8 1.7 collective-permute-done.55.other_ref
  396.5 1.9 back.31
  398.4 9.9 %all_to_all.21 = bf16[4,8,768]{2,1,0:T(8,128)(2,1)S(1)} all-to-all(bf16[4,8,768]{2,1,0:T(8,128)(2,1)S(1)} %fusion), channel_id=1, replica_groups={{0,1,2,3},{4,5,6,7},{8,9,10,11},{12,13,14,15},{16,17,18,19},{20,21,22,2..., dimensions={0} | all-to-all | bytes 98304 | tf_op jit(solution)/shard_map/all_to_all | solution.py:209
  409.1 70.7 %all-to-all-start.3 = ((bf16[8,2,8,192]{3,2,1,0:T(8,128)(2,1)}), bf16[8,2,8,192]{3,2,1,0:T(8,128)(2,1)S(1)}, u32[]{:S(2)}, u32[]{:S(2)}) async-start(bf16[8,2,8,192]{3,2,1,0:T(8,128)(2,1)} %bitcast.14), calls=%async_computation.3 | async-start | bytes 131072 | tf_op jit(solution)/shard_map/all_to_all | solution.py:214
  481.1 3.9 all-to-all-done.3
  (143 shorter events, 70.6 us)
Async XLA Ops:
  1.3 4.3 collective-permute-start.1
  4.6 14.8 %copy-start.4 = (bf16[2,8,192]{2,1,0:T(8,128)(2,1)S(1)}, bf16[2,8,192]{2,1,0:T(8,128)(2,1)}, u32[]{:S(2)}) copy-start(bf16[2,8,192]{2,1,0:T(8,128)(2,1)} %param.8) | copy-start | bytes 18436
  6.0 9.8 %collective-permute-start.2 = (bf16[96,1536]{1,0:T(8,128)(2,1)S(1)}, bf16[96,1536]{1,0:T(8,128)(2,1)S(1)}, u32[]{:S(2)}, u32[]{:S(2)}) collective-permute-start(bf16[96,1536]{1,0:T(8,128)(2,1)S(1)} %constant_dynamic-update-slice_fusion), channel_id=1, source_target_pairs={{0,2},{1,3},{2,0},{3,1},{4,6},{5,7},{6,4},{7,5},{8,10},{9,11},{10,... | collective-permute-start | bytes 884744 | tf_op jit(solution)/shard_map/ppermute | solution.py:130
  7.2 38.8 %copy-start.6 = (s32[2,2]{1,0:T(2,128)S(1)}, s32[2,2]{1,0:T(2,128)}, u32[]{:S(2)}) copy-start(s32[2,2]{1,0:T(2,128)} %param.9) | copy-start | bytes 52
  19.5 26.6 %collective-permute-start.3 = (bf16[192,1536]{1,0:T(8,128)(2,1)}, bf16[192,1536]{1,0:T(8,128)(2,1)S(1)}, u32[]{:S(2)}, u32[]{:S(2)}) collective-permute-start(bf16[192,1536]{1,0:T(8,128)(2,1)} %get-tuple-element.7), channel_id=1, source_target_pairs={{0,4},{1,5},{2,6},{3,7},{4,8},{5,9},{6,10},{7,11},{8,12},{9,13},{1... | collective-permute-start | bytes 1769480 | tf_op jit(solution)/shard_map/ppermute | solution.py:146
  30.3 43.8 %all-to-all-start.1 = ((bf16[32,8,768]{2,1,0:T(8,128)(2,1)}), bf16[32,8,768]{2,1,0:T(8,128)(2,1)S(1)}, u32[]{:S(2)}, u32[]{:S(2)}) async-start(bf16[32,8,768]{2,1,0:T(8,128)(2,1)} %bitcast.3), calls=%async_computation.1 | async-start | bytes 786432 | tf_op jit(solution)/shard_map/all_to_all | solution.py:170
  43.3 23.4 %collective-permute-start.4 = (bf16[192,1536]{1,0:T(8,128)(2,1)}, bf16[192,1536]{1,0:T(8,128)(2,1)}, u32[]{:S(2)}, u32[]{:S(2)}) collective-permute-start(bf16[192,1536]{1,0:T(8,128)(2,1)} %get-tuple-element.7), channel_id=1, source_target_pairs={{0,28},{1,29},{2,30},{3,31},{4,0},{5,1},{6,2},{7,3},{8,4},{9,5},{1... | collective-permute-start | bytes 1769480 | tf_op jit(solution)/shard_map/ppermute | solution.py:149
  46.0 29.2 %collective-permute-start.5 = (bf16[192,1536]{1,0:T(8,128)(2,1)S(1)}, bf16[192,1536]{1,0:T(8,128)(2,1)}, u32[]{:S(2)}, u32[]{:S(2)}) collective-permute-start(bf16[192,1536]{1,0:T(8,128)(2,1)S(1)} %collective-permute-done.3), channel_id=1, source_target_pairs={{0,4},{1,5},{2,6},{3,7},{4,8},{5,9},{6,10},{7,11},{8,12},{9,13},{1... | collective-permute-start | bytes 1769480 | tf_op jit(solution)/shard_map/ppermute | solution.py:146
  47.9 66.3 %copy-start = (bf16[1536,768]{1,0:T(8,128)(2,1)}, bf16[1536,768]{1,0:T(8,128)(2,1)S(1)}, u32[]{:S(2)}) copy-start(bf16[1536,768]{1,0:T(8,128)(2,1)S(1)} %dynamic-slice_bitcast_fusion.1.wq_ref) | copy-start | bytes 7077892
  47.9 59.8 %copy-start.3 = (f32[1,2,128]{2,1,0:T(2,128)S(1)}, f32[1,2,128]{2,1,0:T(2,128)}, u32[]{:S(2)}) copy-start(f32[1,2,128]{2,1,0:T(2,128)} %param.12) | copy-start | bytes 3076
  66.7 14.3 %collective-permute-start.6 = (bf16[192,1536]{1,0:T(8,128)(2,1)}, bf16[192,1536]{1,0:T(8,128)(2,1)}, u32[]{:S(2)}, u32[]{:S(2)}) collective-permute-start(bf16[192,1536]{1,0:T(8,128)(2,1)} %collective-permute-done.4), channel_id=1, source_target_pairs={{0,28},{1,29},{2,30},{3,31},{4,0},{5,1},{6,2},{7,3},{8,4},{9,5},{1... | collective-permute-start | bytes 1769480 | tf_op jit(solution)/shard_map/ppermute | solution.py:149
  74.2 33.6 %collective-permute-start = (bf16[256,768]{1,0:T(8,128)(2,1)S(1)}, bf16[256,768]{1,0:T(8,128)(2,1)S(1)}, u32[]{:S(2)}, u32[]{:S(2)}) collective-permute-start(bf16[256,768]{1,0:T(8,128)(2,1)S(1)} %bitcast.39), channel_id=1, source_target_pairs={{0,1},{1,0},{2,3},{3,2},{4,5},{5,4},{6,7},{7,6},{8,9},{9,8},{10,11... | collective-permute-start | bytes 1179656 | tf_op jit(solution)/shard_map/ppermute | solution.py:117
  75.2 16.3 %collective-permute-start.7 = (bf16[192,1536]{1,0:T(8,128)(2,1)}, bf16[192,1536]{1,0:T(8,128)(2,1)S(1)}, u32[]{:S(2)}, u32[]{:S(2)}) collective-permute-start(bf16[192,1536]{1,0:T(8,128)(2,1)} %collective-permute-done.5), channel_id=1, source_target_pairs={{0,4},{1,5},{2,6},{3,7},{4,8},{5,9},{6,10},{7,11},{8,12},{9,13},{1... | collective-permute-start | bytes 1769480 | tf_op jit(solution)/shard_map/ppermute | solution.py:146
  81.0 14.3 %collective-permute-start.8 = (bf16[192,1536]{1,0:T(8,128)(2,1)}, bf16[192,1536]{1,0:T(8,128)(2,1)S(1)}, u32[]{:S(2)}, u32[]{:S(2)}) collective-permute-start(bf16[192,1536]{1,0:T(8,128)(2,1)} %collective-permute-done.6), channel_id=1, source_target_pairs={{0,28},{1,29},{2,30},{3,31},{4,0},{5,1},{6,2},{7,3},{8,4},{9,5},{1... | collective-permute-start | bytes 1769480 | tf_op jit(solution)/shard_map/ppermute | solution.py:149
  91.5 15.4 %collective-permute-start.9 = (bf16[192,1536]{1,0:T(8,128)(2,1)S(1)}, bf16[192,1536]{1,0:T(8,128)(2,1)S(1)}, u32[]{:S(2)}, u32[]{:S(2)}) collective-permute-start(bf16[192,1536]{1,0:T(8,128)(2,1)S(1)} %collective-permute-done.7), channel_id=1, source_target_pairs={{0,4},{1,5},{2,6},{3,7},{4,8},{5,9},{6,10},{7,11},{8,12},{9,13},{1... | collective-permute-start | bytes 1769480 | tf_op jit(solution)/shard_map/ppermute | solution.py:146
  96.1 20.0 %slice-start = ((s8[4718592]{0:T(1024)(128)(4,1)}), s8[4194304]{0:T(1024)(128)(4,1)S(1)}, s32[]{:S(2)}) async-start(s8[4718592]{0:T(1024)(128)(4,1)} %bitcast.58), calls=%async_computation.4 | async-start | bytes 8388608
  114.3 3.2 collective-permute-start.10
  118.3 10.0 %collective-permute-start.11 = (bf16[256,768]{1,0:T(8,128)(2,1)S(1)}, bf16[256,768]{1,0:T(8,128)(2,1)S(1)}, u32[]{:S(2)}, u32[]{:S(2)}) collective-permute-start(bf16[256,768]{1,0:T(8,128)(2,1)S(1)} %back.16), channel_id=1, source_target_pairs={{0,32},{1,33},{2,34},{3,35},{4,36},{5,37},{6,38},{7,39},{8,40},{9,... | collective-permute-start | bytes 1179656 | tf_op jit(solution)/shard_map/ppermute | solution.py:195
  128.2 2.6 collective-permute-start.12
  137.2 1.8 collective-permute-start.13
  139.8 0.7 collective-permute-start.14
  140.5 2.2 collective-permute-start.15
  149.1 1.8 collective-permute-start.16
  151.7 0.7 collective-permute-start.17
  152.5 1.8 collective-permute-start.18
  160.7 1.8 collective-permute-start.19
  163.3 0.7 collective-permute-start.20
  164.0 2.0 collective-permute-start.21
  172.4 1.8 collective-permute-start.22
  175.0 0.7 collective-permute-start.23
  175.7 1.8 collective-permute-start.24
  183.9 1.8 collective-permute-start.25
  186.5 0.7 collective-permute-start.26
  187.2 2.0 collective-permute-start.27
  195.7 1.8 collective-permute-start.28
  198.3 17.0 %copy-start.5 = (f32[16]{0:T(128)S(1)}, f32[16]{0:T(128)}, u32[]{:S(2)}) copy-start(f32[16]{0:T(128)} %param.10) | copy-start | bytes 196
  198.3 0.7 collective-permute-start.29
  199.0 1.8 collective-permute-start.30
  207.2 1.8 collective-permute-start.31
  209.8 80.6 %collective-permute-start.32 = (bf16[256,768]{1,0:T(8,128)(2,1)S(1)}, bf16[256,768]{1,0:T(8,128)(2,1)}, u32[]{:S(2)}, u32[]{:S(2)}) collective-permute-start(bf16[256,768]{1,0:T(8,128)(2,1)S(1)} %back.23), channel_id=1, source_target_pairs={{224,0},{225,1},{226,2},{227,3},{228,4},{229,5},{230,6},{231,7},{2... | collective-permute-start | bytes 1179656 | tf_op jit(solution)/shard_map/ppermute | solution.py:195
  292.1 2.7 collective-permute-start.33
  302.9 1.8 collective-permute-start.34
  305.5 9.7 %collective-permute-start.35 = (bf16[256,768]{1,0:T(8,128)(2,1)S(1)}, bf16[256,768]{1,0:T(8,128)(2,1)S(1)}, u32[]{:S(2)}, u32[]{:S(2)}) collective-permute-start(bf16[256,768]{1,0:T(8,128)(2,1)S(1)} %back.24), channel_id=1, source_target_pairs={{0,32},{1,33},{2,34},{3,35},{4,36},{5,37},{6,38},{7,39},{8,40},{9,... | collective-permute-start | bytes 1179656 | tf_op jit(solution)/shard_map/ppermute | solution.py:195
  315.2 2.2 collective-permute-start.36
  323.8 1.8 collective-permute-start.37
  326.4 0.7 collective-permute-start.38
  327.1 2.0 collective-permute-start.39
  335.5 1.8 collective-permute-start.40
  338.1 0.7 collective-permute-start.41
  338.9 1.8 collective-permute-start.42
  347.1 1.8 collective-permute-start.43
  349.7 0.7 collective-permute-start.44
  350.4 2.0 collective-permute-start.45
  358.8 1.8 collective-permute-start.46
  361.4 0.7 collective-permute-start.47
  362.1 1.8 collective-permute-start.48
  370.4 1.8 collective-permute-start.49
  373.0 0.7 collective-permute-start.50
  373.7 2.1 collective-permute-start.51
  382.1 1.8 collective-permute-start.52
  384.7 0.7 collective-permute-start.53
  385.4 1.8 collective-permute-start.54
  394.4 2.1 collective-permute-start.55
  409.1 75.8 %all-to-all-start.3 = ((bf16[8,2,8,192]{3,2,1,0:T(8,128)(2,1)}), bf16[8,2,8,192]{3,2,1,0:T(8,128)(2,1)S(1)}, u32[]{:S(2)}, u32[]{:S(2)}) async-start(bf16[8,2,8,192]{3,2,1,0:T(8,128)(2,1)} %bitcast.14), calls=%async_computation.3 | async-start | bytes 131072 | tf_op jit(solution)/shard_map/all_to_all | solution.py:214
  (3 other events, 24.7 us)

commit v2 on v1

--- a/solution.py
+++ b/solution.py
@@ -10,11 +10,14 @@
 norm_eps = 1e-06
 
 
-def layer_front(head_dim):
+def layer_front(head_dim, step):
     score_scale = 1.0 / math.sqrt(head_dim)
 
-    def body(core_ref, own_ref, other_ref, mod_ref, gain_ref, wq_ref, wkv_ref, out_ref):
-        core = core_ref[0]
+    def body(
+        word_ref, time_ref, own_ref, other_ref, mod_ref, gain_ref, wq_ref, wkv_ref, out_ref
+    ):
+        core = word_ref[0]
+        tau = time_ref[step, word_ref[1]]
         half = own_ref.shape[1]
         width = 2 * half
         near = pl.multiple_of(core * half, half)
@@ -33,8 +36,8 @@
         inverse = lax.rsqrt(spread + norm_eps)
 
         def modulated(values, at):
-            shift_row = mod_ref[pl.ds(at, 1), :]
-            scale_row = mod_ref[pl.ds(2 + at, 1), :]
+            shift_row = mod_ref[pl.ds(tau, 1), pl.ds(pl.multiple_of(at * half, half), half)]
+            scale_row = mod_ref[pl.ds(tau, 1), pl.ds(pl.multiple_of((2 + at) * half, half), half)]
             return (values * inverse * (1.0 + scale_row) + shift_row).astype(jnp.bfloat16)
 
         own = modulated(own, core)
@@ -85,16 +88,74 @@
     return body
 
 
-def layer_back(core_ref, own_ref, other_ref, hidden_ref, mod_ref, wo_ref, out_ref):
-    core = core_ref[0]
-    half = own_ref.shape[1]
-    near = pl.multiple_of(core * half, half)
-    far = pl.multiple_of((1 - core) * half, half)
-    projected = jnp.dot(
-        own_ref[...], wo_ref[pl.ds(near, half), :], preferred_element_type=jnp.float32
-    ) + jnp.dot(other_ref[...], wo_ref[pl.ds(far, half), :], preferred_element_type=jnp.float32)
-    gate_row = mod_ref[pl.ds(4 + core, 1), :]
-    out_ref[...] = (hidden_ref[...].astype(jnp.float32) + gate_row * projected).astype(jnp.bfloat16)
+def layer_back(step):
+    def body(word_ref, time_ref, own_ref, other_ref, hidden_ref, mod_ref, wo_ref, out_ref):
+        core = word_ref[0]
+        tau = time_ref[step, word_ref[1]]
+        half = own_ref.shape[1]
+        near = pl.multiple_of(core * half, half)
+        far = pl.multiple_of((1 - core) * half, half)
+        projected = jnp.dot(
+            own_ref[...], wo_ref[pl.ds(near, half), :], preferred_element_type=jnp.float32
+        ) + jnp.dot(
+            other_ref[...], wo_ref[pl.ds(far, half), :], preferred_element_type=jnp.float32
+        )
+        gate_row = mod_ref[pl.ds(tau, 1), pl.ds(pl.multiple_of((4 + core) * half, half), half)]
+        out_ref[...] = (hidden_ref[...].astype(jnp.float32) + gate_row * projected).astype(
+            jnp.bfloat16
+        )
+
+    return body
+
+
+def load_own(spots):
+    def body(word_ref, *refs):
+        part_refs = refs[: len(spots)]
+        query_ref, out_ref = refs[len(spots) : len(spots) + 2]
+        query_held, kv_held, out_held, sems = refs[len(spots) + 2 :]
+        half = query_held.shape[1]
+        ring = kv_held.shape[0] // part_refs[0].shape[0]
+        block = kv_held.shape[0] // ring
+        copies = []
+        for index, ((turn, start), part_ref) in enumerate(zip(spots, part_refs)):
+            rows = part_ref.shape[0]
+            at = pl.multiple_of(lax.rem(word_ref[2] + turn, ring) * block + start, rows)
+            copies.append(
+                pltpu.make_async_copy(part_ref, kv_held.at[pl.ds(at, rows), :], sems.at[index])
+            )
+        cols = pl.ds(pl.multiple_of(word_ref[0] * half, half), half)
+        for index, (source, held) in enumerate(((query_ref, query_held), (out_ref, out_held))):
+            copies.append(
+                pltpu.make_async_copy(source.at[0, :, cols], held, sems.at[len(spots) + index])
+            )
+        for copy in copies:
+            copy.start()
+        for copy in copies:
+            copy.wait()
+
+    return body
+
+
+def load_next(*refs):
+    count = (len(refs) - 1) // 2
+    sems = refs[-1]
+    copies = [
+        pltpu.make_async_copy(refs[at], refs[count + at], sems.at[at]) for at in range(count)
+    ]
+    for copy in copies:
+        copy.start()
+    for copy in copies:
+        copy.wait()
+
+
+def advance_slot(step):
+    def body(word_ref, time_ref, size_ref, slot_ref, hidden_ref, out_ref):
+        size = size_ref[time_ref[step, word_ref[1]]]
+        out_ref[...] = (
+            slot_ref[...].astype(jnp.float32) - size * hidden_ref[...].astype(jnp.float32)
+        ).astype(jnp.bfloat16)
+
+    return body
 
 
 def shards(latents, timesteps, step_sizes, mod_table, qk_gain, w_query, w_kv, w_out):
@@ -127,41 +188,34 @@
     low = jnp.where(core == 0, mine, theirs)
     high = jnp.where(core == 0, theirs, mine)
     block = jnp.concatenate([low, high], axis=0)
+    latents, block = lax.optimization_barrier((latents, block))
     theirs = lax.ppermute(block, "seq", [(at, at ^ 2) for at in range(n_seq)])
+
+    sent = jnp.broadcast_to(latents[None], (n_pipe,) + latents.shape)
+    rows = lax.all_to_all(sent, "pipe", 0, 0, tiled=True)
     low = jnp.where(micro == 0, block, theirs)
     high = jnp.where(micro == 0, theirs, block)
     block = jnp.concatenate([low, high], axis=0)
-    block_rows = block.shape[0]
+    rows, block = lax.optimization_barrier((rows, block))
     ring = n_seq // 4
-    place = seq_at // 4
     rings = [[(at, (at + turn) % n_seq) for at in range(n_seq)] for turn in (4, -4)]
-    kv_half = jnp.zeros((ring * block_rows, width), jnp.bfloat16)
-
-    def placed(whole, part, at):
-        return lax.dynamic_update_slice_in_dim(whole, part, ((place + at) % ring) * block_rows, 0)
-
-    kv_half = placed(kv_half, block, 0)
+    middle = block.shape[0] // 2
     rising = falling = block
-    for turn in range(1, ring // 2 + 1):
+    parts = [block]
+    spots = [(0, 0)]
+    for turn in range(1, ring // 2):
         rising = lax.ppermute(rising, "seq", rings[0])
-        kv_half = placed(kv_half, rising, ring - turn)
-        if turn < ring - turn:
-            falling = lax.ppermute(falling, "seq", rings[1])
-            kv_half = placed(kv_half, falling, turn)
-    query_half = columns(w_query[0], core, 1)
-    out_half = columns(w_out[0], core, 1)
-    core_word = core.astype(jnp.int32).reshape(1)
-
-    taus = lax.dynamic_index_in_dim(timesteps, micro, 1, keepdims=False)
-    mods = [
-        lax.dynamic_index_in_dim(mod_table[0], taus[at], 0, keepdims=False).reshape(6, half)
-        for at in range(step_count)
+        falling = lax.ppermute(falling, "seq", rings[1])
+        parts += [rising, falling]
+        spots += [(ring - turn, 0), (turn, 0)]
+        if turn == 1:
+            rows, rising, falling = lax.optimization_barrier((rows, rising, falling))
+    parts += [
+        lax.ppermute(rising[:middle], "seq", rings[0]),
+        lax.ppermute(falling[middle:], "seq", rings[1]),
     ]
-    first_size = lax.dynamic_index_in_dim(step_sizes, taus[0], 0, keepdims=False)
-    last_sizes = jnp.stack([step_sizes[timesteps[step_count - 1, at]] for at in range(micro_count)])
-
-    sent = jnp.broadcast_to(latents[None], (n_pipe,) + latents.shape)
-    rows = lax.all_to_all(sent, "pipe", 0, 0, tiled=True)
+    spots += [(ring // 2, 0), (ring // 2, middle)]
+
     rows = jnp.transpose(rows, (1, 2, 0, 3)).reshape(micro_count, row_share, 2, half)
     sent = jnp.transpose(rows, (0, 2, 1, 3)).reshape(1, 4, row_share, half)
     sent = jnp.broadcast_to(sent, (n_seq // 4, 4, row_share, half)).reshape(
@@ -169,39 +223,63 @@
     )
     slot = lax.all_to_all(sent, "seq", 0, 0, tiled=True).reshape(tokens, half)
 
+    words = jnp.stack([core, micro, seq_at // 4]).astype(jnp.int32)
+    last_sizes = jnp.stack([step_sizes[timesteps[step_count - 1, at]] for at in range(micro_count)])
     smem = pl.BlockSpec(memory_space=pltpu.SMEM)
     vmem = pl.BlockSpec(memory_space=pltpu.VMEM)
-    front = pl.pallas_call(
-        layer_front(head_dim),
-        out_shape=jax.ShapeDtypeStruct((tokens, half), jnp.bfloat16),
-        in_specs=[smem] + [vmem] * 6,
-        out_specs=vmem,
-        compiler_params=pltpu.CompilerParams(vmem_limit_bytes=32 << 20),
-        name="front",
-    )
-    back = pl.pallas_call(
-        layer_back,
-        out_shape=jax.ShapeDtypeStruct((tokens, half), jnp.bfloat16),
-        in_specs=[smem] + [vmem] * 5,
-        out_specs=vmem,
-        compiler_params=pltpu.CompilerParams(vmem_limit_bytes=16 << 20),
-        name="back",
-    )
-
+    hbm = pl.BlockSpec(memory_space=pltpu.HBM)
+    held_shapes = [
+        jax.ShapeDtypeStruct(shape, jnp.bfloat16)
+        for shape in ((width, half), (width, width), (width, half))
+    ]
+    held = pl.pallas_call(
+        load_own(spots),
+        out_shape=held_shapes,
+        in_specs=[smem] + [hbm] * (len(parts) + 2),
+        out_specs=[vmem] * 3,
+        scratch_shapes=[pltpu.SemaphoreType.DMA((len(parts) + 2,))],
+        compiler_params=pltpu.CompilerParams(vmem_limit_bytes=12 << 20),
+        name="load_own",
+    )(words, *parts, w_query, w_out)
+    lone = (mod_table[0], qk_gain[0], *held)
+
+    def layer(hidden, step, weights):
+        mods, gains, query_part, kv_part, out_part = weights
+        attended = pl.pallas_call(
+            layer_front(head_dim, step),
+            out_shape=jax.ShapeDtypeStruct((tokens, half), jnp.bfloat16),
+            in_specs=[smem] * 2 + [vmem] * 6,
+            out_specs=vmem,
+            compiler_params=pltpu.CompilerParams(vmem_limit_bytes=16 << 20),
+            name="front",
+        )(words, timesteps, hidden, swapped(hidden), mods, gains, query_part, kv_part)
+        return pl.pallas_call(
+            layer_back(step),
+            out_shape=jax.ShapeDtypeStruct((tokens, half), jnp.bfloat16),
+            in_specs=[smem] * 2 + [vmem] * 5,
+            out_specs=vmem,
+            compiler_params=pltpu.CompilerParams(vmem_limit_bytes=12 << 20),
+            name="back",
+        )(words, timesteps, attended, swapped(attended), hidden, mods, out_part)
+
+    holder = 0
     hidden = slot
-    for tick in range(step_count * n_pipe):
-        step = tick // n_pipe
-        if tick > 0:
-            hidden = lax.ppermute(hidden, "pipe", [((tick - 1) % n_pipe, tick % n_pipe)])
-        if tick > 0 and tick % n_pipe == 0:
-            slot = (
-                slot.astype(jnp.float32) - first_size * hidden.astype(jnp.float32)
-            ).astype(jnp.bfloat16)
-            hidden = slot
-        attended = front(
-            core_word, hidden, swapped(hidden), mods[step], qk_gain[0], query_half, kv_half
-        )
-        hidden = back(core_word, attended, swapped(attended), hidden, mods[step], out_half)
+    for step in range(step_count):
+        for section in range(n_pipe):
+            if section != holder:
+                hidden = lax.ppermute(hidden, "pipe", [(holder, section)])
+                holder = section
+            if step > 0 and section == 0:
+                slot = pl.pallas_call(
+                    advance_slot(step - 1),
+                    out_shape=jax.ShapeDtypeStruct((tokens, half), jnp.bfloat16),
+                    in_specs=[smem] * 3 + [vmem] * 2,
+                    out_specs=vmem,
+                    compiler_params=pltpu.CompilerParams(vmem_limit_bytes=8 << 20),
+                    name="advance_slot",
+                )(words, timesteps, step_sizes, slot, hidden)
+                hidden = slot
+            hidden = layer(hidden, step, lone)
 
     kept = jnp.where(pipe_at == 0, slot, hidden)
     kept = lax.dynamic_slice_in_dim(kept, (seq_at // 4) * 4 * row_share, 4 * row_share, 0)
@@ -212,7 +290,7 @@
         n_pipe, micro_count, row_share, feature_share
     )
     got = lax.all_to_all(sent, "pipe", 0, 0, tiled=True).astype(jnp.float32)
-    return (got[0] - last_sizes[:, None, None] * got[n_pipe - 1]).astype(jnp.bfloat16)
+    return (got[0] - last_sizes[:, None, None] * got[holder]).astype(jnp.bfloat16)
 
 
 def solution(mesh):

time: 494 us -> 467 us (0.945)
  blocking collectives: 19.8 us -> 0 us
  Pallas kernels: 117 us -> 101 us
  starting transfers between devices: 128 us -> 140 us
    all_to_all x2 -> x0, blocking collectives: 19.8 us -> none  [the longest x1 9.91 us: shards(): lax.all_to_all(kept, 'seq', 0, 0, tiled=True, axis_index_groups=quads)]
    pallas_call x32 -> x34, Pallas kernels: 117 us -> 101 us  [the longest x16 76.2 us: layer(): pl.pallas_call(layer_front(head_dim, step), out_shape=jax.ShapeDtypeStruc...]
    unnamed x21 -> x48, local copies, waits for them, and re-layouts: 1.75 us -> 16.1 us
    ppermute x3, waiting for transfers between devices: 22.3 us -> 8.47 us  [shards(): falling = lax.ppermute(falling, 'seq', rings[1])]
    ppermute x15 -> x17, waiting for transfers between devices: 91 us -> 104 us  [the longest x15 95.7 us: shards(): hidden = lax.ppermute(hidden, 'pipe', [(holder, section)])]
    all_to_all x1, waiting for transfers between devices: 0.01 us -> 10.8 us  [shards(): slot = lax.all_to_all(sent, 'seq', 0, 0, tiled=True).reshape(tokens, half)]
    dynamic_update_slice x7 -> x0, local copies, waits for them, and re-layouts: 9.26 us -> none  [placed(): lax.dynamic_update_slice_in_dim(whole, part, (place + at) % ring * block_...]
    all_to_all x0 -> x2, starting transfers between devices: none -> 8.97 us  [the longest x1 4.84 us: shards(): lax.all_to_all(kept, 'seq', 0, 0, tiled=True, axis_index_groups=quads)]
  transfers between devices with their start and end apart: 58 -> 61, of which waited for: 42 -> 43; matrix products, arithmetic and copies ran while one was open for 4% -> 1% of each run, Pallas kernels for 0% -> 0%
where the time goes in v2:
time: 467 us; the launch traced here: 458 us
  waiting for transfers between devices  187 us (40%)
  starting transfers between devices  140 us (30%)
  Pallas kernels  101 us (22%)
  local copies, waits for them, and re-layouts  22.6 us (5%)
  between operations  4.86 us (1%)
    ppermute x15, waiting for transfers between devices, shards(): hidden = lax.ppermute(hidden, 'pipe', [(holder, section)])  95.7 us
    pallas_call x16, Pallas kernels, layer(): pl.pallas_call(layer_front(head_dim, step), out_shape=jax.ShapeDtypeStruc...  76.2 us
    all_to_all x1, starting transfers between devices, shards(): got = lax.all_to_all(sent, 'pipe', 0, 0, tiled=True).astype(jnp.float32)  70.7 us
    ppermute x33, waiting for transfers between devices, swapped(): return lax.ppermute(value, 'seq', core_pairs)  43.3 us
    ppermute x33, starting transfers between devices, swapped(): return lax.ppermute(value, 'seq', core_pairs)  22.8 us
    pallas_call x16, Pallas kernels, layer(): pl.pallas_call(layer_back(step), out_shape=jax.ShapeDtypeStruct((tokens,...  22 us
    unnamed x48, local copies, waits for them, and re-layouts  16.1 us
    ppermute x15, starting transfers between devices, shards(): hidden = lax.ppermute(hidden, 'pipe', [(holder, section)])  13 us
  transfers between devices with their start and end apart: 61, of which 43 were waited for; matrix products, arithmetic and copies ran while one was open for 1% of the time, Pallas kernels for 0%

profile of v2, /device:TPU:1, one launch (start us, length us, event | category | flops | bytes accessed | tf_op | source)
XLA Modules:
  0.0 458.4 jit_solution(7594956491219507544)
XLA Ops:
  1.3 3.3 collective-permute-start
  7.9 4.1 all-to-all-start
  12.0 3.8 collective-permute-done.1
  17.2 1.6 collective-permute-start.2
  18.8 3.9 collective-permute-start.3
  22.7 11.6 %collective-permute-done.2.refs_1_ = bf16[192,1536]{1,0:T(8,128)(2,1)S(1)} collective-permute-done((bf16[192,1536]{1,0:T(8,128)(2,1)S(1)}, bf16[192,1536]{1,0:T(8,128)(2,1)S(1)}, u32[]{:S(2)}, u32[]{:S(2)}) %collective-permute-start.2) | collective-permute-done | bytes 589856 | tf_op jit(solution)/shard_map/ppermute | solution.py:207
  34.4 2.4 collective-permute-start.6
  38.5 10.8 %all-to-all-start.1 = ((bf16[32,8,768]{2,1,0:T(8,128)(2,1)}), bf16[32,8,768]{2,1,0:T(8,128)(2,1)S(1)}, u32[]{:S(2)}, u32[]{:S(2)}) async-start(bf16[32,8,768]{2,1,0:T(8,128)(2,1)} %bitcast.6), calls=%async_computation.1 | async-start | bytes 786432 | tf_op jit(solution)/shard_map/all_to_all | solution.py:224
  49.3 2.7 collective-permute-start.8
  52.9 10.8 %all-to-all-done.1 = bf16[32,8,768]{2,1,0:T(8,128)(2,1)S(1)} async-done(((bf16[32,8,768]{2,1,0:T(8,128)(2,1)}), bf16[32,8,768]{2,1,0:T(8,128)(2,1)S(1)}, u32[]{:S(2)}, u32[]{:S(2)}) %all-to-all-start.1) | async-done | bytes 393248 | tf_op jit(solution)/shard_map/all_to_all | solution.py:224
  64.2 8.5 %collective-permute-done.8.refs_6_ = bf16[192,1536]{1,0:T(8,128)(2,1)S(1)} collective-permute-done((bf16[192,1536]{1,0:T(8,128)(2,1)S(1)}, bf16[192,1536]{1,0:T(8,128)(2,1)S(1)}, u32[]{:S(2)}, u32[]{:S(2)}) %collective-permute-start.8) | collective-permute-done | bytes 589856 | tf_op jit(solution)/shard_map/ppermute | solution.py:208
  73.5 1.5 collective-permute-start.10
  76.0 5.3 %collective-permute-done.10.refs_8_ = bf16[96,1536]{1,0:T(8,128)(2,1)S(1)} collective-permute-done((bf16[96,1536]{1,0:T(8,128)(2,1)}, bf16[96,1536]{1,0:T(8,128)(2,1)S(1)}, u32[]{:S(2)}, u32[]{:S(2)}) %collective-permute-start.10) | collective-permute-done | bytes 294944 | tf_op jit(solution)/shard_map/ppermute | solution.py:215
  82.1 2.8 collective-permute-done.9.refs_7_
  85.6 2.3 copy-done.1
  87.9 2.3 copy-done.2
  98.6 2.1 load_own.1
  100.7 4.7 %front.16.own_ref = bf16[256,768]{1,0:T(8,128)(2,1)S(1)} custom-call(s32[3]{0:T(128)S(1)} %pad_add_fusion.word_ref, s32[2,2]{1,0:T(2,128)S(1)} %copy-done.9, bf16[256,768]{1,0:T(8,128)(2,1)S(1)} %bitcast.67, bf16[256,768]{1,0:T(8,128)(2,1)S(1)} %collective-permute-done.4.other_ref, f32[16,4608]{1,0:T(8,128)S(1)} %bitcast.34, f32[2,128]{1,0:T(2,128)S(1)} %bitcast.70, ...), custom_call_target="tpu_custom_call" | custom-call | tf_op jit(solution)/shard_map/front/pallas_call | solution.py:248
  105.5 1.9 collective-permute-start.11
  107.4 1.3 collective-permute-done.11.other_ref
  110.1 2.2 collective-permute-start.12
  112.3 8.1 %collective-permute-done.12.own_ref.hidden_ref = bf16[256,768]{1,0:T(8,128)(2,1)S(1)} collective-permute-done((bf16[256,768]{1,0:T(8,128)(2,1)S(1)}, bf16[256,768]{1,0:T(8,128)(2,1)S(1)}, u32[]{:S(2)}, u32[]{:S(2)}) %collective-permute-start.12) | collective-permute-done | bytes 393248 | tf_op jit(solution)/shard_map/ppermute | solution.py:270
  121.6 1.3 collective-permute-done.13.other_ref
  122.9 4.7 %front.17.own_ref = bf16[256,768]{1,0:T(8,128)(2,1)S(1)} custom-call(s32[3]{0:T(128)S(1)} %pad_add_fusion.word_ref, s32[2,2]{1,0:T(2,128)S(1)} %copy-done.9, bf16[256,768]{1,0:T(8,128)(2,1)S(1)} %collective-permute-done.12.own_ref.hidden_ref, bf16[256,768]{1,0:T(8,128)(2,1)S(1)} %collective-permute-done.13.other_ref, f32[16,4608]{1,0:T(8,128)S(1)} %bitcast.36, ...), custom_call_target="tpu_custom_call" | custom-call | tf_op jit(solution)/shard_map/front/pallas_call | solution.py:248
  132.4 1.3 collective-permute-done.16.other_ref
  133.7 4.7 %front.18.own_ref = bf16[256,768]{1,0:T(8,128)(2,1)S(1)} custom-call(s32[3]{0:T(128)S(1)} %pad_add_fusion.word_ref, s32[2,2]{1,0:T(2,128)S(1)} %copy-done.9, bf16[256,768]{1,0:T(8,128)(2,1)S(1)} %collective-permute-done.15.own_ref.hidden_ref, bf16[256,768]{1,0:T(8,128)(2,1)S(1)} %collective-permute-done.16.other_ref, f32[16,4608]{1,0:T(8,128)S(1)} %bitcast.38, ...), custom_call_target="tpu_custom_call" | custom-call | tf_op jit(solution)/shard_map/front/pallas_call | solution.py:248
  138.9 1.4 collective-permute-done.17.other_ref
  142.8 1.4 collective-permute-done.19.other_ref
  144.1 4.7 %front.19.own_ref = bf16[256,768]{1,0:T(8,128)(2,1)S(1)} custom-call(s32[3]{0:T(128)S(1)} %pad_add_fusion.word_ref, s32[2,2]{1,0:T(2,128)S(1)} %copy-done.9, bf16[256,768]{1,0:T(8,128)(2,1)S(1)} %collective-permute-done.18.own_ref.hidden_ref, bf16[256,768]{1,0:T(8,128)(2,1)S(1)} %collective-permute-done.19.other_ref, f32[16,4608]{1,0:T(8,128)S(1)} %bitcast.40, ...), custom_call_target="tpu_custom_call" | custom-call | tf_op jit(solution)/shard_map/front/pallas_call | solution.py:248
  149.3 1.4 collective-permute-done.20.other_ref
  153.3 1.4 collective-permute-done.22.other_ref
  154.7 4.7 %front.20.own_ref = bf16[256,768]{1,0:T(8,128)(2,1)S(1)} custom-call(s32[3]{0:T(128)S(1)} %pad_add_fusion.word_ref, s32[2,2]{1,0:T(2,128)S(1)} %copy-done.9, bf16[256,768]{1,0:T(8,128)(2,1)S(1)} %collective-permute-done.21.own_ref.hidden_ref, bf16[256,768]{1,0:T(8,128)(2,1)S(1)} %collective-permute-done.22.other_ref, f32[16,4608]{1,0:T(8,128)S(1)} %bitcast.42, ...), custom_call_target="tpu_custom_call" | custom-call | tf_op jit(solution)/shard_map/front/pallas_call | solution.py:248
  159.9 1.4 collective-permute-done.23.other_ref
  163.7 1.4 collective-permute-done.25.other_ref
  165.1 4.7 %front.21.own_ref = bf16[256,768]{1,0:T(8,128)(2,1)S(1)} custom-call(s32[3]{0:T(128)S(1)} %pad_add_fusion.word_ref, s32[2,2]{1,0:T(2,128)S(1)} %copy-done.9, bf16[256,768]{1,0:T(8,128)(2,1)S(1)} %collective-permute-done.24.own_ref.hidden_ref, bf16[256,768]{1,0:T(8,128)(2,1)S(1)} %collective-permute-done.25.other_ref, f32[16,4608]{1,0:T(8,128)S(1)} %bitcast.44, ...), custom_call_target="tpu_custom_call" | custom-call | tf_op jit(solution)/shard_map/front/pallas_call | solution.py:248
  170.2 1.4 collective-permute-done.26.other_ref
  174.3 1.4 collective-permute-done.28.other_ref
  175.7 4.7 %front.22.own_ref = bf16[256,768]{1,0:T(8,128)(2,1)S(1)} custom-call(s32[3]{0:T(128)S(1)} %pad_add_fusion.word_ref, s32[2,2]{1,0:T(2,128)S(1)} %copy-done.9, bf16[256,768]{1,0:T(8,128)(2,1)S(1)} %collective-permute-done.27.own_ref.hidden_ref, bf16[256,768]{1,0:T(8,128)(2,1)S(1)} %collective-permute-done.28.other_ref, f32[16,4608]{1,0:T(8,128)S(1)} %bitcast.46, ...), custom_call_target="tpu_custom_call" | custom-call | tf_op jit(solution)/shard_map/front/pallas_call | solution.py:248
  180.8 1.4 collective-permute-done.29.other_ref
  184.7 1.4 collective-permute-done.31.other_ref
  186.1 4.7 %front.23.own_ref = bf16[256,768]{1,0:T(8,128)(2,1)S(1)} custom-call(s32[3]{0:T(128)S(1)} %pad_add_fusion.word_ref, s32[2,2]{1,0:T(2,128)S(1)} %copy-done.9, bf16[256,768]{1,0:T(8,128)(2,1)S(1)} %collective-permute-done.30.own_ref.hidden_ref, bf16[256,768]{1,0:T(8,128)(2,1)S(1)} %collective-permute-done.31.other_ref, f32[16,4608]{1,0:T(8,128)S(1)} %bitcast.48, ...), custom_call_target="tpu_custom_call" | custom-call | tf_op jit(solution)/shard_map/front/pallas_call | solution.py:248
  191.2 1.4 collective-permute-done.32.other_ref
  195.2 79.2 %collective-permute-done.33.hidden_ref = bf16[256,768]{1,0:T(8,128)(2,1)S(1)} collective-permute-done((bf16[256,768]{1,0:T(8,128)(2,1)S(1)}, bf16[256,768]{1,0:T(8,128)(2,1)S(1)}, u32[]{:S(2)}, u32[]{:S(2)}) %collective-permute-start.33) | collective-permute-done | bytes 393248 | tf_op jit(solution)/shard_map/ppermute | solution.py:270
  275.1 1.4 collective-permute-start.34
  277.8 4.7 %front.24.own_ref = bf16[256,768]{1,0:T(8,128)(2,1)S(1)} custom-call(s32[3]{0:T(128)S(1)} %pad_add_fusion.word_ref, s32[2,2]{1,0:T(2,128)S(1)} %copy-done.9, bf16[256,768]{1,0:T(8,128)(2,1)S(1)} %advance_slot.1.own_ref.hidden_ref, bf16[256,768]{1,0:T(8,128)(2,1)S(1)} %collective-permute-done.34.other_ref, f32[16,4608]{1,0:T(8,128)S(1)} %bitcast.50, ...), custom_call_target="tpu_custom_call" | custom-call | tf_op jit(solution)/shard_map/front/pallas_call | solution.py:248
  283.0 1.4 collective-permute-done.35.other_ref
  287.0 8.4 %collective-permute-done.36.own_ref.hidden_ref = bf16[256,768]{1,0:T(8,128)(2,1)S(1)} collective-permute-done((bf16[256,768]{1,0:T(8,128)(2,1)S(1)}, bf16[256,768]{1,0:T(8,128)(2,1)S(1)}, u32[]{:S(2)}, u32[]{:S(2)}) %collective-permute-start.36) | collective-permute-done | bytes 393248 | tf_op jit(solution)/shard_map/ppermute | solution.py:270
  297.7 4.7 %front.25.own_ref = bf16[256,768]{1,0:T(8,128)(2,1)S(1)} custom-call(s32[3]{0:T(128)S(1)} %pad_add_fusion.word_ref, s32[2,2]{1,0:T(2,128)S(1)} %copy-done.9, bf16[256,768]{1,0:T(8,128)(2,1)S(1)} %collective-permute-done.36.own_ref.hidden_ref, bf16[256,768]{1,0:T(8,128)(2,1)S(1)} %collective-permute-done.37.other_ref, f32[16,4608]{1,0:T(8,128)S(1)} %bitcast.52, ...), custom_call_target="tpu_custom_call" | custom-call | tf_op jit(solution)/shard_map/front/pallas_call | solution.py:248
  308.2 4.7 %front.26.own_ref = bf16[256,768]{1,0:T(8,128)(2,1)S(1)} custom-call(s32[3]{0:T(128)S(1)} %pad_add_fusion.word_ref, s32[2,2]{1,0:T(2,128)S(1)} %copy-done.9, bf16[256,768]{1,0:T(8,128)(2,1)S(1)} %collective-permute-done.39.own_ref.hidden_ref, bf16[256,768]{1,0:T(8,128)(2,1)S(1)} %collective-permute-done.40.other_ref, f32[16,4608]{1,0:T(8,128)S(1)} %bitcast.54, ...), custom_call_target="tpu_custom_call" | custom-call | tf_op jit(solution)/shard_map/front/pallas_call | solution.py:248
  318.6 4.7 %front.27.own_ref = bf16[256,768]{1,0:T(8,128)(2,1)S(1)} custom-call(s32[3]{0:T(128)S(1)} %pad_add_fusion.word_ref, s32[2,2]{1,0:T(2,128)S(1)} %copy-done.9, bf16[256,768]{1,0:T(8,128)(2,1)S(1)} %collective-permute-done.42.own_ref.hidden_ref, bf16[256,768]{1,0:T(8,128)(2,1)S(1)} %collective-permute-done.43.other_ref, f32[16,4608]{1,0:T(8,128)S(1)} %bitcast.56, ...), custom_call_target="tpu_custom_call" | custom-call | tf_op jit(solution)/shard_map/front/pallas_call | solution.py:248
  329.2 4.7 %front.28.own_ref = bf16[256,768]{1,0:T(8,128)(2,1)S(1)} custom-call(s32[3]{0:T(128)S(1)} %pad_add_fusion.word_ref, s32[2,2]{1,0:T(2,128)S(1)} %copy-done.9, bf16[256,768]{1,0:T(8,128)(2,1)S(1)} %collective-permute-done.45.own_ref.hidden_ref, bf16[256,768]{1,0:T(8,128)(2,1)S(1)} %collective-permute-done.46.other_ref, f32[16,4608]{1,0:T(8,128)S(1)} %bitcast.58, ...), custom_call_target="tpu_custom_call" | custom-call | tf_op jit(solution)/shard_map/front/pallas_call | solution.py:248
  339.6 4.7 %front.29.own_ref = bf16[256,768]{1,0:T(8,128)(2,1)S(1)} custom-call(s32[3]{0:T(128)S(1)} %pad_add_fusion.word_ref, s32[2,2]{1,0:T(2,128)S(1)} %copy-done.9, bf16[256,768]{1,0:T(8,128)(2,1)S(1)} %collective-permute-done.48.own_ref.hidden_ref, bf16[256,768]{1,0:T(8,128)(2,1)S(1)} %collective-permute-done.49.other_ref, f32[16,4608]{1,0:T(8,128)S(1)} %bitcast.60, ...), custom_call_target="tpu_custom_call" | custom-call | tf_op jit(solution)/shard_map/front/pallas_call | solution.py:248
  344.8 1.4 collective-permute-done.50.other_ref
  348.9 1.4 collective-permute-done.52.other_ref
  350.3 4.7 %front.30.own_ref = bf16[256,768]{1,0:T(8,128)(2,1)S(1)} custom-call(s32[3]{0:T(128)S(1)} %pad_add_fusion.word_ref, s32[2,2]{1,0:T(2,128)S(1)} %copy-done.9, bf16[256,768]{1,0:T(8,128)(2,1)S(1)} %collective-permute-done.51.own_ref.hidden_ref, bf16[256,768]{1,0:T(8,128)(2,1)S(1)} %collective-permute-done.52.other_ref, f32[16,4608]{1,0:T(8,128)S(1)} %bitcast.62, ...), custom_call_target="tpu_custom_call" | custom-call | tf_op jit(solution)/shard_map/front/pallas_call | solution.py:248
  355.5 1.4 collective-permute-done.53.other_ref
  359.3 1.4 collective-permute-done.55.other_ref
  360.7 5.5 %front.31.own_ref = bf16[256,768]{1,0:T(8,128)(2,1)} custom-call(s32[3]{0:T(128)S(1)} %pad_add_fusion.word_ref, s32[2,2]{1,0:T(2,128)S(1)} %copy-done.9, bf16[256,768]{1,0:T(8,128)(2,1)S(1)} %collective-permute-done.54.own_ref.hidden_ref, bf16[256,768]{1,0:T(8,128)(2,1)S(1)} %collective-permute-done.55.other_ref, f32[16,4608]{1,0:T(8,128)S(1)} %bitcast.64, ...), custom_call_target="tpu_custom_call" | custom-call | tf_op jit(solution)/shard_map/front/pallas_call | solution.py:248
  366.5 1.7 collective-permute-done.56.other_ref
  368.2 1.9 back.31
  370.8 4.8 %all-to-all-start.2 = ((bf16[4,8,768]{2,1,0:T(8,128)(2,1)}), bf16[4,8,768]{2,1,0:T(8,128)(2,1)S(1)}, u32[]{:S(2)}, u32[]{:S(2)}) async-start(bf16[4,8,768]{2,1,0:T(8,128)(2,1)} %fusion), calls=%async_computation.2 | async-start | bytes 98304 | tf_op jit(solution)/shard_map/all_to_all | solution.py:287
  381.4 70.7 %all-to-all-start.3 = ((bf16[8,2,8,192]{3,2,1,0:T(8,128)(2,1)}), bf16[8,2,8,192]{3,2,1,0:T(8,128)(2,1)S(1)}, u32[]{:S(2)}, u32[]{:S(2)}) async-start(bf16[8,2,8,192]{3,2,1,0:T(8,128)(2,1)} %bitcast.12), calls=%async_computation.3 | async-start | bytes 131072 | tf_op jit(solution)/shard_map/all_to_all | solution.py:292
  452.1 1.4 pad_maximum_fusion.2
  453.5 3.8 all-to-all-done.3
  (162 shorter events, 86.1 us)
Async XLA Ops:
  1.3 4.3 collective-permute-start
  6.0 9.8 %collective-permute-start.1 = (bf16[96,1536]{1,0:T(8,128)(2,1)S(1)}, bf16[96,1536]{1,0:T(8,128)(2,1)S(1)}, u32[]{:S(2)}, u32[]{:S(2)}) collective-permute-start(bf16[96,1536]{1,0:T(8,128)(2,1)S(1)} %pad_maximum_fusion.1), channel_id=1, source_target_pairs={{0,2},{1,3},{2,0},{3,1},{4,6},{5,7},{6,4},{7,5},{8,10},{9,11},{10,... | collective-permute-start | bytes 884744 | tf_op jit(solution)/shard_map/ppermute | solution.py:192
  7.9 9.3 %all-to-all-start = ((bf16[8,2,8,192]{3,2,1,0:T(8,128)(2,1)}), bf16[8,2,8,192]{3,2,1,0:T(8,128)(2,1)S(1)}, u32[]{:S(2)}, u32[]{:S(2)}) async-start(bf16[8,2,8,192]{3,2,1,0:T(8,128)(2,1)} %broadcast_in_dim.6), calls=%async_computation | async-start | bytes 131072 | tf_op jit(solution)/shard_map/all_to_all | solution.py:195
  15.9 65.4 %copy-start.3 = (bf16[192,1536]{1,0:T(8,128)(2,1)}, bf16[192,1536]{1,0:T(8,128)(2,1)S(1)}, u32[]{:S(2)}) copy-start(bf16[192,1536]{1,0:T(8,128)(2,1)S(1)} %pad_maximum_fusion.refs_0_) | copy-start | bytes 1769476
  17.2 17.2 %collective-permute-start.2 = (bf16[192,1536]{1,0:T(8,128)(2,1)S(1)}, bf16[192,1536]{1,0:T(8,128)(2,1)S(1)}, u32[]{:S(2)}, u32[]{:S(2)}) collective-permute-start(bf16[192,1536]{1,0:T(8,128)(2,1)S(1)} %pad_maximum_fusion.refs_0_), channel_id=1, source_target_pairs={{0,4},{1,5},{2,6},{3,7},{4,8},{5,9},{6,10},{7,11},{8,12},{9,13},{1... | collective-permute-start | bytes 1769480 | tf_op jit(solution)/shard_map/ppermute | solution.py:207
  18.8 15.6 %collective-permute-start.3 = (bf16[192,1536]{1,0:T(8,128)(2,1)S(1)}, bf16[192,1536]{1,0:T(8,128)(2,1)S(1)}, u32[]{:S(2)}, u32[]{:S(2)}) collective-permute-start(bf16[192,1536]{1,0:T(8,128)(2,1)S(1)} %pad_maximum_fusion.refs_0_), channel_id=1, source_target_pairs={{0,28},{1,29},{2,30},{3,31},{4,0},{5,1},{6,2},{7,3},{8,4},{9,5},{1... | collective-permute-start | bytes 1769480 | tf_op jit(solution)/shard_map/ppermute | solution.py:208
  34.4 15.0 %collective-permute-start.6 = (bf16[192,1536]{1,0:T(8,128)(2,1)S(1)}, bf16[192,1536]{1,0:T(8,128)(2,1)S(1)}, u32[]{:S(2)}, u32[]{:S(2)}) collective-permute-start(bf16[192,1536]{1,0:T(8,128)(2,1)S(1)} %collective-permute-done.3.refs_2_), channel_id=1, source_target_pairs={{0,28},{1,29},{2,30},{3,31},{4,0},{5,1},{6,2},{7,3},{8,4},{9,5},{1... | collective-permute-start | bytes 1769480 | tf_op jit(solution)/shard_map/ppermute | solution.py:208
  37.6 15.4 %collective-permute-start.5 = (bf16[192,1536]{1,0:T(8,128)(2,1)S(1)}, bf16[192,1536]{1,0:T(8,128)(2,1)}, u32[]{:S(2)}, u32[]{:S(2)}) collective-permute-start(bf16[192,1536]{1,0:T(8,128)(2,1)S(1)} %collective-permute-done.2.refs_1_), channel_id=1, source_target_pairs={{0,4},{1,5},{2,6},{3,7},{4,8},{5,9},{6,10},{7,11},{8,12},{9,13},{1... | collective-permute-start | bytes 1769480 | tf_op jit(solution)/shard_map/ppermute | solution.py:207
  38.5 25.2 %all-to-all-start.1 = ((bf16[32,8,768]{2,1,0:T(8,128)(2,1)}), bf16[32,8,768]{2,1,0:T(8,128)(2,1)S(1)}, u32[]{:S(2)}, u32[]{:S(2)}) async-start(bf16[32,8,768]{2,1,0:T(8,128)(2,1)} %bitcast.6), calls=%async_computation.1 | async-start | bytes 786432 | tf_op jit(solution)/shard_map/all_to_all | solution.py:224
  49.3 23.3 %collective-permute-start.8 = (bf16[192,1536]{1,0:T(8,128)(2,1)S(1)}, bf16[192,1536]{1,0:T(8,128)(2,1)S(1)}, u32[]{:S(2)}, u32[]{:S(2)}) collective-permute-start(bf16[192,1536]{1,0:T(8,128)(2,1)S(1)} %collective-permute-done.6.refs_4_), channel_id=1, source_target_pairs={{0,28},{1,29},{2,30},{3,31},{4,0},{5,1},{6,2},{7,3},{8,4},{9,5},{1... | collective-permute-start | bytes 1769480 | tf_op jit(solution)/shard_map/ppermute | solution.py:208
  52.9 22.0 %collective-permute-start.7 = (bf16[192,1536]{1,0:T(8,128)(2,1)}, bf16[192,1536]{1,0:T(8,128)(2,1)S(1)}, u32[]{:S(2)}, u32[]{:S(2)}) collective-permute-start(bf16[192,1536]{1,0:T(8,128)(2,1)} %collective-permute-done.5.refs_3_), channel_id=1, source_target_pairs={{0,4},{1,5},{2,6},{3,7},{4,8},{5,9},{6,10},{7,11},{8,12},{9,13},{1... | collective-permute-start | bytes 1769480 | tf_op jit(solution)/shard_map/ppermute | solution.py:207
  63.8 36.9 %collective-permute-start.4 = (bf16[256,768]{1,0:T(8,128)(2,1)S(1)}, bf16[256,768]{1,0:T(8,128)(2,1)S(1)}, u32[]{:S(2)}, u32[]{:S(2)}) collective-permute-start(bf16[256,768]{1,0:T(8,128)(2,1)S(1)} %bitcast.66), channel_id=1, source_target_pairs={{0,1},{1,0},{2,3},{3,2},{4,5},{5,4},{6,7},{7,6},{8,9},{9,8},{10,11... | collective-permute-start | bytes 1179656 | tf_op jit(solution)/shard_map/ppermute | solution.py:178
  73.5 7.9 %collective-permute-start.10 = (bf16[96,1536]{1,0:T(8,128)(2,1)}, bf16[96,1536]{1,0:T(8,128)(2,1)S(1)}, u32[]{:S(2)}, u32[]{:S(2)}) collective-permute-start(bf16[96,1536]{1,0:T(8,128)(2,1)} %slice.25), channel_id=1, source_target_pairs={{0,28},{1,29},{2,30},{3,31},{4,0},{5,1},{6,2},{7,3},{8,4},{9,5},{1... | collective-permute-start | bytes 884744 | tf_op jit(solution)/shard_map/ppermute | solution.py:215
  75.7 9.2 %collective-permute-start.9 = (bf16[96,1536]{1,0:T(8,128)(2,1)}, bf16[96,1536]{1,0:T(8,128)(2,1)S(1)}, u32[]{:S(2)}, u32[]{:S(2)}) collective-permute-start(bf16[96,1536]{1,0:T(8,128)(2,1)} %slice.24), channel_id=1, source_target_pairs={{0,4},{1,5},{2,6},{3,7},{4,8},{5,9},{6,10},{7,11},{8,12},{9,13},{1... | collective-permute-start | bytes 884744 | tf_op jit(solution)/shard_map/ppermute | solution.py:214
  75.9 24.8 %copy-start.9 = (s32[2,2]{1,0:T(2,128)S(1)}, s32[2,2]{1,0:T(2,128)}, u32[]{:S(2)}) copy-start(s32[2,2]{1,0:T(2,128)} %time_ref.65) | copy-start | bytes 52
  105.5 3.3 collective-permute-start.11
  110.1 10.3 %collective-permute-start.12 = (bf16[256,768]{1,0:T(8,128)(2,1)S(1)}, bf16[256,768]{1,0:T(8,128)(2,1)S(1)}, u32[]{:S(2)}, u32[]{:S(2)}) collective-permute-start(bf16[256,768]{1,0:T(8,128)(2,1)S(1)} %back.16), channel_id=1, source_target_pairs={{0,32},{1,33},{2,34},{3,35},{4,36},{5,37},{6,38},{7,39},{8,40},{9,... | collective-permute-start | bytes 1179656 | tf_op jit(solution)/shard_map/ppermute | solution.py:270
  120.4 2.6 collective-permute-start.13
  127.7 1.8 collective-permute-start.14
  130.8 0.7 collective-permute-start.15
  131.5 2.2 collective-permute-start.16
  138.4 1.8 collective-permute-start.17
  141.6 0.7 collective-permute-start.18
  142.3 1.8 collective-permute-start.19
  148.8 1.8 collective-permute-start.20
  152.0 0.7 collective-permute-start.21
  152.7 2.0 collective-permute-start.22
  159.4 1.8 collective-permute-start.23
  162.6 0.7 collective-permute-start.24
  163.3 1.8 collective-permute-start.25
  169.8 1.8 collective-permute-start.26
  172.9 0.7 collective-permute-start.27
  173.6 2.0 collective-permute-start.28
  180.4 1.8 collective-permute-start.29
  183.5 0.7 collective-permute-start.30
  184.2 1.8 collective-permute-start.31
  190.8 83.7 %copy-start.21 = (f32[16]{0:T(128)S(1)}, f32[16]{0:T(128)}, u32[]{:S(2)}) copy-start(f32[16]{0:T(128)} %size_ref.1) | copy-start | bytes 196
  190.8 1.8 collective-permute-start.32
  193.9 80.5 %collective-permute-start.33 = (bf16[256,768]{1,0:T(8,128)(2,1)S(1)}, bf16[256,768]{1,0:T(8,128)(2,1)S(1)}, u32[]{:S(2)}, u32[]{:S(2)}) collective-permute-start(bf16[256,768]{1,0:T(8,128)(2,1)S(1)} %back.23), channel_id=1, source_target_pairs={{224,0},{225,1},{226,2},{227,3},{228,4},{229,5},{230,6},{231,7},{2... | collective-permute-start | bytes 1179656 | tf_op jit(solution)/shard_map/ppermute | solution.py:270
  275.1 2.7 collective-permute-start.34
  282.6 1.8 collective-permute-start.35
  285.7 9.7 %collective-permute-start.36 = (bf16[256,768]{1,0:T(8,128)(2,1)S(1)}, bf16[256,768]{1,0:T(8,128)(2,1)S(1)}, u32[]{:S(2)}, u32[]{:S(2)}) collective-permute-start(bf16[256,768]{1,0:T(8,128)(2,1)S(1)} %back.24), channel_id=1, source_target_pairs={{0,32},{1,33},{2,34},{3,35},{4,36},{5,37},{6,38},{7,39},{8,40},{9,... | collective-permute-start | bytes 1179656 | tf_op jit(solution)/shard_map/ppermute | solution.py:270
  295.4 2.2 collective-permute-start.37
  302.4 1.8 collective-permute-start.38
  305.6 0.7 collective-permute-start.39
  306.3 2.0 collective-permute-start.40
  313.0 1.8 collective-permute-start.41
  316.1 0.7 collective-permute-start.42
  316.8 1.8 collective-permute-start.43
  323.4 1.8 collective-permute-start.44
  326.5 0.7 collective-permute-start.45
  327.2 2.0 collective-permute-start.46
  334.0 1.8 collective-permute-start.47
  337.1 0.7 collective-permute-start.48
  337.8 1.8 collective-permute-start.49
  344.4 1.8 collective-permute-start.50
  347.5 0.7 collective-permute-start.51
  348.2 2.1 collective-permute-start.52
  355.0 1.8 collective-permute-start.53
  358.2 0.7 collective-permute-start.54
  358.9 1.8 collective-permute-start.55
  366.2 2.1 collective-permute-start.56
  370.8 9.9 %all-to-all-start.2 = ((bf16[4,8,768]{2,1,0:T(8,128)(2,1)}), bf16[4,8,768]{2,1,0:T(8,128)(2,1)S(1)}, u32[]{:S(2)}, u32[]{:S(2)}) async-start(bf16[4,8,768]{2,1,0:T(8,128)(2,1)} %fusion), calls=%async_computation.2 | async-start | bytes 98304 | tf_op jit(solution)/shard_map/all_to_all | solution.py:287
  381.4 75.8 %all-to-all-start.3 = ((bf16[8,2,8,192]{3,2,1,0:T(8,128)(2,1)}), bf16[8,2,8,192]{3,2,1,0:T(8,128)(2,1)S(1)}, u32[]{:S(2)}, u32[]{:S(2)}) async-start(bf16[8,2,8,192]{3,2,1,0:T(8,128)(2,1)} %bitcast.12), calls=%async_computation.3 | async-start | bytes 131072 | tf_op jit(solution)/shard_map/all_to_all | solution.py:292
  (20 other events, 105.6 us)

commit v3 on v2

--- a/solution.py
+++ b/solution.py
@@ -10,18 +10,12 @@
 norm_eps = 1e-06
 
 
-def layer_front(head_dim, step):
+def layer_front(head_dim):
     score_scale = 1.0 / math.sqrt(head_dim)
 
-    def body(
-        word_ref, time_ref, own_ref, other_ref, mod_ref, gain_ref, wq_ref, wkv_ref, out_ref
-    ):
-        core = word_ref[0]
-        tau = time_ref[step, word_ref[1]]
+    def body(own_ref, other_ref, mod_ref, gain_ref, wq_ref, wkv_ref, out_ref):
         half = own_ref.shape[1]
         width = 2 * half
-        near = pl.multiple_of(core * half, half)
-        far = pl.multiple_of((1 - core) * half, half)
         own = own_ref[...].astype(jnp.float32)
         other = other_ref[...].astype(jnp.float32)
         center = (
@@ -36,20 +30,18 @@
         inverse = lax.rsqrt(spread + norm_eps)
 
         def modulated(values, at):
-            shift_row = mod_ref[pl.ds(tau, 1), pl.ds(pl.multiple_of(at * half, half), half)]
-            scale_row = mod_ref[pl.ds(tau, 1), pl.ds(pl.multiple_of((2 + at) * half, half), half)]
+            shift_row = mod_ref[at : at + 1, :]
+            scale_row = mod_ref[2 + at : 3 + at, :]
             return (values * inverse * (1.0 + scale_row) + shift_row).astype(jnp.bfloat16)
 
-        own = modulated(own, core)
-        other = modulated(other, 1 - core)
+        own = modulated(own, 0)
+        other = modulated(other, 1)
 
         def project(weight_ref, start, size):
-            cols = pl.ds(start, size)
+            cols = slice(start, start + size)
             return jnp.dot(
-                own, weight_ref[pl.ds(near, half), cols], preferred_element_type=jnp.float32
-            ) + jnp.dot(
-                other, weight_ref[pl.ds(far, half), cols], preferred_element_type=jnp.float32
-            )
+                own, weight_ref[:half, cols], preferred_element_type=jnp.float32
+            ) + jnp.dot(other, weight_ref[half:, cols], preferred_element_type=jnp.float32)
 
         def rms(values, gain_row):
             mean_square = jnp.mean(values * values, axis=-1, keepdims=True)
@@ -88,64 +80,56 @@
     return body
 
 
-def layer_back(step):
-    def body(word_ref, time_ref, own_ref, other_ref, hidden_ref, mod_ref, wo_ref, out_ref):
-        core = word_ref[0]
-        tau = time_ref[step, word_ref[1]]
-        half = own_ref.shape[1]
-        near = pl.multiple_of(core * half, half)
-        far = pl.multiple_of((1 - core) * half, half)
-        projected = jnp.dot(
-            own_ref[...], wo_ref[pl.ds(near, half), :], preferred_element_type=jnp.float32
-        ) + jnp.dot(
-            other_ref[...], wo_ref[pl.ds(far, half), :], preferred_element_type=jnp.float32
-        )
-        gate_row = mod_ref[pl.ds(tau, 1), pl.ds(pl.multiple_of((4 + core) * half, half), half)]
-        out_ref[...] = (hidden_ref[...].astype(jnp.float32) + gate_row * projected).astype(
-            jnp.bfloat16
-        )
-
-    return body
+def layer_back(own_ref, other_ref, hidden_ref, mod_ref, wo_ref, out_ref):
+    half = own_ref.shape[1]
+    projected = jnp.dot(
+        own_ref[...], wo_ref[:half, :], preferred_element_type=jnp.float32
+    ) + jnp.dot(other_ref[...], wo_ref[half:, :], preferred_element_type=jnp.float32)
+    out_ref[...] = (
+        hidden_ref[...].astype(jnp.float32) + mod_ref[4:5, :] * projected
+    ).astype(jnp.bfloat16)
 
 
 def load_own(spots):
     def body(word_ref, *refs):
         part_refs = refs[: len(spots)]
-        query_ref, out_ref = refs[len(spots) : len(spots) + 2]
-        query_held, kv_held, out_held, sems = refs[len(spots) + 2 :]
-        half = query_held.shape[1]
-        ring = kv_held.shape[0] // part_refs[0].shape[0]
-        block = kv_held.shape[0] // ring
+        time_ref, mod_ref, gain_ref, query_ref, out_ref = refs[len(spots) : len(spots) + 5]
+        query_held, kv_held, out_held, gain_held = refs[len(spots) + 5 : len(spots) + 9]
+        mods_held, sems = refs[len(spots) + 9 : -1], refs[-1]
+        core = word_ref[0]
+        width, half = query_held.shape
+        block = part_refs[0].shape[0]
+        ring = width // block
         copies = []
-        for index, ((turn, start), part_ref) in enumerate(zip(spots, part_refs)):
+
+        def copied(source, target):
+            copies.append(pltpu.make_async_copy(source, target, sems.at[len(copies)]))
+
+        for (turn, start), part_ref in zip(spots, part_refs):
             rows = part_ref.shape[0]
-            at = pl.multiple_of(lax.rem(word_ref[2] + turn, ring) * block + start, rows)
-            copies.append(
-                pltpu.make_async_copy(part_ref, kv_held.at[pl.ds(at, rows), :], sems.at[index])
-            )
-        cols = pl.ds(pl.multiple_of(word_ref[0] * half, half), half)
-        for index, (source, held) in enumerate(((query_ref, query_held), (out_ref, out_held))):
-            copies.append(
-                pltpu.make_async_copy(source.at[0, :, cols], held, sems.at[len(spots) + index])
-            )
+            at = lax.rem(word_ref[2] + turn + core * (ring // 2), ring) * block + start
+            copied(part_ref, kv_held.at[pl.ds(pl.multiple_of(at, rows), rows), :])
+        cols = pl.ds(pl.multiple_of(core * half, half), half)
+        for source, held in ((query_ref, query_held), (out_ref, out_held)):
+            for side in range(2):
+                first = pl.multiple_of(lax.rem(core + side, 2) * half, half)
+                copied(
+                    source.at[0, pl.ds(first, half), cols], held.at[pl.ds(side * half, half), :]
+                )
         for copy in copies:
             copy.start()
+        gain_held[...] = gain_ref[0]
+        for step, held in enumerate(mods_held):
+            row = pl.ds(time_ref[step, word_ref[1]], 1)
+            for third in range(3):
+                for side in range(2):
+                    first = (2 * third + lax.rem(core + side, 2)) * half
+                    first = pl.ds(pl.multiple_of(first, half), half)
+                    held[2 * third + side : 2 * third + side + 1, :] = mod_ref[0, row, first]
         for copy in copies:
             copy.wait()
 
     return body
-
-
-def load_next(*refs):
-    count = (len(refs) - 1) // 2
-    sems = refs[-1]
-    copies = [
-        pltpu.make_async_copy(refs[at], refs[count + at], sems.at[at]) for at in range(count)
-    ]
-    for copy in copies:
-        copy.start()
-    for copy in copies:
-        copy.wait()
 
 
 def advance_slot(step):
@@ -154,6 +138,17 @@
         out_ref[...] = (
             slot_ref[...].astype(jnp.float32) - size * hidden_ref[...].astype(jnp.float32)
         ).astype(jnp.bfloat16)
+
+    return body
+
+
+def finish(step, holder):
+    def body(time_ref, size_ref, got_ref, out_ref):
+        for micro in range(out_ref.shape[0]):
+            size = size_ref[time_ref[step, micro]]
+            slot = got_ref[0, micro].astype(jnp.float32)
+            hidden = got_ref[holder, micro].astype(jnp.float32)
+            out_ref[micro] = (slot - size * hidden).astype(jnp.bfloat16)
 
     return body
 
@@ -180,11 +175,12 @@
     def columns(value, side, axis):
         return lax.dynamic_slice_in_dim(value, side * half, half, axis)
 
-    pair = w_kv[0].reshape(w_kv.shape[1], 2, half * 2)
-    mine = columns(pair, core, 2)
-    theirs = swapped(columns(pair, 1 - core, 2))
-    mine = mine.reshape(mine.shape[0], width)
-    theirs = theirs.reshape(mine.shape)
+    def kv_columns(side):
+        keys, values = w_kv[0, :, :width], w_kv[0, :, width:]
+        return jnp.concatenate([columns(keys, side, 1), columns(values, side, 1)], axis=1)
+
+    mine = kv_columns(core)
+    theirs = swapped(kv_columns(1 - core))
     low = jnp.where(core == 0, mine, theirs)
     high = jnp.where(core == 0, theirs, mine)
     block = jnp.concatenate([low, high], axis=0)
@@ -196,6 +192,11 @@
     low = jnp.where(micro == 0, block, theirs)
     high = jnp.where(micro == 0, theirs, block)
     block = jnp.concatenate([low, high], axis=0)
+    backward = [(at + 1, at) for at in range(0, n_pipe, 2)]
+
+    def to_even(value):
+        return lax.ppermute(value, "pipe", backward)
+
     rows, block = lax.optimization_barrier((rows, block))
     ring = n_seq // 4
     rings = [[(at, (at + turn) % n_seq) for at in range(n_seq)] for turn in (4, -4)]
@@ -224,7 +225,6 @@
     slot = lax.all_to_all(sent, "seq", 0, 0, tiled=True).reshape(tokens, half)
 
     words = jnp.stack([core, micro, seq_at // 4]).astype(jnp.int32)
-    last_sizes = jnp.stack([step_sizes[timesteps[step_count - 1, at]] for at in range(micro_count)])
     smem = pl.BlockSpec(memory_space=pltpu.SMEM)
     vmem = pl.BlockSpec(memory_space=pltpu.VMEM)
     hbm = pl.BlockSpec(memory_space=pltpu.HBM)
@@ -232,43 +232,62 @@
         jax.ShapeDtypeStruct(shape, jnp.bfloat16)
         for shape in ((width, half), (width, width), (width, half))
     ]
-    held = pl.pallas_call(
+    small_shapes = [jax.ShapeDtypeStruct(qk_gain.shape[1:], jnp.float32)] + [
+        jax.ShapeDtypeStruct((6, half), jnp.float32)
+    ] * step_count
+
+    def in_hbm(value):
+        return pltpu.with_memory_space_constraint(value, pltpu.HBM)
+
+    loaded = pl.pallas_call(
         load_own(spots),
-        out_shape=held_shapes,
-        in_specs=[smem] + [hbm] * (len(parts) + 2),
-        out_specs=[vmem] * 3,
-        scratch_shapes=[pltpu.SemaphoreType.DMA((len(parts) + 2,))],
+        out_shape=held_shapes + small_shapes,
+        in_specs=[smem] + [hbm] * len(parts) + [smem, vmem, vmem, hbm, hbm],
+        out_specs=[vmem] * (4 + step_count),
+        scratch_shapes=[pltpu.SemaphoreType.DMA((len(parts) + 4,))],
         compiler_params=pltpu.CompilerParams(vmem_limit_bytes=12 << 20),
         name="load_own",
-    )(words, *parts, w_query, w_out)
-    lone = (mod_table[0], qk_gain[0], *held)
-
-    def layer(hidden, step, weights):
-        mods, gains, query_part, kv_part, out_part = weights
+    )(
+        words,
+        *(in_hbm(part) for part in parts),
+        timesteps,
+        mod_table,
+        qk_gain,
+        in_hbm(w_query),
+        in_hbm(w_out),
+    )
+    held, gains, mods = loaded[:3], loaded[3], loaded[4:]
+
+    def layer(hidden, mods, gains, query_part, kv_part, out_part):
         attended = pl.pallas_call(
-            layer_front(head_dim, step),
+            layer_front(head_dim),
             out_shape=jax.ShapeDtypeStruct((tokens, half), jnp.bfloat16),
-            in_specs=[smem] * 2 + [vmem] * 6,
+            in_specs=[vmem] * 6,
             out_specs=vmem,
             compiler_params=pltpu.CompilerParams(vmem_limit_bytes=16 << 20),
             name="front",
-        )(words, timesteps, hidden, swapped(hidden), mods, gains, query_part, kv_part)
+        )(hidden, swapped(hidden), mods, gains, query_part, kv_part)
         return pl.pallas_call(
-            layer_back(step),
+            layer_back,
             out_shape=jax.ShapeDtypeStruct((tokens, half), jnp.bfloat16),
-            in_specs=[smem] * 2 + [vmem] * 5,
+            in_specs=[vmem] * 5,
             out_specs=vmem,
             compiler_params=pltpu.CompilerParams(vmem_limit_bytes=12 << 20),
             name="back",
-        )(words, timesteps, attended, swapped(attended), hidden, mods, out_part)
+        )(attended, swapped(attended), hidden, mods, out_part)
+
+    following = [to_even(value) for value in (mods[-1], gains, *held)]
+    due = {2: (2,), 4: (0, 1, 4), n_pipe: (3,)}
 
     holder = 0
     hidden = slot
     for step in range(step_count):
         for section in range(n_pipe):
-            if section != holder:
-                hidden = lax.ppermute(hidden, "pipe", [(holder, section)])
-                holder = section
+            joined = step > 0
+            place = section - section % 2 if joined else section
+            if place != holder:
+                hidden = lax.ppermute(hidden, "pipe", [(holder, place)])
+                holder = place
             if step > 0 and section == 0:
                 slot = pl.pallas_call(
                     advance_slot(step - 1),
@@ -279,7 +298,9 @@
                     name="advance_slot",
                 )(words, timesteps, step_sizes, slot, hidden)
                 hidden = slot
-            hidden = layer(hidden, step, lone)
+            hidden = layer(hidden, *(following if section != place else (mods[step], gains, *held)))
+            for at in due.get(step * n_pipe + section, ()):
+                hidden, following[at] = lax.optimization_barrier((hidden, following[at]))
 
     kept = jnp.where(pipe_at == 0, slot, hidden)
     kept = lax.dynamic_slice_in_dim(kept, (seq_at // 4) * 4 * row_share, 4 * row_share, 0)
@@ -289,8 +310,15 @@
     sent = jnp.transpose(kept, (1, 3, 0, 2, 4)).reshape(
         n_pipe, micro_count, row_share, feature_share
     )
-    got = lax.all_to_all(sent, "pipe", 0, 0, tiled=True).astype(jnp.float32)
-    return (got[0] - last_sizes[:, None, None] * got[holder]).astype(jnp.bfloat16)
+    got = lax.all_to_all(sent, "pipe", 0, 0, tiled=True)
+    return pl.pallas_call(
+        finish(step_count - 1, holder),
+        out_shape=jax.ShapeDtypeStruct(latents.shape, jnp.bfloat16),
+        in_specs=[smem] * 2 + [vmem],
+        out_specs=vmem,
+        compiler_params=pltpu.CompilerParams(vmem_limit_bytes=8 << 20),
+        name="finish",
+    )(timesteps, step_sizes, got)
 
 
 def solution(mesh):

time: 467 us -> 444 us (0.951)
  starting transfers between devices: 140 us -> 76.6 us
  waiting for transfers between devices: 187 us -> 228 us
  blocking collectives: 0 us -> 39.4 us
  local copies, waits for them, and re-layouts: 22.6 us -> 4.31 us
  Pallas kernels: 101 us -> 87.3 us
    all_to_all x2 -> x0, starting transfers between devices: 75.5 us -> none  [the longest x1 70.7 us: shards(): got = lax.all_to_all(sent, 'pipe', 0, 0, tiled=True).astype(jnp.float32)]
    ppermute x15 -> x16, waiting for transfers between devices: 95.7 us -> 142 us  [the longest x5 79.1 us: to_even(): return lax.ppermute(value, 'pipe', backward)]
    all_to_all x0 -> x2, blocking collectives: none -> 39.4 us  [the longest x1 30.8 us: shards(): got = lax.all_to_all(sent, 'pipe', 0, 0, tiled=True)]
    unnamed x48 -> x18, local copies, waits for them, and re-layouts: 16.1 us -> 0.47 us
    pallas_call x33 -> x34, Pallas kernels: 100 us -> 86.6 us  [the longest x16 67.4 us: layer(): pl.pallas_call(layer_front(head_dim), out_shape=jax.ShapeDtypeStruct((tok...]
    ppermute x33, starting transfers between devices: 22.8 us -> 32 us  [swapped(): return lax.ppermute(value, 'seq', core_pairs)]
    ppermute x1, waiting for transfers between devices: 5.29 us -> 0.29 us  [shards(): lax.ppermute(falling[middle:], 'seq', rings[1])]
    ppermute x15 -> x16, starting transfers between devices: 13 us -> 17.2 us  [the longest x11 10.8 us: shards(): hidden = lax.ppermute(hidden, 'pipe', [(holder, place)])]
  transfers between devices with their start and end apart: 61 -> 60, of which waited for: 43 -> 46; matrix products, arithmetic and copies ran while one was open for 1% -> 1% of each run, Pallas kernels for 0% -> 10%
where the time goes in v3:
time: 444 us; the launch traced here: 437 us
  waiting for transfers between devices  228 us (51%)
  Pallas kernels  87.3 us (20%)
  starting transfers between devices  76.6 us (17%)
  blocking collectives  39.4 us (9%)
    ppermute x5, waiting for transfers between devices, to_even(): return lax.ppermute(value, 'pipe', backward)  79.1 us
    pallas_call x16, Pallas kernels, layer(): pl.pallas_call(layer_front(head_dim), out_shape=jax.ShapeDtypeStruct((tok...  67.4 us
    ppermute x11, waiting for transfers between devices, shards(): hidden = lax.ppermute(hidden, 'pipe', [(holder, place)])  63.4 us
    ppermute x33, waiting for transfers between devices, swapped(): return lax.ppermute(value, 'seq', core_pairs)  41.9 us
    ppermute x33, starting transfers between devices, swapped(): return lax.ppermute(value, 'seq', core_pairs)  32 us
    all_to_all x1, blocking collectives, shards(): got = lax.all_to_all(sent, 'pipe', 0, 0, tiled=True)  30.8 us
    pallas_call x16, Pallas kernels, layer(): pl.pallas_call(layer_back, out_shape=jax.ShapeDtypeStruct((tokens, half),...  13.7 us
    ppermute x3, waiting for transfers between devices, shards(): rising = lax.ppermute(rising, 'seq', rings[0])  12.1 us
  transfers between devices with their start and end apart: 60, of which 46 were waited for; matrix products, arithmetic and copies ran while one was open for 1% of the time, Pallas kernels for 10%

profile of v3, /device:TPU:1, one launch (start us, length us, event | category | flops | bytes accessed | tf_op | source)
XLA Modules:
  0.0 436.5 jit_solution(1281864935391155543)
XLA Ops:
  1.1 3.3 collective-permute-start
  7.4 4.1 all-to-all-start
  11.6 3.8 collective-permute-done.1
  16.7 5.6 %collective-permute-start.3 = (bf16[192,1536]{1,0:T(8,128)(2,1)S(1)}, bf16[192,1536]{1,0:T(8,128)(2,1)}, u32[]{:S(2)}, u32[]{:S(2)}) collective-permute-start(bf16[192,1536]{1,0:T(8,128)(2,1)S(1)} %pad_maximum_fusion.refs_0_), channel_id=1, source_target_pairs={{0,28},{1,29},{2,30},{3,31},{4,0},{5,1},{6,2},{7,3},{8,4},{9,5},{1... | collective-permute-start | bytes 1769480 | tf_op jit(solution)/shard_map/ppermute | solution.py:209
  22.3 10.6 %collective-permute-done.3.refs_2_ = bf16[192,1536]{1,0:T(8,128)(2,1)} collective-permute-done((bf16[192,1536]{1,0:T(8,128)(2,1)S(1)}, bf16[192,1536]{1,0:T(8,128)(2,1)}, u32[]{:S(2)}, u32[]{:S(2)}) %collective-permute-start.3) | collective-permute-done | bytes 589856 | tf_op jit(solution)/shard_map/ppermute | solution.py:209
  32.8 3.1 collective-permute-done.2.refs_1_
  36.0 2.7 collective-permute-start.6
  39.6 8.1 %all-to-all-start.1 = ((bf16[32,8,768]{2,1,0:T(8,128)(2,1)}), bf16[32,8,768]{2,1,0:T(8,128)(2,1)S(1)}, u32[]{:S(2)}, u32[]{:S(2)}) async-start(bf16[32,8,768]{2,1,0:T(8,128)(2,1)} %bitcast.10), calls=%async_computation.1 | async-start | bytes 786432 | tf_op jit(solution)/shard_map/all_to_all | solution.py:225
  49.2 2.3 collective-permute-start.8
  51.5 10.8 %all-to-all-done.1 = bf16[32,8,768]{2,1,0:T(8,128)(2,1)S(1)} async-done(((bf16[32,8,768]{2,1,0:T(8,128)(2,1)}), bf16[32,8,768]{2,1,0:T(8,128)(2,1)S(1)}, u32[]{:S(2)}, u32[]{:S(2)}) %all-to-all-start.1) | async-done | bytes 393248 | tf_op jit(solution)/shard_map/all_to_all | solution.py:225
  62.3 2.8 collective-permute-start.4
  65.1 7.8 %collective-permute-done.7.refs_5_ = bf16[192,1536]{1,0:T(8,128)(2,1)S(1)} collective-permute-done((bf16[192,1536]{1,0:T(8,128)(2,1)}, bf16[192,1536]{1,0:T(8,128)(2,1)S(1)}, u32[]{:S(2)}, u32[]{:S(2)}) %collective-permute-start.7) | collective-permute-done | bytes 589856 | tf_op jit(solution)/shard_map/ppermute | solution.py:208
  74.1 2.8 collective-permute-start.10
  77.0 4.6 %collective-permute-done.9.refs_7_ = bf16[96,1536]{1,0:T(8,128)(2,1)S(1)} collective-permute-done((bf16[96,1536]{1,0:T(8,128)(2,1)S(1)}, bf16[96,1536]{1,0:T(8,128)(2,1)S(1)}, u32[]{:S(2)}, u32[]{:S(2)}) %collective-permute-start.9) | collective-permute-done | bytes 294944 | tf_op jit(solution)/shard_map/ppermute | solution.py:215
  82.3 4.4 %load_own.1 = (bf16[1536,768]{1,0:T(8,128)(2,1)S(1)}, bf16[1536,1536]{1,0:T(8,128)(2,1)S(1)}, bf16[1536,768]{1,0:T(8,128)(2,1)S(1)}, f32[2,128]{1,0:T(2,128)S(1)...) custom-call(s32[3]{0:T(128)S(1)} %pad_add_fusion.word_ref, bf16[192,1536]{1,0:T(8,128)(2,1)} %copy-done.4, ...), custom_call_target="tpu_custom_call" | custom-call | tf_op jit(solution)/shard_map/load_own/pallas_call | solution.py:242
  86.7 4.2 front.16.own_ref
  90.9 2.1 collective-permute-start.11
  95.2 1.8 collective-permute-start.12
  98.3 6.8 %collective-permute-done.12.own_ref.hidden_ref = bf16[256,768]{1,0:T(8,128)(2,1)S(1)} collective-permute-done((bf16[256,768]{1,0:T(8,128)(2,1)S(1)}, bf16[256,768]{1,0:T(8,128)(2,1)S(1)}, u32[]{:S(2)}, u32[]{:S(2)}) %collective-permute-start.12) | collective-permute-done | bytes 393248 | tf_op jit(solution)/shard_map/ppermute | solution.py:289
  106.3 1.3 collective-permute-done.13.other_ref
  107.7 4.2 front.17.own_ref
  112.3 1.4 collective-permute-done.14.other_ref
  116.0 1.4 collective-permute-done.16.other_ref
  117.4 4.2 front.18.own_ref
  122.0 1.4 collective-permute-done.17.other_ref
  124.1 26.9 %collective-permute-done.18.wq_ref = bf16[1536,768]{1,0:T(8,128)(2,1)S(1)} collective-permute-done((bf16[1536,768]{1,0:T(8,128)(2,1)S(1)}, bf16[1536,768]{1,0:T(8,128)(2,1)S(1)}, u32[]{:S(2)}, u32[]{:S(2)}) %collective-permute-start.18) | collective-permute-done | bytes 2359328 | tf_op jit(solution)/shard_map/ppermute | solution.py:198
  153.0 1.6 collective-permute-start.20
  154.7 1.3 collective-permute-done.20.other_ref
  156.0 4.2 front.19.own_ref
  160.6 1.3 collective-permute-done.21.other_ref
  165.5 4.2 front.20.own_ref
  173.5 31.9 %collective-permute-done.25.mod_ref = f32[6,768]{1,0:T(8,128)S(1)} collective-permute-done((f32[6,768]{1,0:T(8,128)S(1)}, f32[6,768]{1,0:T(8,128)S(1)}, u32[]{:S(2)}, u32[]{:S(2)}) %collective-permute-start.25) | collective-permute-done | bytes 18464 | tf_op jit(solution)/shard_map/ppermute | solution.py:198
  207.4 2.6 collective-permute-start.29
  211.3 4.2 front.21.own_ref
  220.8 4.2 front.22.own_ref
  230.1 4.2 front.23.own_ref
  238.2 48.5 %collective-permute-done.37.hidden_ref = bf16[256,768]{1,0:T(8,128)(2,1)S(1)} collective-permute-done((bf16[256,768]{1,0:T(8,128)(2,1)S(1)}, bf16[256,768]{1,0:T(8,128)(2,1)S(1)}, u32[]{:S(2)}, u32[]{:S(2)}) %collective-permute-start.37) | collective-permute-done | bytes 393248 | tf_op jit(solution)/shard_map/ppermute | solution.py:289
  287.3 1.4 collective-permute-start.38
  290.1 4.2 front.24.own_ref
  296.9 20.3 %collective-permute-done.40.wkv_ref = bf16[1536,1536]{1,0:T(8,128)(2,1)S(1)} collective-permute-done((bf16[1536,1536]{1,0:T(8,128)(2,1)S(1)}, bf16[1536,1536]{1,0:T(8,128)(2,1)S(1)}, u32[]{:S(2)}, u32[]{:S(2)}) %collective-permute-start.40) | collective-permute-done | bytes 4718624 | tf_op jit(solution)/shard_map/ppermute | solution.py:198
  317.2 3.4 collective-permute-start.41
  322.0 4.2 front.25.own_ref
  326.6 1.4 collective-permute-done.42.other_ref
  328.7 2.2 collective-permute-start.43
  330.9 8.1 %collective-permute-done.43.own_ref.hidden_ref = bf16[256,768]{1,0:T(8,128)(2,1)S(1)} collective-permute-done((bf16[256,768]{1,0:T(8,128)(2,1)S(1)}, bf16[256,768]{1,0:T(8,128)(2,1)S(1)}, u32[]{:S(2)}, u32[]{:S(2)}) %collective-permute-start.43) | collective-permute-done | bytes 393248 | tf_op jit(solution)/shard_map/ppermute | solution.py:289
  339.0 1.4 collective-permute-start.44
  341.7 4.2 front.26.own_ref
  350.3 4.2 front.27.own_ref
  354.9 1.4 collective-permute-done.47.other_ref
  358.4 1.4 collective-permute-done.49.other_ref
  359.8 4.2 front.28.own_ref
  364.4 1.4 collective-permute-done.50.other_ref
  367.0 1.4 collective-permute-done.51.other_ref
  368.4 4.2 front.29.own_ref
  373.0 1.4 collective-permute-done.52.other_ref
  376.5 1.4 collective-permute-done.54.other_ref
  377.9 4.2 front.30.own_ref
  382.5 1.4 collective-permute-done.55.other_ref
  385.1 1.4 collective-permute-done.56.other_ref
  386.5 5.0 %front.31.own_ref = bf16[256,768]{1,0:T(8,128)(2,1)} custom-call(bf16[256,768]{1,0:T(8,128)(2,1)S(1)} %back.30.own_ref.hidden_ref, bf16[256,768]{1,0:T(8,128)(2,1)S(1)} %collective-permute-done.56.other_ref, f32[6,768]{1,0:T(8,128)S(1)} %collective-permute-done.25.mod_ref, f32[2,128]{1,0:T(2,128)S(1)} %collective-permute-done.26.gain_ref, ...), custom_call_target="tpu_custom_call" | custom-call | tf_op jit(solution)/shard_map/front/pallas_call | solution.py:262
  391.8 1.7 collective-permute-done.57.other_ref
  393.5 1.9 back.31
  395.4 8.6 %all_to_all.20 = bf16[4,8,768]{2,1,0:T(8,128)(2,1)S(1)} all-to-all(bf16[4,8,768]{2,1,0:T(8,128)(2,1)S(1)} %fusion), channel_id=1, replica_groups={{0,1,2,3},{4,5,6,7},{8,9,10,11},{12,13,14,15},{16,17,18,19},{20,21,22,2..., dimensions={0} | all-to-all | bytes 98304 | tf_op jit(solution)/shard_map/all_to_all | solution.py:308
  404.2 30.8 %all_to_all.21.got_ref = bf16[8,2,8,192]{3,2,1,0:T(8,128)(2,1)S(1)} all-to-all(bf16[8,2,8,192]{3,2,1,0:T(8,128)(2,1)S(1)} %bitcast.28), channel_id=1, replica_groups=mesh['pipe'=8,'seq'=32] {'pipe'}, dimensions={0} | all-to-all | bytes 98304 | tf_op jit(solution)/shard_map/all_to_all | solution.py:313
  (129 shorter events, 69.1 us)
Async XLA Ops:
  1.1 4.3 collective-permute-start
  5.5 9.8 %collective-permute-start.1 = (bf16[96,1536]{1,0:T(8,128)(2,1)S(1)}, bf16[96,1536]{1,0:T(8,128)(2,1)S(1)}, u32[]{:S(2)}, u32[]{:S(2)}) collective-permute-start(bf16[96,1536]{1,0:T(8,128)(2,1)S(1)} %pad_maximum_fusion.1), channel_id=1, source_target_pairs={{0,2},{1,3},{2,0},{3,1},{4,6},{5,7},{6,4},{7,5},{8,10},{9,11},{10,... | collective-permute-start | bytes 884744 | tf_op jit(solution)/shard_map/ppermute | solution.py:188
  7.4 9.3 %all-to-all-start = ((bf16[8,2,8,192]{3,2,1,0:T(8,128)(2,1)}), bf16[8,2,8,192]{3,2,1,0:T(8,128)(2,1)S(1)}, u32[]{:S(2)}, u32[]{:S(2)}) async-start(bf16[8,2,8,192]{3,2,1,0:T(8,128)(2,1)} %broadcast_in_dim.6), calls=%async_computation | async-start | bytes 131072 | tf_op jit(solution)/shard_map/all_to_all | solution.py:191
  11.5 70.8 %copy-start = (f32[1,16,4608]{2,1,0:T(8,128)S(1)}, f32[1,16,4608]{2,1,0:T(8,128)}, u32[]{:S(2)}) copy-start(f32[1,16,4608]{2,1,0:T(8,128)} %refs_10_.1) | copy-start | bytes 884740
  11.5 70.8 %copy-start.1 = (s32[2,2]{1,0:T(2,128)S(1)}, s32[2,2]{1,0:T(2,128)}, u32[]{:S(2)}) copy-start(s32[2,2]{1,0:T(2,128)} %time_ref.3) | copy-start | bytes 52
  11.6 70.8 %copy-start.3 = (f32[1,2,128]{2,1,0:T(2,128)S(1)}, f32[1,2,128]{2,1,0:T(2,128)}, u32[]{:S(2)}) copy-start(f32[1,2,128]{2,1,0:T(2,128)} %refs_11_.1) | copy-start | bytes 3076
  15.4 66.5 %copy-start.4 = (bf16[192,1536]{1,0:T(8,128)(2,1)}, bf16[192,1536]{1,0:T(8,128)(2,1)S(1)}, u32[]{:S(2)}) copy-start(bf16[192,1536]{1,0:T(8,128)(2,1)S(1)} %pad_maximum_fusion.refs_0_) | copy-start | bytes 1769476
  16.7 16.2 %collective-permute-start.3 = (bf16[192,1536]{1,0:T(8,128)(2,1)S(1)}, bf16[192,1536]{1,0:T(8,128)(2,1)}, u32[]{:S(2)}, u32[]{:S(2)}) collective-permute-start(bf16[192,1536]{1,0:T(8,128)(2,1)S(1)} %pad_maximum_fusion.refs_0_), channel_id=1, source_target_pairs={{0,28},{1,29},{2,30},{3,31},{4,0},{5,1},{6,2},{7,3},{8,4},{9,5},{1... | collective-permute-start | bytes 1769480 | tf_op jit(solution)/shard_map/ppermute | solution.py:209
  22.3 13.7 %collective-permute-start.2 = (bf16[192,1536]{1,0:T(8,128)(2,1)S(1)}, bf16[192,1536]{1,0:T(8,128)(2,1)S(1)}, u32[]{:S(2)}, u32[]{:S(2)}) collective-permute-start(bf16[192,1536]{1,0:T(8,128)(2,1)S(1)} %pad_maximum_fusion.refs_0_), channel_id=1, source_target_pairs={{0,4},{1,5},{2,6},{3,7},{4,8},{5,9},{6,10},{7,11},{8,12},{9,13},{1... | collective-permute-start | bytes 1769480 | tf_op jit(solution)/shard_map/ppermute | solution.py:208
  36.0 12.9 %collective-permute-start.5 = (bf16[192,1536]{1,0:T(8,128)(2,1)S(1)}, bf16[192,1536]{1,0:T(8,128)(2,1)}, u32[]{:S(2)}, u32[]{:S(2)}) collective-permute-start(bf16[192,1536]{1,0:T(8,128)(2,1)S(1)} %collective-permute-done.2.refs_1_), channel_id=1, source_target_pairs={{0,4},{1,5},{2,6},{3,7},{4,8},{5,9},{6,10},{7,11},{8,12},{9,13},{1... | collective-permute-start | bytes 1769480 | tf_op jit(solution)/shard_map/ppermute | solution.py:208
  36.0 13.3 %collective-permute-start.6 = (bf16[192,1536]{1,0:T(8,128)(2,1)}, bf16[192,1536]{1,0:T(8,128)(2,1)}, u32[]{:S(2)}, u32[]{:S(2)}) collective-permute-start(bf16[192,1536]{1,0:T(8,128)(2,1)} %collective-permute-done.3.refs_2_), channel_id=1, source_target_pairs={{0,28},{1,29},{2,30},{3,31},{4,0},{5,1},{6,2},{7,3},{8,4},{9,5},{1... | collective-permute-start | bytes 1769480 | tf_op jit(solution)/shard_map/ppermute | solution.py:209
  39.6 22.7 %all-to-all-start.1 = ((bf16[32,8,768]{2,1,0:T(8,128)(2,1)}), bf16[32,8,768]{2,1,0:T(8,128)(2,1)S(1)}, u32[]{:S(2)}, u32[]{:S(2)}) async-start(bf16[32,8,768]{2,1,0:T(8,128)(2,1)} %bitcast.10), calls=%async_computation.1 | async-start | bytes 786432 | tf_op jit(solution)/shard_map/all_to_all | solution.py:225
  48.9 24.0 %collective-permute-start.7 = (bf16[192,1536]{1,0:T(8,128)(2,1)}, bf16[192,1536]{1,0:T(8,128)(2,1)S(1)}, u32[]{:S(2)}, u32[]{:S(2)}) collective-permute-start(bf16[192,1536]{1,0:T(8,128)(2,1)} %collective-permute-done.5.refs_3_), channel_id=1, source_target_pairs={{0,4},{1,5},{2,6},{3,7},{4,8},{5,9},{6,10},{7,11},{8,12},{9,13},{1... | collective-permute-start | bytes 1769480 | tf_op jit(solution)/shard_map/ppermute | solution.py:208
  49.2 23.8 %collective-permute-start.8 = (bf16[192,1536]{1,0:T(8,128)(2,1)}, bf16[192,1536]{1,0:T(8,128)(2,1)}, u32[]{:S(2)}, u32[]{:S(2)}) collective-permute-start(bf16[192,1536]{1,0:T(8,128)(2,1)} %collective-permute-done.6.refs_4_), channel_id=1, source_target_pairs={{0,28},{1,29},{2,30},{3,31},{4,0},{5,1},{6,2},{7,3},{8,4},{9,5},{1... | collective-permute-start | bytes 1769480 | tf_op jit(solution)/shard_map/ppermute | solution.py:209
  62.3 24.4 %collective-permute-start.4 = (bf16[256,768]{1,0:T(8,128)(2,1)S(1)}, bf16[256,768]{1,0:T(8,128)(2,1)S(1)}, u32[]{:S(2)}, u32[]{:S(2)}) collective-permute-start(bf16[256,768]{1,0:T(8,128)(2,1)S(1)} %bitcast.22), channel_id=1, source_target_pairs={{0,1},{1,0},{2,3},{3,2},{4,5},{5,4},{6,7},{7,6},{8,9},{9,8},{10,11... | collective-permute-start | bytes 1179656 | tf_op jit(solution)/shard_map/ppermute | solution.py:173
  72.9 8.7 %collective-permute-start.9 = (bf16[96,1536]{1,0:T(8,128)(2,1)S(1)}, bf16[96,1536]{1,0:T(8,128)(2,1)S(1)}, u32[]{:S(2)}, u32[]{:S(2)}) collective-permute-start(bf16[96,1536]{1,0:T(8,128)(2,1)S(1)} %slice.18), channel_id=1, source_target_pairs={{0,4},{1,5},{2,6},{3,7},{4,8},{5,9},{6,10},{7,11},{8,12},{9,13},{1... | collective-permute-start | bytes 884744 | tf_op jit(solution)/shard_map/ppermute | solution.py:215
  74.1 7.8 %collective-permute-start.10 = (bf16[96,1536]{1,0:T(8,128)(2,1)S(1)}, bf16[96,1536]{1,0:T(8,128)(2,1)}, u32[]{:S(2)}, u32[]{:S(2)}) collective-permute-start(bf16[96,1536]{1,0:T(8,128)(2,1)S(1)} %slice.19), channel_id=1, source_target_pairs={{0,28},{1,29},{2,30},{3,31},{4,0},{5,1},{6,2},{7,3},{8,4},{9,5},{1... | collective-permute-start | bytes 884744 | tf_op jit(solution)/shard_map/ppermute | solution.py:216
  90.9 3.5 collective-permute-start.11
  95.2 9.9 %collective-permute-start.12 = (bf16[256,768]{1,0:T(8,128)(2,1)S(1)}, bf16[256,768]{1,0:T(8,128)(2,1)S(1)}, u32[]{:S(2)}, u32[]{:S(2)}) collective-permute-start(bf16[256,768]{1,0:T(8,128)(2,1)S(1)} %back.16), channel_id=1, source_target_pairs={{0,32},{1,33},{2,34},{3,35},{4,36},{5,37},{6,38},{7,39},{8,40},{9,... | collective-permute-start | bytes 1179656 | tf_op jit(solution)/shard_map/ppermute | solution.py:289
  97.0 54.0 %collective-permute-start.18 = (bf16[1536,768]{1,0:T(8,128)(2,1)S(1)}, bf16[1536,768]{1,0:T(8,128)(2,1)S(1)}, u32[]{:S(2)}, u32[]{:S(2)}) collective-permute-start(bf16[1536,768]{1,0:T(8,128)(2,1)S(1)} %get-tuple-element.37.wq_ref), channel_id=1, source_target_pairs={{32,0},{96,64},{160,128},{224,192},{33,1},{97,65},{161,129},{225,1... | collective-permute-start | bytes 7077896 | tf_op jit(solution)/shard_map/ppermute | solution.py:198
  105.1 2.6 collective-permute-start.13
  111.8 1.8 collective-permute-start.14
  114.4 0.7 collective-permute-start.15
  115.1 2.2 collective-permute-start.16
  121.5 1.8 collective-permute-start.17
  151.0 2.0 collective-permute-start.19
  151.7 53.7 %collective-permute-start.27 = (bf16[1536,768]{1,0:T(8,128)(2,1)S(1)}, bf16[1536,768]{1,0:T(8,128)(2,1)S(1)}, u32[]{:S(2)}, u32[]{:S(2)}) collective-permute-start(bf16[1536,768]{1,0:T(8,128)(2,1)S(1)} %get-tuple-element.39.wo_ref), channel_id=1, source_target_pairs={{32,0},{96,64},{160,128},{224,192},{33,1},{97,65},{161,129},{225,1... | collective-permute-start | bytes 7077896 | tf_op jit(solution)/shard_map/ppermute | solution.py:198
  153.0 3.0 collective-permute-start.20
  160.2 1.8 collective-permute-start.21
  162.8 0.7 collective-permute-start.22
  163.5 2.0 collective-permute-start.23
  169.6 3.1 collective-permute-start.24
  170.1 35.3 %collective-permute-start.25 = (f32[6,768]{1,0:T(8,128)S(1)}, f32[6,768]{1,0:T(8,128)S(1)}, u32[]{:S(2)}, u32[]{:S(2)}) collective-permute-start(f32[6,768]{1,0:T(8,128)S(1)} %get-tuple-element.41.mod_ref), channel_id=1, source_target_pairs={{32,0},{96,64},{160,128},{224,192},{33,1},{97,65},{161,129},{225,1... | collective-permute-start | bytes 55304 | tf_op jit(solution)/shard_map/ppermute | solution.py:198
  171.4 34.0 %collective-permute-start.26 = (f32[2,128]{1,0:T(2,128)S(1)}, f32[2,128]{1,0:T(2,128)S(1)}, u32[]{:S(2)}, u32[]{:S(2)}) collective-permute-start(f32[2,128]{1,0:T(2,128)S(1)} %get-tuple-element.36.gain_ref), channel_id=1, source_target_pairs={{32,0},{96,64},{160,128},{224,192},{33,1},{97,65},{161,129},{225,1... | collective-permute-start | bytes 3080 | tf_op jit(solution)/shard_map/ppermute | solution.py:198
  205.4 2.0 collective-permute-start.28
  206.1 111.1 %collective-permute-start.40 = (bf16[1536,1536]{1,0:T(8,128)(2,1)S(1)}, bf16[1536,1536]{1,0:T(8,128)(2,1)S(1)}, u32[]{:S(2)}, u32[]{:S(2)}) collective-permute-start(bf16[1536,1536]{1,0:T(8,128)(2,1)S(1)} %get-tuple-element.38.wkv_ref), channel_id=1, source_target_pairs={{32,0},{96,64},{160,128},{224,192},{33,1},{97,65},{161,129},{225,1... | collective-permute-start | bytes 14155784 | tf_op jit(solution)/shard_map/ppermute | solution.py:198
  207.4 3.9 collective-permute-start.29
  215.5 1.8 collective-permute-start.30
  218.1 0.7 collective-permute-start.31
  218.8 2.0 collective-permute-start.32
  225.0 1.8 collective-permute-start.33
  227.6 0.7 collective-permute-start.34
  228.3 1.8 collective-permute-start.35
  234.3 1.8 collective-permute-start.36
  236.9 49.8 %collective-permute-start.37 = (bf16[256,768]{1,0:T(8,128)(2,1)S(1)}, bf16[256,768]{1,0:T(8,128)(2,1)S(1)}, u32[]{:S(2)}, u32[]{:S(2)}) collective-permute-start(bf16[256,768]{1,0:T(8,128)(2,1)S(1)} %back.23), channel_id=1, source_target_pairs={{224,0},{225,1},{226,2},{227,3},{228,4},{229,5},{230,6},{231,7},{2... | collective-permute-start | bytes 1179656 | tf_op jit(solution)/shard_map/ppermute | solution.py:289
  287.3 2.8 collective-permute-start.38
  294.3 1.8 collective-permute-start.39
  317.2 4.8 %collective-permute-start.41 = (bf16[256,768]{1,0:T(8,128)(2,1)S(1)}, bf16[256,768]{1,0:T(8,128)(2,1)S(1)}, u32[]{:S(2)}, u32[]{:S(2)}) collective-permute-start(bf16[256,768]{1,0:T(8,128)(2,1)S(1)} %back.24.own_ref.hidden_ref), channel_id=1, source_target_pairs={{0,1},{1,0},{2,3},{3,2},{4,5},{5,4},{6,7},{7,6},{8,9},{9,8},{10,11... | collective-permute-start | bytes 1179656 | tf_op jit(solution)/shard_map/ppermute | solution.py:173
  326.1 1.8 collective-permute-start.42
  328.7 10.3 %collective-permute-start.43 = (bf16[256,768]{1,0:T(8,128)(2,1)S(1)}, bf16[256,768]{1,0:T(8,128)(2,1)S(1)}, u32[]{:S(2)}, u32[]{:S(2)}) collective-permute-start(bf16[256,768]{1,0:T(8,128)(2,1)S(1)} %back.25), channel_id=1, source_target_pairs={{0,64},{1,65},{2,66},{3,67},{4,68},{5,69},{6,70},{7,71},{8,72},{9,... | collective-permute-start | bytes 1179656 | tf_op jit(solution)/shard_map/ppermute | solution.py:289
  339.0 2.7 collective-permute-start.44
  345.9 1.8 collective-permute-start.45
  348.5 1.8 collective-permute-start.46
  354.5 1.8 collective-permute-start.47
  357.1 0.7 collective-permute-start.48
  357.8 2.0 collective-permute-start.49
  363.9 1.8 collective-permute-start.50
  366.5 1.8 collective-permute-start.51
  372.5 1.8 collective-permute-start.52
  375.1 0.7 collective-permute-start.53
  375.8 2.1 collective-permute-start.54
  382.1 1.8 collective-permute-start.55
  384.7 1.8 collective-permute-start.56
  391.4 2.1 collective-permute-start.57
  (5 other events, 80.7 us)

commit v4 on v3

--- a/solution.py
+++ b/solution.py
@@ -13,7 +13,7 @@
 def layer_front(head_dim):
     score_scale = 1.0 / math.sqrt(head_dim)
 
-    def body(own_ref, other_ref, mod_ref, gain_ref, wq_ref, wkv_ref, out_ref):
+    def body(own_ref, other_ref, mod_ref, gain_ref, weight_ref, out_ref):
         half = own_ref.shape[1]
         width = 2 * half
         own = own_ref[...].astype(jnp.float32)
@@ -37,7 +37,7 @@
         own = modulated(own, 0)
         other = modulated(other, 1)
 
-        def project(weight_ref, start, size):
+        def project(start, size):
             cols = slice(start, start + size)
             return jnp.dot(
                 own, weight_ref[:half, cols], preferred_element_type=jnp.float32
@@ -51,9 +51,9 @@
         gain_key = gain_ref[1:2, :]
         group = 2 * head_dim
         for start in range(0, half, group):
-            queries = project(wq_ref, start, group)
-            keys = project(wkv_ref, start, group)
-            values = project(wkv_ref, half + start, group).astype(jnp.bfloat16)
+            queries = project(start, group)
+            keys = project(half + start, group)
+            values = project(2 * half + start, group).astype(jnp.bfloat16)
             for at in range(0, group, head_dim):
                 query_head = rms(queries[:, at : at + head_dim], gain_query)
                 key_head = rms(keys[:, at : at + head_dim], gain_key)
@@ -80,11 +80,12 @@
     return body
 
 
-def layer_back(own_ref, other_ref, hidden_ref, mod_ref, wo_ref, out_ref):
+def layer_back(own_ref, other_ref, hidden_ref, mod_ref, weight_ref, out_ref):
     half = own_ref.shape[1]
+    cols = slice(3 * half, 4 * half)
     projected = jnp.dot(
-        own_ref[...], wo_ref[:half, :], preferred_element_type=jnp.float32
-    ) + jnp.dot(other_ref[...], wo_ref[half:, :], preferred_element_type=jnp.float32)
+        own_ref[...], weight_ref[:half, cols], preferred_element_type=jnp.float32
+    ) + jnp.dot(other_ref[...], weight_ref[half:, cols], preferred_element_type=jnp.float32)
     out_ref[...] = (
         hidden_ref[...].astype(jnp.float32) + mod_ref[4:5, :] * projected
     ).astype(jnp.bfloat16)
@@ -93,11 +94,16 @@
 def load_own(spots):
     def body(word_ref, *refs):
         part_refs = refs[: len(spots)]
-        time_ref, mod_ref, gain_ref, query_ref, out_ref = refs[len(spots) : len(spots) + 5]
-        query_held, kv_held, out_held, gain_held = refs[len(spots) + 5 : len(spots) + 9]
-        mods_held, sems = refs[len(spots) + 9 : -1], refs[-1]
+        time_ref, mod_ref, gain_ref, next_mod_ref, next_gain_ref, query_ref, out_ref = refs[
+            len(spots) : len(spots) + 7
+        ]
+        held_ref, gain_held, next_gain_held, next_mods_held = refs[
+            len(spots) + 7 : len(spots) + 11
+        ]
+        mods_held, sems = refs[len(spots) + 11 : -1], refs[-1]
         core = word_ref[0]
-        width, half = query_held.shape
+        width = held_ref.shape[0]
+        half = width // 2
         block = part_refs[0].shape[0]
         ring = width // block
         copies = []
@@ -108,24 +114,33 @@
         for (turn, start), part_ref in zip(spots, part_refs):
             rows = part_ref.shape[0]
             at = lax.rem(word_ref[2] + turn + core * (ring // 2), ring) * block + start
-            copied(part_ref, kv_held.at[pl.ds(pl.multiple_of(at, rows), rows), :])
+            copied(
+                part_ref, held_ref.at[pl.ds(pl.multiple_of(at, rows), rows), pl.ds(half, width)]
+            )
         cols = pl.ds(pl.multiple_of(core * half, half), half)
-        for source, held in ((query_ref, query_held), (out_ref, out_held)):
+        for source, left in ((query_ref, 0), (out_ref, half + width)):
             for side in range(2):
                 first = pl.multiple_of(lax.rem(core + side, 2) * half, half)
                 copied(
-                    source.at[0, pl.ds(first, half), cols], held.at[pl.ds(side * half, half), :]
+                    source.at[0, pl.ds(first, half), cols],
+                    held_ref.at[pl.ds(side * half, half), pl.ds(left, half)],
                 )
         for copy in copies:
             copy.start()
         gain_held[...] = gain_ref[0]
-        for step, held in enumerate(mods_held):
+        next_gain_held[...] = next_gain_ref[0]
+
+        def picked(table_ref, step, held):
             row = pl.ds(time_ref[step, word_ref[1]], 1)
             for third in range(3):
                 for side in range(2):
                     first = (2 * third + lax.rem(core + side, 2)) * half
                     first = pl.ds(pl.multiple_of(first, half), half)
-                    held[2 * third + side : 2 * third + side + 1, :] = mod_ref[0, row, first]
+                    held[2 * third + side : 2 * third + side + 1, :] = table_ref[0, row, first]
+
+        for step, held in enumerate(mods_held):
+            picked(mod_ref, step, held)
+        picked(next_mod_ref, len(mods_held) - 1, next_mods_held)
         for copy in copies:
             copy.wait()
 
@@ -224,25 +239,26 @@
     )
     slot = lax.all_to_all(sent, "seq", 0, 0, tiled=True).reshape(tokens, half)
 
+    next_table, next_gain = to_even(mod_table), to_even(qk_gain)
+    parts[-1], next_table, next_gain = lax.optimization_barrier(
+        (parts[-1], next_table, next_gain)
+    )
     words = jnp.stack([core, micro, seq_at // 4]).astype(jnp.int32)
     smem = pl.BlockSpec(memory_space=pltpu.SMEM)
     vmem = pl.BlockSpec(memory_space=pltpu.VMEM)
     hbm = pl.BlockSpec(memory_space=pltpu.HBM)
-    held_shapes = [
-        jax.ShapeDtypeStruct(shape, jnp.bfloat16)
-        for shape in ((width, half), (width, width), (width, half))
-    ]
-    small_shapes = [jax.ShapeDtypeStruct(qk_gain.shape[1:], jnp.float32)] + [
+    held_shape = jax.ShapeDtypeStruct((width, 2 * width), jnp.bfloat16)
+    small_shapes = [jax.ShapeDtypeStruct(qk_gain.shape[1:], jnp.float32)] * 2 + [
         jax.ShapeDtypeStruct((6, half), jnp.float32)
-    ] * step_count
+    ] * (1 + step_count)
 
     def in_hbm(value):
         return pltpu.with_memory_space_constraint(value, pltpu.HBM)
 
     loaded = pl.pallas_call(
         load_own(spots),
-        out_shape=held_shapes + small_shapes,
-        in_specs=[smem] + [hbm] * len(parts) + [smem, vmem, vmem, hbm, hbm],
+        out_shape=[held_shape] + small_shapes,
+        in_specs=[smem] + [hbm] * len(parts) + [smem] + [vmem] * 4 + [hbm, hbm],
         out_specs=[vmem] * (4 + step_count),
         scratch_shapes=[pltpu.SemaphoreType.DMA((len(parts) + 4,))],
         compiler_params=pltpu.CompilerParams(vmem_limit_bytes=12 << 20),
@@ -253,20 +269,23 @@
         timesteps,
         mod_table,
         qk_gain,
+        next_table,
+        next_gain,
         in_hbm(w_query),
         in_hbm(w_out),
     )
-    held, gains, mods = loaded[:3], loaded[3], loaded[4:]
-
-    def layer(hidden, mods, gains, query_part, kv_part, out_part):
+    held, gains, next_gains, next_mods = loaded[:4]
+    mods = loaded[4:]
+
+    def layer(hidden, mods, gains, weights):
         attended = pl.pallas_call(
             layer_front(head_dim),
             out_shape=jax.ShapeDtypeStruct((tokens, half), jnp.bfloat16),
-            in_specs=[vmem] * 6,
+            in_specs=[vmem] * 5,
             out_specs=vmem,
             compiler_params=pltpu.CompilerParams(vmem_limit_bytes=16 << 20),
             name="front",
-        )(hidden, swapped(hidden), mods, gains, query_part, kv_part)
+        )(hidden, swapped(hidden), mods, gains, weights)
         return pl.pallas_call(
             layer_back,
             out_shape=jax.ShapeDtypeStruct((tokens, half), jnp.bfloat16),
@@ -274,10 +293,9 @@
             out_specs=vmem,
             compiler_params=pltpu.CompilerParams(vmem_limit_bytes=12 << 20),
             name="back",
-        )(attended, swapped(attended), hidden, mods, out_part)
-
-    following = [to_even(value) for value in (mods[-1], gains, *held)]
-    due = {2: (2,), 4: (0, 1, 4), n_pipe: (3,)}
+        )(attended, swapped(attended), hidden, mods, weights)
+
+    following = [next_mods, next_gains, to_even(held)]
 
     holder = 0
     hidden = slot
@@ -289,6 +307,7 @@
                 hidden = lax.ppermute(hidden, "pipe", [(holder, place)])
                 holder = place
             if step > 0 and section == 0:
+                hidden, following[2] = lax.optimization_barrier((hidden, following[2]))
                 slot = pl.pallas_call(
                     advance_slot(step - 1),
                     out_shape=jax.ShapeDtypeStruct((tokens, half), jnp.bfloat16),
@@ -298,9 +317,7 @@
                     name="advance_slot",
                 )(words, timesteps, step_sizes, slot, hidden)
                 hidden = slot
-            hidden = layer(hidden, *(following if section != place else (mods[step], gains, *held)))
-            for at in due.get(step * n_pipe + section, ()):
-                hidden, following[at] = lax.optimization_barrier((hidden, following[at]))
+            hidden = layer(hidden, *(following if section != place else (mods[step], gains, held)))
 
     kept = jnp.where(pipe_at == 0, slot, hidden)
     kept = lax.dynamic_slice_in_dim(kept, (seq_at // 4) * 4 * row_share, 4 * row_share, 0)

time: 444 us -> 436 us (0.982)
  waiting for transfers between devices: 228 us -> 219 us
  local copies, waits for them, and re-layouts: 4.31 us -> 8.77 us
    ppermute x5 -> x3, waiting for transfers between devices: 79.1 us -> 40.8 us  [to_even(): return lax.ppermute(value, 'pipe', backward)]
    ppermute x11, waiting for transfers between devices: 63.4 us -> 95.7 us  [shards(): hidden = lax.ppermute(hidden, 'pipe', [(holder, place)])]
    ppermute x3, waiting for transfers between devices: 10.6 us -> 20.8 us  [shards(): falling = lax.ppermute(falling, 'seq', rings[1])]
    ppermute x3, waiting for transfers between devices: 12.1 us -> 3.13 us  [shards(): rising = lax.ppermute(rising, 'seq', rings[0])]
    ppermute x1, waiting for transfers between devices: 4.57 us -> 0.01 us  [shards(): lax.ppermute(rising[:middle], 'seq', rings[0])]
  transfers between devices with their start and end apart: 60 -> 58, of which waited for: 46 -> 43; matrix products, arithmetic and copies ran while one was open for 1% -> 1% of each run, Pallas kernels for 10% -> 10%
where the time goes in v4:
time: 436 us; the launch traced here: 428 us
  waiting for transfers between devices  219 us (50%)
  Pallas kernels  85.2 us (20%)
  starting transfers between devices  73.1 us (17%)
  blocking collectives  41.2 us (9%)
  local copies, waits for them, and re-layouts  8.77 us (2%)
    ppermute x11, waiting for transfers between devices, shards(): hidden = lax.ppermute(hidden, 'pipe', [(holder, place)])  95.7 us
    pallas_call x16, Pallas kernels, layer(): pl.pallas_call(layer_front(head_dim), out_shape=jax.ShapeDtypeStruct((tok...  66.2 us
    ppermute x33, waiting for transfers between devices, swapped(): return lax.ppermute(value, 'seq', core_pairs)  42.9 us
    ppermute x3, waiting for transfers between devices, to_even(): return lax.ppermute(value, 'pipe', backward)  40.8 us
    all_to_all x1, blocking collectives, shards(): got = lax.all_to_all(sent, 'pipe', 0, 0, tiled=True)  30.8 us
    ppermute x33, starting transfers between devices, swapped(): return lax.ppermute(value, 'seq', core_pairs)  28 us
    ppermute x3, waiting for transfers between devices, shards(): falling = lax.ppermute(falling, 'seq', rings[1])  20.8 us
    ppermute x11, starting transfers between devices, shards(): hidden = lax.ppermute(hidden, 'pipe', [(holder, place)])  13.9 us
  transfers between devices with their start and end apart: 58, of which 43 were waited for; matrix products, arithmetic and copies ran while one was open for 1% of the time, Pallas kernels for 10%

profile of v4, /device:TPU:1, one launch (start us, length us, event | category | flops | bytes accessed | tf_op | source)
XLA Modules:
  0.0 428.1 jit_solution(460027837062019499)
XLA Ops:
  1.1 3.3 collective-permute-start
  8.2 4.1 all-to-all-start
  12.3 3.1 collective-permute-done.1
  15.5 2.0 all-to-all-done
  17.4 5.6 %collective-permute-start.3 = (bf16[192,1536]{1,0:T(8,128)(2,1)S(1)}, bf16[192,1536]{1,0:T(8,128)(2,1)S(1)}, u32[]{:S(2)}, u32[]{:S(2)}) collective-permute-start(bf16[192,1536]{1,0:T(8,128)(2,1)S(1)} %pad_maximum_fusion.refs_0_), channel_id=1, source_target_pairs={{0,28},{1,29},{2,30},{3,31},{4,0},{5,1},{6,2},{7,3},{8,4},{9,5},{1... | collective-permute-start | bytes 1769480 | tf_op jit(solution)/shard_map/ppermute | solution.py:224
  23.0 10.6 %collective-permute-done.3.refs_2_ = bf16[192,1536]{1,0:T(8,128)(2,1)S(1)} collective-permute-done((bf16[192,1536]{1,0:T(8,128)(2,1)S(1)}, bf16[192,1536]{1,0:T(8,128)(2,1)S(1)}, u32[]{:S(2)}, u32[]{:S(2)}) %collective-permute-start.3) | collective-permute-done | bytes 589856 | tf_op jit(solution)/shard_map/ppermute | solution.py:224
  33.6 3.1 collective-permute-done.2.refs_1_
  38.2 10.2 %collective-permute-done.6.refs_4_ = bf16[192,1536]{1,0:T(8,128)(2,1)} collective-permute-done((bf16[192,1536]{1,0:T(8,128)(2,1)S(1)}, bf16[192,1536]{1,0:T(8,128)(2,1)}, u32[]{:S(2)}, u32[]{:S(2)}) %collective-permute-start.6) | collective-permute-done | bytes 589856 | tf_op jit(solution)/shard_map/ppermute | solution.py:224
  48.4 1.8 collective-permute-start.8
  51.3 10.1 %all-to-all-start.1 = ((bf16[32,8,768]{2,1,0:T(8,128)(2,1)}), bf16[32,8,768]{2,1,0:T(8,128)(2,1)S(1)}, u32[]{:S(2)}, u32[]{:S(2)}) async-start(bf16[32,8,768]{2,1,0:T(8,128)(2,1)} %bitcast.10), calls=%async_computation.1 | async-start | bytes 786432 | tf_op jit(solution)/shard_map/all_to_all | solution.py:240
  63.5 2.7 collective-permute-start.10
  68.3 8.6 %all-to-all-done.1 = bf16[32,8,768]{2,1,0:T(8,128)(2,1)S(1)} async-done(((bf16[32,8,768]{2,1,0:T(8,128)(2,1)}), bf16[32,8,768]{2,1,0:T(8,128)(2,1)S(1)}, u32[]{:S(2)}, u32[]{:S(2)}) %all-to-all-start.1) | async-done | bytes 393248 | tf_op jit(solution)/shard_map/all_to_all | solution.py:240
  77.5 1.6 collective-permute-done.10.refs_8_
  79.1 4.5 %load_own.1 = (bf16[1536,3072]{1,0:T(8,128)(2,1)S(1)}, f32[2,128]{1,0:T(2,128)S(1)}, f32[2,128]{1,0:T(2,128)S(1)}, f32[6,768]{1,0:T(8,128)S(1)}, f32[6,768]{1,0:T(8,128)S(1)}, /*index=5*/f32[6,768]{1,0:T(8,128)S(1)}) custom-call(s32[3]{0:T(128)S(1)} %pad_add_fusion.word_ref, bf16[192,1536]{1,0:T(8,128)(2,1)} %copy-done.6, bf16[192,1536]{1,0:T(8,128)(2,1)} %copy-done.10, ...), custom_call_target="tpu_custom_call" | custom-call | tf_op jit(solution)/shard_map/load_own/pallas_call | solution.py:258
  83.6 1.5 collective-permute-start.36
  85.1 4.1 front.16.own_ref
  89.2 3.3 collective-permute-start.13
  94.7 4.9 %collective-permute-start.14 = (bf16[256,768]{1,0:T(8,128)(2,1)S(1)}, bf16[256,768]{1,0:T(8,128)(2,1)S(1)}, u32[]{:S(2)}, u32[]{:S(2)}) collective-permute-start(bf16[256,768]{1,0:T(8,128)(2,1)S(1)} %back.16), channel_id=1, source_target_pairs={{0,32},{1,33},{2,34},{3,35},{4,36},{5,37},{6,38},{7,39},{8,40},{9,... | collective-permute-start | bytes 1179656 | tf_op jit(solution)/shard_map/ppermute | solution.py:307
  99.6 8.1 %collective-permute-done.14.own_ref.hidden_ref = bf16[256,768]{1,0:T(8,128)(2,1)S(1)} collective-permute-done((bf16[256,768]{1,0:T(8,128)(2,1)S(1)}, bf16[256,768]{1,0:T(8,128)(2,1)S(1)}, u32[]{:S(2)}, u32[]{:S(2)}) %collective-permute-start.14) | collective-permute-done | bytes 393248 | tf_op jit(solution)/shard_map/ppermute | solution.py:307
  108.9 1.3 collective-permute-done.15.other_ref
  110.3 4.1 front.17.own_ref
  114.9 1.3 collective-permute-done.16.other_ref
  119.9 4.1 front.18.own_ref
  129.2 4.1 front.19.own_ref
  138.6 4.1 front.20.own_ref
  143.2 1.4 collective-permute-done.25.other_ref
  146.6 1.4 collective-permute-done.27.other_ref
  147.9 4.1 front.21.own_ref
  152.5 1.4 collective-permute-done.28.other_ref
  156.0 1.4 collective-permute-done.30.other_ref
  157.4 4.1 front.22.own_ref
  162.0 1.4 collective-permute-done.31.other_ref
  165.3 1.4 collective-permute-done.33.other_ref
  166.7 4.1 front.23.own_ref
  171.3 1.4 collective-permute-done.34.other_ref
  174.7 79.5 %collective-permute-done.35.hidden_ref = bf16[256,768]{1,0:T(8,128)(2,1)S(1)} collective-permute-done((bf16[256,768]{1,0:T(8,128)(2,1)S(1)}, bf16[256,768]{1,0:T(8,128)(2,1)S(1)}, u32[]{:S(2)}, u32[]{:S(2)}) %collective-permute-start.35) | collective-permute-done | bytes 393248 | tf_op jit(solution)/shard_map/ppermute | solution.py:307
  254.3 40.8 %collective-permute-done.36.weight_ref = bf16[1536,3072]{1,0:T(8,128)(2,1)S(1)} collective-permute-done((bf16[1536,3072]{1,0:T(8,128)(2,1)S(1)}, bf16[1536,3072]{1,0:T(8,128)(2,1)S(1)}, u32[]{:S(2)}, u32[]{:S(2)}) %collective-permute-start.36) | collective-permute-done | bytes 9437216 | tf_op jit(solution)/shard_map/ppermute | solution.py:213
  295.7 4.7 %collective-permute-start.37 = (bf16[256,768]{1,0:T(8,128)(2,1)S(1)}, bf16[256,768]{1,0:T(8,128)(2,1)S(1)}, u32[]{:S(2)}, u32[]{:S(2)}) collective-permute-start(bf16[256,768]{1,0:T(8,128)(2,1)S(1)} %advance_slot.1.own_ref.hidden_ref), channel_id=1, source_target_pairs={{0,1},{1,0},{2,3},{3,2},{4,5},{5,4},{6,7},{7,6},{8,9},{9,8},{10,11... | collective-permute-start | bytes 1179656 | tf_op jit(solution)/shard_map/ppermute | solution.py:188
  301.8 4.1 front.24.own_ref
  306.4 1.4 collective-permute-done.38.other_ref
  310.3 4.1 front.25.own_ref
  314.9 1.4 collective-permute-done.40.other_ref
  317.1 2.2 collective-permute-start.41
  319.3 8.1 %collective-permute-done.41.own_ref.hidden_ref = bf16[256,768]{1,0:T(8,128)(2,1)S(1)} collective-permute-done((bf16[256,768]{1,0:T(8,128)(2,1)S(1)}, bf16[256,768]{1,0:T(8,128)(2,1)S(1)}, u32[]{:S(2)}, u32[]{:S(2)}) %collective-permute-start.41) | collective-permute-done | bytes 393248 | tf_op jit(solution)/shard_map/ppermute | solution.py:307
  327.4 1.4 collective-permute-start.42
  330.1 4.1 front.26.own_ref
  334.7 1.4 collective-permute-done.43.other_ref
  337.3 1.4 collective-permute-done.44.other_ref
  338.6 4.1 front.27.own_ref
  343.2 1.4 collective-permute-done.45.other_ref
  348.1 4.1 front.28.own_ref
  352.7 1.4 collective-permute-done.48.other_ref
  355.3 1.4 collective-permute-done.49.other_ref
  356.7 4.1 front.29.own_ref
  361.3 1.4 collective-permute-done.50.other_ref
  364.8 1.4 collective-permute-done.52.other_ref
  366.2 4.1 front.30.own_ref
  370.8 1.4 collective-permute-done.53.other_ref
  373.4 1.4 collective-permute-done.54.other_ref
  374.7 4.1 front.31.own_ref
  379.3 1.4 collective-permute-done.55.other_ref
  380.7 3.7 copy-done.1
  385.2 10.4 %all_to_all.20 = bf16[4,8,768]{2,1,0:T(8,128)(2,1)S(1)} all-to-all(bf16[4,8,768]{2,1,0:T(8,128)(2,1)S(1)} %fusion), channel_id=1, replica_groups={{0,1,2,3},{4,5,6,7},{8,9,10,11},{12,13,14,15},{16,17,18,19},{20,21,22,2..., dimensions={0} | all-to-all | bytes 98304 | tf_op jit(solution)/shard_map/all_to_all | solution.py:325
  395.8 30.8 %all_to_all.21.got_ref = bf16[8,2,8,192]{3,2,1,0:T(8,128)(2,1)S(1)} all-to-all(bf16[8,2,8,192]{3,2,1,0:T(8,128)(2,1)S(1)} %bitcast.28), channel_id=1, replica_groups=mesh['pipe'=8,'seq'=32] {'pipe'}, dimensions={0} | all-to-all | bytes 98304 | tf_op jit(solution)/shard_map/all_to_all | solution.py:330
  (129 shorter events, 62.0 us)
Async XLA Ops:
  0.0 61.4 %copy-start.2 = (f32[1,16,4608]{2,1,0:T(8,128)S(1)}, f32[1,16,4608]{2,1,0:T(8,128)}, u32[]{:S(2)}) copy-start(f32[1,16,4608]{2,1,0:T(8,128)} %refs_10_.1) | copy-start | bytes 884740
  0.0 67.0 %copy-start.5 = (f32[1,2,128]{2,1,0:T(2,128)S(1)}, f32[1,2,128]{2,1,0:T(2,128)}, u32[]{:S(2)}) copy-start(f32[1,2,128]{2,1,0:T(2,128)} %refs_11_.1) | copy-start | bytes 3076
  0.0 79.1 %copy-start.3 = (s32[2,2]{1,0:T(2,128)S(1)}, s32[2,2]{1,0:T(2,128)}, u32[]{:S(2)}) copy-start(s32[2,2]{1,0:T(2,128)} %time_ref.3) | copy-start | bytes 52
  1.1 4.3 %collective-permute-start = (bf16[48,1536]{1,0:T(8,128)(2,1)S(1)}, bf16[48,1536]{1,0:T(8,128)(2,1)S(1)}, u32[]{:S(2)}, u32[]{:S(2)}) collective-permute-start(bf16[48,1536]{1,0:T(8,128)(2,1)S(1)} %pad_maximum_fusion.3), channel_id=1, source_target_pairs={{0,1},{1,0},{2,3},{3,2},{4,5},{5,4},{6,7},{7,6},{8,9},{9,8},{10,11... | collective-permute-start | bytes 442376 | tf_op jit(solution)/shard_map/ppermute | solution.py:188
  5.5 9.8 %collective-permute-start.1 = (bf16[96,1536]{1,0:T(8,128)(2,1)S(1)}, bf16[96,1536]{1,0:T(8,128)(2,1)S(1)}, u32[]{:S(2)}, u32[]{:S(2)}) collective-permute-start(bf16[96,1536]{1,0:T(8,128)(2,1)S(1)} %pad_maximum_fusion.1), channel_id=1, source_target_pairs={{0,2},{1,3},{2,0},{3,1},{4,6},{5,7},{6,4},{7,5},{8,10},{9,11},{10,... | collective-permute-start | bytes 884744 | tf_op jit(solution)/shard_map/ppermute | solution.py:203
  8.2 9.3 %all-to-all-start = ((bf16[8,2,8,192]{3,2,1,0:T(8,128)(2,1)}), bf16[8,2,8,192]{3,2,1,0:T(8,128)(2,1)S(1)}, u32[]{:S(2)}, u32[]{:S(2)}) async-start(bf16[8,2,8,192]{3,2,1,0:T(8,128)(2,1)} %broadcast_in_dim.6), calls=%async_computation | async-start | bytes 131072 | tf_op jit(solution)/shard_map/all_to_all | solution.py:206
  15.5 63.6 %copy-start.6 = (bf16[192,1536]{1,0:T(8,128)(2,1)}, bf16[192,1536]{1,0:T(8,128)(2,1)S(1)}, u32[]{:S(2)}) copy-start(bf16[192,1536]{1,0:T(8,128)(2,1)S(1)} %pad_maximum_fusion.refs_0_) | copy-start | bytes 1769476
  17.4 16.2 %collective-permute-start.3 = (bf16[192,1536]{1,0:T(8,128)(2,1)S(1)}, bf16[192,1536]{1,0:T(8,128)(2,1)S(1)}, u32[]{:S(2)}, u32[]{:S(2)}) collective-permute-start(bf16[192,1536]{1,0:T(8,128)(2,1)S(1)} %pad_maximum_fusion.refs_0_), channel_id=1, source_target_pairs={{0,28},{1,29},{2,30},{3,31},{4,0},{5,1},{6,2},{7,3},{8,4},{9,5},{1... | collective-permute-start | bytes 1769480 | tf_op jit(solution)/shard_map/ppermute | solution.py:224
  23.0 13.7 %collective-permute-start.2 = (bf16[192,1536]{1,0:T(8,128)(2,1)S(1)}, bf16[192,1536]{1,0:T(8,128)(2,1)S(1)}, u32[]{:S(2)}, u32[]{:S(2)}) collective-permute-start(bf16[192,1536]{1,0:T(8,128)(2,1)S(1)} %pad_maximum_fusion.refs_0_), channel_id=1, source_target_pairs={{0,4},{1,5},{2,6},{3,7},{4,8},{5,9},{6,10},{7,11},{8,12},{9,13},{1... | collective-permute-start | bytes 1769480 | tf_op jit(solution)/shard_map/ppermute | solution.py:223
  36.7 11.7 %collective-permute-start.6 = (bf16[192,1536]{1,0:T(8,128)(2,1)S(1)}, bf16[192,1536]{1,0:T(8,128)(2,1)}, u32[]{:S(2)}, u32[]{:S(2)}) collective-permute-start(bf16[192,1536]{1,0:T(8,128)(2,1)S(1)} %collective-permute-done.3.refs_2_), channel_id=1, source_target_pairs={{0,28},{1,29},{2,30},{3,31},{4,0},{5,1},{6,2},{7,3},{8,4},{9,5},{1... | collective-permute-start | bytes 1769480 | tf_op jit(solution)/shard_map/ppermute | solution.py:224
  37.1 13.2 %collective-permute-start.5 = (bf16[192,1536]{1,0:T(8,128)(2,1)S(1)}, bf16[192,1536]{1,0:T(8,128)(2,1)}, u32[]{:S(2)}, u32[]{:S(2)}) collective-permute-start(bf16[192,1536]{1,0:T(8,128)(2,1)S(1)} %collective-permute-done.2.refs_1_), channel_id=1, source_target_pairs={{0,4},{1,5},{2,6},{3,7},{4,8},{5,9},{6,10},{7,11},{8,12},{9,13},{1... | collective-permute-start | bytes 1769480 | tf_op jit(solution)/shard_map/ppermute | solution.py:223
  48.4 14.3 %collective-permute-start.8 = (bf16[192,1536]{1,0:T(8,128)(2,1)}, bf16[192,1536]{1,0:T(8,128)(2,1)S(1)}, u32[]{:S(2)}, u32[]{:S(2)}) collective-permute-start(bf16[192,1536]{1,0:T(8,128)(2,1)} %collective-permute-done.6.refs_4_), channel_id=1, source_target_pairs={{0,28},{1,29},{2,30},{3,31},{4,0},{5,1},{6,2},{7,3},{8,4},{9,5},{1... | collective-permute-start | bytes 1769480 | tf_op jit(solution)/shard_map/ppermute | solution.py:224
  50.3 15.9 %collective-permute-start.7 = (bf16[192,1536]{1,0:T(8,128)(2,1)}, bf16[192,1536]{1,0:T(8,128)(2,1)S(1)}, u32[]{:S(2)}, u32[]{:S(2)}) collective-permute-start(bf16[192,1536]{1,0:T(8,128)(2,1)} %collective-permute-done.5.refs_3_), channel_id=1, source_target_pairs={{0,4},{1,5},{2,6},{3,7},{4,8},{5,9},{6,10},{7,11},{8,12},{9,13},{1... | collective-permute-start | bytes 1769480 | tf_op jit(solution)/shard_map/ppermute | solution.py:223
  51.3 25.6 %all-to-all-start.1 = ((bf16[32,8,768]{2,1,0:T(8,128)(2,1)}), bf16[32,8,768]{2,1,0:T(8,128)(2,1)S(1)}, u32[]{:S(2)}, u32[]{:S(2)}) async-start(bf16[32,8,768]{2,1,0:T(8,128)(2,1)} %bitcast.10), calls=%async_computation.1 | async-start | bytes 786432 | tf_op jit(solution)/shard_map/all_to_all | solution.py:240
  61.4 16.0 %collective-permute-start.11 = (f32[1,16,4608]{2,1,0:T(8,128)S(1)}, f32[1,16,4608]{2,1,0:T(8,128)S(1)}, u32[]{:S(2)}, u32[]{:S(2)}) collective-permute-start(f32[1,16,4608]{2,1,0:T(8,128)S(1)} %copy-done.2), channel_id=1, source_target_pairs={{32,0},{96,64},{160,128},{224,192},{33,1},{97,65},{161,129},{225,1... | collective-permute-start | bytes 884744 | tf_op jit(solution)/shard_map/ppermute | solution.py:213
  63.5 15.5 %collective-permute-start.10 = (bf16[96,1536]{1,0:T(8,128)(2,1)}, bf16[96,1536]{1,0:T(8,128)(2,1)}, u32[]{:S(2)}, u32[]{:S(2)}) collective-permute-start(bf16[96,1536]{1,0:T(8,128)(2,1)} %slice.19), channel_id=1, source_target_pairs={{0,28},{1,29},{2,30},{3,31},{4,0},{5,1},{6,2},{7,3},{8,4},{9,5},{1... | collective-permute-start | bytes 884744 | tf_op jit(solution)/shard_map/ppermute | solution.py:231
  67.0 12.1 %collective-permute-start.9 = (bf16[96,1536]{1,0:T(8,128)(2,1)}, bf16[96,1536]{1,0:T(8,128)(2,1)}, u32[]{:S(2)}, u32[]{:S(2)}) collective-permute-start(bf16[96,1536]{1,0:T(8,128)(2,1)} %slice.18), channel_id=1, source_target_pairs={{0,4},{1,5},{2,6},{3,7},{4,8},{5,9},{6,10},{7,11},{8,12},{9,13},{1... | collective-permute-start | bytes 884744 | tf_op jit(solution)/shard_map/ppermute | solution.py:230
  67.0 10.4 %collective-permute-start.12 = (f32[1,2,128]{2,1,0:T(2,128)S(1)}, f32[1,2,128]{2,1,0:T(2,128)S(1)}, u32[]{:S(2)}, u32[]{:S(2)}) collective-permute-start(f32[1,2,128]{2,1,0:T(2,128)S(1)} %copy-done.5), channel_id=1, source_target_pairs={{32,0},{96,64},{160,128},{224,192},{33,1},{97,65},{161,129},{225,1... | collective-permute-start | bytes 3080 | tf_op jit(solution)/shard_map/ppermute | solution.py:213
  76.9 8.2 %collective-permute-start.4 = (bf16[256,768]{1,0:T(8,128)(2,1)S(1)}, bf16[256,768]{1,0:T(8,128)(2,1)S(1)}, u32[]{:S(2)}, u32[]{:S(2)}) collective-permute-start(bf16[256,768]{1,0:T(8,128)(2,1)S(1)} %bitcast.22), channel_id=1, source_target_pairs={{0,1},{1,0},{2,3},{3,2},{4,5},{5,4},{6,7},{7,6},{8,9},{9,8},{10,11... | collective-permute-start | bytes 1179656 | tf_op jit(solution)/shard_map/ppermute | solution.py:188
  83.6 211.5 %collective-permute-start.36 = (bf16[1536,3072]{1,0:T(8,128)(2,1)S(1)}, bf16[1536,3072]{1,0:T(8,128)(2,1)S(1)}, u32[]{:S(2)}, u32[]{:S(2)}) collective-permute-start(bf16[1536,3072]{1,0:T(8,128)(2,1)S(1)} %get-tuple-element.35.weight_ref), channel_id=1, source_target_pairs={{32,0},{96,64},{160,128},{224,192},{33,1},{97,65},{161,129},{225,1... | collective-permute-start | bytes 28311560 | tf_op jit(solution)/shard_map/ppermute | solution.py:213
  89.2 4.7 %collective-permute-start.13 = (bf16[256,768]{1,0:T(8,128)(2,1)S(1)}, bf16[256,768]{1,0:T(8,128)(2,1)S(1)}, u32[]{:S(2)}, u32[]{:S(2)}) collective-permute-start(bf16[256,768]{1,0:T(8,128)(2,1)S(1)} %front.16.own_ref), channel_id=1, source_target_pairs={{0,1},{1,0},{2,3},{3,2},{4,5},{5,4},{6,7},{7,6},{8,9},{9,8},{10,11... | collective-permute-start | bytes 1179656 | tf_op jit(solution)/shard_map/ppermute | solution.py:188
  94.7 13.0 %collective-permute-start.14 = (bf16[256,768]{1,0:T(8,128)(2,1)S(1)}, bf16[256,768]{1,0:T(8,128)(2,1)S(1)}, u32[]{:S(2)}, u32[]{:S(2)}) collective-permute-start(bf16[256,768]{1,0:T(8,128)(2,1)S(1)} %back.16), channel_id=1, source_target_pairs={{0,32},{1,33},{2,34},{3,35},{4,36},{5,37},{6,38},{7,39},{8,40},{9,... | collective-permute-start | bytes 1179656 | tf_op jit(solution)/shard_map/ppermute | solution.py:307
  107.7 2.6 collective-permute-start.15
  114.4 1.8 collective-permute-start.16
  117.0 0.7 collective-permute-start.17
  117.7 2.2 collective-permute-start.18
  124.1 1.8 collective-permute-start.19
  126.7 0.7 collective-permute-start.20
  127.4 1.8 collective-permute-start.21
  133.3 1.8 collective-permute-start.22
  135.9 0.7 collective-permute-start.23
  136.7 2.0 collective-permute-start.24
  142.8 1.8 collective-permute-start.25
  145.4 0.7 collective-permute-start.26
  146.1 1.8 collective-permute-start.27
  152.1 1.8 collective-permute-start.28
  154.7 0.7 collective-permute-start.29
  155.4 2.0 collective-permute-start.30
  161.5 1.8 collective-permute-start.31
  164.1 0.7 collective-permute-start.32
  164.9 1.8 collective-permute-start.33
  170.8 124.2 %copy-start.4 = (f32[16]{0:T(128)S(1)}, f32[16]{0:T(128)}, u32[]{:S(2)}) copy-start(f32[16]{0:T(128)} %size_ref.3) | copy-start | bytes 196
  170.8 1.8 collective-permute-start.34
  173.4 80.8 %collective-permute-start.35 = (bf16[256,768]{1,0:T(8,128)(2,1)S(1)}, bf16[256,768]{1,0:T(8,128)(2,1)S(1)}, u32[]{:S(2)}, u32[]{:S(2)}) collective-permute-start(bf16[256,768]{1,0:T(8,128)(2,1)S(1)} %back.23), channel_id=1, source_target_pairs={{224,0},{225,1},{226,2},{227,3},{228,4},{229,5},{230,6},{231,7},{2... | collective-permute-start | bytes 1179656 | tf_op jit(solution)/shard_map/ppermute | solution.py:307
  295.0 79.7 %copy-start = (bf16[1536,3072]{1,0:T(8,128)(2,1)}, bf16[1536,3072]{1,0:T(8,128)(2,1)S(1)}, u32[]{:S(2)}) copy-start(bf16[1536,3072]{1,0:T(8,128)(2,1)S(1)} %collective-permute-done.36.weight_ref) | copy-start | bytes 28311556
  295.7 6.0 %collective-permute-start.37 = (bf16[256,768]{1,0:T(8,128)(2,1)S(1)}, bf16[256,768]{1,0:T(8,128)(2,1)S(1)}, u32[]{:S(2)}, u32[]{:S(2)}) collective-permute-start(bf16[256,768]{1,0:T(8,128)(2,1)S(1)} %advance_slot.1.own_ref.hidden_ref), channel_id=1, source_target_pairs={{0,1},{1,0},{2,3},{3,2},{4,5},{5,4},{6,7},{7,6},{8,9},{9,8},{10,11... | collective-permute-start | bytes 1179656 | tf_op jit(solution)/shard_map/ppermute | solution.py:188
  305.9 1.8 collective-permute-start.38
  308.5 1.8 collective-permute-start.39
  314.5 1.8 collective-permute-start.40
  317.1 10.3 %collective-permute-start.41 = (bf16[256,768]{1,0:T(8,128)(2,1)S(1)}, bf16[256,768]{1,0:T(8,128)(2,1)S(1)}, u32[]{:S(2)}, u32[]{:S(2)}) collective-permute-start(bf16[256,768]{1,0:T(8,128)(2,1)S(1)} %back.25), channel_id=1, source_target_pairs={{0,64},{1,65},{2,66},{3,67},{4,68},{5,69},{6,70},{7,71},{8,72},{9,... | collective-permute-start | bytes 1179656 | tf_op jit(solution)/shard_map/ppermute | solution.py:307
  327.4 2.7 collective-permute-start.42
  334.2 1.8 collective-permute-start.43
  336.8 1.8 collective-permute-start.44
  342.8 1.8 collective-permute-start.45
  345.4 0.7 collective-permute-start.46
  346.1 2.0 collective-permute-start.47
  352.2 1.8 collective-permute-start.48
  354.9 1.8 collective-permute-start.49
  360.8 1.8 collective-permute-start.50
  363.4 0.7 collective-permute-start.51
  364.1 2.1 collective-permute-start.52
  370.3 1.8 collective-permute-start.53
  372.9 1.8 collective-permute-start.54
  378.9 1.8 collective-permute-start.55
  (5 other events, 63.1 us)

commit v5 on v4

--- a/solution.py
+++ b/solution.py
@@ -13,7 +13,7 @@
 def layer_front(head_dim):
     score_scale = 1.0 / math.sqrt(head_dim)
 
-    def body(own_ref, other_ref, mod_ref, gain_ref, weight_ref, out_ref):
+    def body(own_ref, other_ref, mod_ref, gain_ref, sides_ref, kv_ref, out_ref):
         half = own_ref.shape[1]
         width = 2 * half
         own = own_ref[...].astype(jnp.float32)
@@ -37,7 +37,7 @@
         own = modulated(own, 0)
         other = modulated(other, 1)
 
-        def project(start, size):
+        def project(weight_ref, start, size):
             cols = slice(start, start + size)
             return jnp.dot(
                 own, weight_ref[:half, cols], preferred_element_type=jnp.float32
@@ -51,9 +51,9 @@
         gain_key = gain_ref[1:2, :]
         group = 2 * head_dim
         for start in range(0, half, group):
-            queries = project(start, group)
-            keys = project(half + start, group)
-            values = project(2 * half + start, group).astype(jnp.bfloat16)
+            queries = project(sides_ref, start, group)
+            keys = project(kv_ref, start, group)
+            values = project(kv_ref, half + start, group).astype(jnp.bfloat16)
             for at in range(0, group, head_dim):
                 query_head = rms(queries[:, at : at + head_dim], gain_query)
                 key_head = rms(keys[:, at : at + head_dim], gain_key)
@@ -82,7 +82,7 @@
 
 def layer_back(own_ref, other_ref, hidden_ref, mod_ref, weight_ref, out_ref):
     half = own_ref.shape[1]
-    cols = slice(3 * half, 4 * half)
+    cols = slice(half, 2 * half)
     projected = jnp.dot(
         own_ref[...], weight_ref[:half, cols], preferred_element_type=jnp.float32
     ) + jnp.dot(other_ref[...], weight_ref[half:, cols], preferred_element_type=jnp.float32)
@@ -97,12 +97,12 @@
         time_ref, mod_ref, gain_ref, next_mod_ref, next_gain_ref, query_ref, out_ref = refs[
             len(spots) : len(spots) + 7
         ]
-        held_ref, gain_held, next_gain_held, next_mods_held = refs[
-            len(spots) + 7 : len(spots) + 11
+        sides_held, kv_held, gain_held, next_gain_held, next_mods_held = refs[
+            len(spots) + 7 : len(spots) + 12
         ]
-        mods_held, sems = refs[len(spots) + 11 : -1], refs[-1]
+        mods_held, sems = refs[len(spots) + 12 : -1], refs[-1]
         core = word_ref[0]
-        width = held_ref.shape[0]
+        width = kv_held.shape[0]
         half = width // 2
         block = part_refs[0].shape[0]
         ring = width // block
@@ -114,16 +114,14 @@
         for (turn, start), part_ref in zip(spots, part_refs):
             rows = part_ref.shape[0]
             at = lax.rem(word_ref[2] + turn + core * (ring // 2), ring) * block + start
-            copied(
-                part_ref, held_ref.at[pl.ds(pl.multiple_of(at, rows), rows), pl.ds(half, width)]
-            )
+            copied(part_ref, kv_held.at[pl.ds(pl.multiple_of(at, rows), rows), :])
         cols = pl.ds(pl.multiple_of(core * half, half), half)
-        for source, left in ((query_ref, 0), (out_ref, half + width)):
+        for source, left in ((query_ref, 0), (out_ref, half)):
             for side in range(2):
                 first = pl.multiple_of(lax.rem(core + side, 2) * half, half)
                 copied(
                     source.at[0, pl.ds(first, half), cols],
-                    held_ref.at[pl.ds(side * half, half), pl.ds(left, half)],
+                    sides_held.at[pl.ds(side * half, half), pl.ds(left, half)],
                 )
         for copy in copies:
             copy.start()
@@ -182,7 +180,7 @@
     half = width // 2
     head_dim = qk_gain.shape[2]
     core_pairs = [(at, at ^ 1) for at in range(n_seq)]
-    quads = [[4 * at + j for j in range(4)] for at in range(n_seq // 4)]
+    octets = [[8 * at + j for j in range(8)] for at in range(n_seq // 8)]
 
     def swapped(value):
         return lax.ppermute(value, "seq", core_pairs)
@@ -247,7 +245,7 @@
     smem = pl.BlockSpec(memory_space=pltpu.SMEM)
     vmem = pl.BlockSpec(memory_space=pltpu.VMEM)
     hbm = pl.BlockSpec(memory_space=pltpu.HBM)
-    held_shape = jax.ShapeDtypeStruct((width, 2 * width), jnp.bfloat16)
+    held_shape = jax.ShapeDtypeStruct((width, width), jnp.bfloat16)
     small_shapes = [jax.ShapeDtypeStruct(qk_gain.shape[1:], jnp.float32)] * 2 + [
         jax.ShapeDtypeStruct((6, half), jnp.float32)
     ] * (1 + step_count)
@@ -257,9 +255,9 @@
 
     loaded = pl.pallas_call(
         load_own(spots),
-        out_shape=[held_shape] + small_shapes,
+        out_shape=[held_shape] * 2 + small_shapes,
         in_specs=[smem] + [hbm] * len(parts) + [smem] + [vmem] * 4 + [hbm, hbm],
-        out_specs=[vmem] * (4 + step_count),
+        out_specs=[vmem] * (5 + step_count),
         scratch_shapes=[pltpu.SemaphoreType.DMA((len(parts) + 4,))],
         compiler_params=pltpu.CompilerParams(vmem_limit_bytes=12 << 20),
         name="load_own",
@@ -274,18 +272,18 @@
         in_hbm(w_query),
         in_hbm(w_out),
     )
-    held, gains, next_gains, next_mods = loaded[:4]
-    mods = loaded[4:]
-
-    def layer(hidden, mods, gains, weights):
+    sides, kv, gains, next_gains, next_mods = loaded[:5]
+    mods = loaded[5:]
+
+    def layer(hidden, mods, gains, sides, kv):
         attended = pl.pallas_call(
             layer_front(head_dim),
             out_shape=jax.ShapeDtypeStruct((tokens, half), jnp.bfloat16),
-            in_specs=[vmem] * 5,
+            in_specs=[vmem] * 6,
             out_specs=vmem,
             compiler_params=pltpu.CompilerParams(vmem_limit_bytes=16 << 20),
             name="front",
-        )(hidden, swapped(hidden), mods, gains, weights)
+        )(hidden, swapped(hidden), mods, gains, sides, kv)
         return pl.pallas_call(
             layer_back,
             out_shape=jax.ShapeDtypeStruct((tokens, half), jnp.bfloat16),
@@ -293,9 +291,19 @@
             out_specs=vmem,
             compiler_params=pltpu.CompilerParams(vmem_limit_bytes=12 << 20),
             name="back",
-        )(attended, swapped(attended), hidden, mods, weights)
-
-    following = [next_mods, next_gains, to_even(held)]
+        )(attended, swapped(attended), hidden, mods, sides)
+
+    evens = [at for at in range(n_seq) if at // 4 % 2 == 0]
+
+    def pairs_from(shift):
+        return [
+            ((place + 1) * n_seq + at + shift, place * n_seq + at)
+            for place in range(0, n_pipe, 2)
+            for at in evens
+        ]
+
+    next_sides = lax.ppermute(sides, ("pipe", "seq"), pairs_from(0))
+    next_kv = lax.ppermute(kv, ("pipe", "seq"), pairs_from(4))
 
     holder = 0
     hidden = slot
@@ -307,7 +315,6 @@
                 hidden = lax.ppermute(hidden, "pipe", [(holder, place)])
                 holder = place
             if step > 0 and section == 0:
-                hidden, following[2] = lax.optimization_barrier((hidden, following[2]))
                 slot = pl.pallas_call(
                     advance_slot(step - 1),
                     out_shape=jax.ShapeDtypeStruct((tokens, half), jnp.bfloat16),
@@ -317,12 +324,20 @@
                     name="advance_slot",
                 )(words, timesteps, step_sizes, slot, hidden)
                 hidden = slot
-            hidden = layer(hidden, *(following if section != place else (mods[step], gains, held)))
+            if section == place:
+                weights = (mods[step], gains, sides, kv)
+            else:
+                weights = (next_mods, next_gains, next_sides, next_kv)
+            hidden = layer(hidden, *weights)
+            if step == 0 and section == n_pipe - 1:
+                hidden, next_sides, next_kv = lax.optimization_barrier(
+                    (hidden, next_sides, next_kv)
+                )
 
     kept = jnp.where(pipe_at == 0, slot, hidden)
-    kept = lax.dynamic_slice_in_dim(kept, (seq_at // 4) * 4 * row_share, 4 * row_share, 0)
-    kept = kept.reshape(4, row_share, half)
-    kept = lax.all_to_all(kept, "seq", 0, 0, tiled=True, axis_index_groups=quads)
+    kept = lax.dynamic_slice_in_dim(kept, (seq_at // 8) * 8 * row_share, 8 * row_share, 0)
+    kept = kept.reshape(8, row_share, half)
+    kept = lax.all_to_all(kept, "seq", 0, 0, tiled=True, axis_index_groups=octets)[:4]
     kept = kept.reshape(micro_count, 2, row_share, n_pipe // 2, feature_share)
     sent = jnp.transpose(kept, (1, 3, 0, 2, 4)).reshape(
         n_pipe, micro_count, row_share, feature_share

time: 436 us -> 502 us (1.15)
  waiting for transfers between devices: 219 us -> 292 us
  starting transfers between devices: 73.1 us -> 67.4 us
    ppermute x0 -> x2, waiting for transfers between devices: none -> 175 us  [the longest x1 102 us: shards(): next_sides = lax.ppermute(sides, ('pipe', 'seq'), pairs_from(0))]
    ppermute x11, waiting for transfers between devices: 95.7 us -> 29.1 us  [shards(): hidden = lax.ppermute(hidden, 'pipe', [(holder, place)])]
    ppermute x3 -> x2, waiting for transfers between devices: 40.8 us -> 3.11 us  [to_even(): return lax.ppermute(value, 'pipe', backward)]
    all_to_all x1, waiting for transfers between devices: 8.58 us -> 13.7 us  [shards(): slot = lax.all_to_all(sent, 'seq', 0, 0, tiled=True).reshape(tokens, half)]
  transfers between devices with their start and end apart: 58 -> 59, of which waited for: 43 -> 46; matrix products, arithmetic and copies ran while one was open for 1% -> 1% of each run, Pallas kernels for 10% -> 5%
where the time goes in v5:
time: 502 us; the launch traced here: 495 us
  waiting for transfers between devices  292 us (58%)
  Pallas kernels  85.6 us (17%)
  starting transfers between devices  67.4 us (13%)
  blocking collectives  40.8 us (8%)
  local copies, waits for them, and re-layouts  7.4 us (1%)
    ppermute x1, waiting for transfers between devices, shards(): next_sides = lax.ppermute(sides, ('pipe', 'seq'), pairs_from(0))  102 us
    ppermute x1, waiting for transfers between devices, shards(): next_kv = lax.ppermute(kv, ('pipe', 'seq'), pairs_from(4))  73.7 us
    pallas_call x16, Pallas kernels, layer(): pl.pallas_call(layer_front(head_dim), out_shape=jax.ShapeDtypeStruct((tok...  66.8 us
    ppermute x33, waiting for transfers between devices, swapped(): return lax.ppermute(value, 'seq', core_pairs)  42.9 us
    all_to_all x1, blocking collectives, shards(): got = lax.all_to_all(sent, 'pipe', 0, 0, tiled=True)  30.8 us
    ppermute x11, waiting for transfers between devices, shards(): hidden = lax.ppermute(hidden, 'pipe', [(holder, place)])  29.1 us
    ppermute x33, starting transfers between devices, swapped(): return lax.ppermute(value, 'seq', core_pairs)  25.5 us
    ppermute x3, waiting for transfers between devices, shards(): falling = lax.ppermute(falling, 'seq', rings[1])  17.6 us
  transfers between devices with their start and end apart: 59, of which 46 were waited for; matrix products, arithmetic and copies ran while one was open for 1% of the time, Pallas kernels for 5%

profile of v5, /device:TPU:1, one launch (start us, length us, event | category | flops | bytes accessed | tf_op | source)
XLA Modules:
  0.0 494.6 jit_solution(9100550667674068451)
XLA Ops:
  1.1 3.3 collective-permute-start
  8.2 4.1 all-to-all-start
  12.3 3.1 collective-permute-done.1
  15.5 2.0 all-to-all-done
  17.4 5.6 %collective-permute-start.3 = (bf16[192,1536]{1,0:T(8,128)(2,1)S(1)}, bf16[192,1536]{1,0:T(8,128)(2,1)S(1)}, u32[]{:S(2)}, u32[]{:S(2)}) collective-permute-start(bf16[192,1536]{1,0:T(8,128)(2,1)S(1)} %pad_maximum_fusion.refs_0_), channel_id=1, source_target_pairs={{0,28},{1,29},{2,30},{3,31},{4,0},{5,1},{6,2},{7,3},{8,4},{9,5},{1... | collective-permute-start | bytes 1769480 | tf_op jit(solution)/shard_map/ppermute | solution.py:222
  23.0 10.6 %collective-permute-done.3.refs_2_ = bf16[192,1536]{1,0:T(8,128)(2,1)S(1)} collective-permute-done((bf16[192,1536]{1,0:T(8,128)(2,1)S(1)}, bf16[192,1536]{1,0:T(8,128)(2,1)S(1)}, u32[]{:S(2)}, u32[]{:S(2)}) %collective-permute-start.3) | collective-permute-done | bytes 589856 | tf_op jit(solution)/shard_map/ppermute | solution.py:222
  33.6 3.1 collective-permute-done.2.refs_1_
  39.1 8.1 %all-to-all-start.1 = ((bf16[32,8,768]{2,1,0:T(8,128)(2,1)}), bf16[32,8,768]{2,1,0:T(8,128)(2,1)S(1)}, u32[]{:S(2)}, u32[]{:S(2)}) async-start(bf16[32,8,768]{2,1,0:T(8,128)(2,1)} %bitcast.10), calls=%async_computation.1 | async-start | bytes 786432 | tf_op jit(solution)/shard_map/all_to_all | solution.py:238
  48.4 1.8 collective-permute-start.8
  50.3 13.7 %all-to-all-done.1 = bf16[32,8,768]{2,1,0:T(8,128)(2,1)S(1)} async-done(((bf16[32,8,768]{2,1,0:T(8,128)(2,1)}), bf16[32,8,768]{2,1,0:T(8,128)(2,1)S(1)}, u32[]{:S(2)}, u32[]{:S(2)}) %all-to-all-start.1) | async-done | bytes 393248 | tf_op jit(solution)/shard_map/all_to_all | solution.py:238
  65.2 5.9 %collective-permute-done.8.refs_6_ = bf16[192,1536]{1,0:T(8,128)(2,1)S(1)} collective-permute-done((bf16[192,1536]{1,0:T(8,128)(2,1)}, bf16[192,1536]{1,0:T(8,128)(2,1)S(1)}, u32[]{:S(2)}, u32[]{:S(2)}) %collective-permute-start.8) | collective-permute-done | bytes 589856 | tf_op jit(solution)/shard_map/ppermute | solution.py:222
  74.2 1.5 collective-permute-start.12
  75.7 3.1 collective-permute-done.12.refs_13_
  78.9 2.2 collective-permute-done.9.refs_7_
  81.1 4.4 load_own.1
  85.5 4.2 front.16.own_ref
  89.7 4.2 collective-permute-start.13
  96.1 2.4 collective-permute-start.14
  98.5 8.1 %collective-permute-done.14.own_ref.hidden_ref = bf16[256,768]{1,0:T(8,128)(2,1)S(1)} collective-permute-done((bf16[256,768]{1,0:T(8,128)(2,1)S(1)}, bf16[256,768]{1,0:T(8,128)(2,1)S(1)}, u32[]{:S(2)}, u32[]{:S(2)}) %collective-permute-start.14) | collective-permute-done | bytes 393248 | tf_op jit(solution)/shard_map/ppermute | solution.py:315
  109.1 4.2 front.17.own_ref
  113.8 1.4 collective-permute-done.16.other_ref
  117.5 1.4 collective-permute-done.18.other_ref
  118.8 4.2 front.18.own_ref
  123.5 1.3 collective-permute-done.19.other_ref
  128.1 4.2 front.19.own_ref
  140.2 4.2 front.20.own_ref
  149.5 4.2 front.21.own_ref
  159.0 4.2 front.22.own_ref
  163.6 1.4 collective-permute-done.31.other_ref
  166.9 1.4 collective-permute-done.33.other_ref
  168.3 4.2 front.23.own_ref
  172.9 1.4 collective-permute-done.34.other_ref
  175.1 73.7 %collective-permute-done.36.kv_ref = bf16[1536,1536]{1,0:T(8,128)(2,1)S(1)} collective-permute-done((bf16[1536,1536]{1,0:T(8,128)(2,1)S(1)}, bf16[1536,1536]{1,0:T(8,128)(2,1)S(1)}, u32[]{:S(2)}, u32[]{:S(2)}) %collective-permute-start.36) | collective-permute-done | bytes 4718624 | tf_op jit(solution)/shard_map/ppermute | solution.py:306
  248.8 101.5 %collective-permute-done.35.sides_ref.weight_ref = bf16[1536,1536]{1,0:T(8,128)(2,1)S(1)} collective-permute-done((bf16[1536,1536]{1,0:T(8,128)(2,1)S(1)}, bf16[1536,1536]{1,0:T(8,128)(2,1)S(1)}, u32[]{:S(2)}, u32[]{:S(2)}) %collective-permute-start.35) | collective-permute-done | bytes 4718624 | tf_op jit(solution)/shard_map/ppermute | solution.py:305
  351.6 12.9 %collective-permute-done.37.hidden_ref = bf16[256,768]{1,0:T(8,128)(2,1)S(1)} collective-permute-done((bf16[256,768]{1,0:T(8,128)(2,1)S(1)}, bf16[256,768]{1,0:T(8,128)(2,1)S(1)}, u32[]{:S(2)}, u32[]{:S(2)}) %collective-permute-start.37) | collective-permute-done | bytes 393248 | tf_op jit(solution)/shard_map/ppermute | solution.py:315
  365.2 1.8 collective-permute-start.38
  368.4 4.2 front.24.own_ref
  373.0 1.4 collective-permute-done.39.other_ref
  375.6 1.4 collective-permute-done.40.other_ref
  377.0 4.2 front.25.own_ref
  381.6 1.4 collective-permute-done.41.other_ref
  383.8 3.5 collective-permute-start.42
  387.3 8.1 %collective-permute-done.42.own_ref.hidden_ref = bf16[256,768]{1,0:T(8,128)(2,1)S(1)} collective-permute-done((bf16[256,768]{1,0:T(8,128)(2,1)S(1)}, bf16[256,768]{1,0:T(8,128)(2,1)S(1)}, u32[]{:S(2)}, u32[]{:S(2)}) %collective-permute-start.42) | collective-permute-done | bytes 393248 | tf_op jit(solution)/shard_map/ppermute | solution.py:315
  395.3 1.4 collective-permute-start.43
  398.0 4.2 front.26.own_ref
  402.7 1.4 collective-permute-done.44.other_ref
  405.3 1.4 collective-permute-done.45.other_ref
  406.7 4.2 front.27.own_ref
  411.3 1.4 collective-permute-done.46.other_ref
  414.8 1.4 collective-permute-done.48.other_ref
  416.2 4.2 front.28.own_ref
  420.8 1.4 collective-permute-done.49.other_ref
  423.4 1.4 collective-permute-done.50.other_ref
  424.8 4.2 front.29.own_ref
  429.4 1.4 collective-permute-done.51.other_ref
  432.9 1.4 collective-permute-done.53.other_ref
  434.3 4.2 front.30.own_ref
  438.9 1.4 collective-permute-done.54.other_ref
  441.5 1.4 collective-permute-done.55.other_ref
  442.9 4.2 front.31.own_ref
  447.5 1.4 collective-permute-done.56.other_ref
  448.9 2.3 copy-done.1
  452.1 10.0 %all_to_all.20 = bf16[8,8,768]{2,1,0:T(8,128)(2,1)S(1)} all-to-all(bf16[8,8,768]{2,1,0:T(8,128)(2,1)S(1)} %fusion), channel_id=1, replica_groups={{0,1,2,3,4,5,6,7},{8,9,10,11,12,13,14,15},{16,17,18,19,20,21,22,23},{24..., dimensions={0} | all-to-all | bytes 196608 | tf_op jit(solution)/shard_map/all_to_all | solution.py:340
  462.2 30.8 %all_to_all.21.got_ref = bf16[8,2,8,192]{3,2,1,0:T(8,128)(2,1)S(1)} all-to-all(bf16[8,2,8,192]{3,2,1,0:T(8,128)(2,1)S(1)} %bitcast.28), channel_id=1, replica_groups=mesh['pipe'=8,'seq'=32] {'pipe'}, dimensions={0} | all-to-all | bytes 98304 | tf_op jit(solution)/shard_map/all_to_all | solution.py:345
  (132 shorter events, 66.4 us)
Async XLA Ops:
  0.0 74.2 %copy-start.5 = (f32[1,2,128]{2,1,0:T(2,128)S(1)}, f32[1,2,128]{2,1,0:T(2,128)}, u32[]{:S(2)}) copy-start(f32[1,2,128]{2,1,0:T(2,128)} %refs_11_.1) | copy-start | bytes 3076
  0.0 81.1 %copy-start.3 = (s32[2,2]{1,0:T(2,128)S(1)}, s32[2,2]{1,0:T(2,128)}, u32[]{:S(2)}) copy-start(s32[2,2]{1,0:T(2,128)} %time_ref.3) | copy-start | bytes 52
  1.1 4.3 collective-permute-start
  5.5 9.8 %collective-permute-start.1 = (bf16[96,1536]{1,0:T(8,128)(2,1)S(1)}, bf16[96,1536]{1,0:T(8,128)(2,1)S(1)}, u32[]{:S(2)}, u32[]{:S(2)}) collective-permute-start(bf16[96,1536]{1,0:T(8,128)(2,1)S(1)} %pad_maximum_fusion.1), channel_id=1, source_target_pairs={{0,2},{1,3},{2,0},{3,1},{4,6},{5,7},{6,4},{7,5},{8,10},{9,11},{10,... | collective-permute-start | bytes 884744 | tf_op jit(solution)/shard_map/ppermute | solution.py:201
  8.2 9.3 %all-to-all-start = ((bf16[8,2,8,192]{3,2,1,0:T(8,128)(2,1)}), bf16[8,2,8,192]{3,2,1,0:T(8,128)(2,1)S(1)}, u32[]{:S(2)}, u32[]{:S(2)}) async-start(bf16[8,2,8,192]{3,2,1,0:T(8,128)(2,1)} %broadcast_in_dim.6), calls=%async_computation | async-start | bytes 131072 | tf_op jit(solution)/shard_map/all_to_all | solution.py:204
  15.5 65.6 %copy-start.6 = (bf16[192,1536]{1,0:T(8,128)(2,1)}, bf16[192,1536]{1,0:T(8,128)(2,1)S(1)}, u32[]{:S(2)}) copy-start(bf16[192,1536]{1,0:T(8,128)(2,1)S(1)} %pad_maximum_fusion.refs_0_) | copy-start | bytes 1769476
  17.4 16.2 %collective-permute-start.3 = (bf16[192,1536]{1,0:T(8,128)(2,1)S(1)}, bf16[192,1536]{1,0:T(8,128)(2,1)S(1)}, u32[]{:S(2)}, u32[]{:S(2)}) collective-permute-start(bf16[192,1536]{1,0:T(8,128)(2,1)S(1)} %pad_maximum_fusion.refs_0_), channel_id=1, source_target_pairs={{0,28},{1,29},{2,30},{3,31},{4,0},{5,1},{6,2},{7,3},{8,4},{9,5},{1... | collective-permute-start | bytes 1769480 | tf_op jit(solution)/shard_map/ppermute | solution.py:222
  23.0 13.7 %collective-permute-start.2 = (bf16[192,1536]{1,0:T(8,128)(2,1)S(1)}, bf16[192,1536]{1,0:T(8,128)(2,1)S(1)}, u32[]{:S(2)}, u32[]{:S(2)}) collective-permute-start(bf16[192,1536]{1,0:T(8,128)(2,1)S(1)} %pad_maximum_fusion.refs_0_), channel_id=1, source_target_pairs={{0,4},{1,5},{2,6},{3,7},{4,8},{5,9},{6,10},{7,11},{8,12},{9,13},{1... | collective-permute-start | bytes 1769480 | tf_op jit(solution)/shard_map/ppermute | solution.py:221
  36.7 11.7 %collective-permute-start.6 = (bf16[192,1536]{1,0:T(8,128)(2,1)S(1)}, bf16[192,1536]{1,0:T(8,128)(2,1)}, u32[]{:S(2)}, u32[]{:S(2)}) collective-permute-start(bf16[192,1536]{1,0:T(8,128)(2,1)S(1)} %collective-permute-done.3.refs_2_), channel_id=1, source_target_pairs={{0,28},{1,29},{2,30},{3,31},{4,0},{5,1},{6,2},{7,3},{8,4},{9,5},{1... | collective-permute-start | bytes 1769480 | tf_op jit(solution)/shard_map/ppermute | solution.py:222
  37.1 13.2 %collective-permute-start.5 = (bf16[192,1536]{1,0:T(8,128)(2,1)S(1)}, bf16[192,1536]{1,0:T(8,128)(2,1)}, u32[]{:S(2)}, u32[]{:S(2)}) collective-permute-start(bf16[192,1536]{1,0:T(8,128)(2,1)S(1)} %collective-permute-done.2.refs_1_), channel_id=1, source_target_pairs={{0,4},{1,5},{2,6},{3,7},{4,8},{5,9},{6,10},{7,11},{8,12},{9,13},{1... | collective-permute-start | bytes 1769480 | tf_op jit(solution)/shard_map/ppermute | solution.py:221
  39.1 24.8 %all-to-all-start.1 = ((bf16[32,8,768]{2,1,0:T(8,128)(2,1)}), bf16[32,8,768]{2,1,0:T(8,128)(2,1)S(1)}, u32[]{:S(2)}, u32[]{:S(2)}) async-start(bf16[32,8,768]{2,1,0:T(8,128)(2,1)} %bitcast.10), calls=%async_computation.1 | async-start | bytes 786432 | tf_op jit(solution)/shard_map/all_to_all | solution.py:238
  48.4 22.7 %collective-permute-start.8 = (bf16[192,1536]{1,0:T(8,128)(2,1)}, bf16[192,1536]{1,0:T(8,128)(2,1)S(1)}, u32[]{:S(2)}, u32[]{:S(2)}) collective-permute-start(bf16[192,1536]{1,0:T(8,128)(2,1)} %collective-permute-done.6.refs_4_), channel_id=1, source_target_pairs={{0,28},{1,29},{2,30},{3,31},{4,0},{5,1},{6,2},{7,3},{8,4},{9,5},{1... | collective-permute-start | bytes 1769480 | tf_op jit(solution)/shard_map/ppermute | solution.py:222
  50.3 22.9 %collective-permute-start.7 = (bf16[192,1536]{1,0:T(8,128)(2,1)}, bf16[192,1536]{1,0:T(8,128)(2,1)S(1)}, u32[]{:S(2)}, u32[]{:S(2)}) collective-permute-start(bf16[192,1536]{1,0:T(8,128)(2,1)} %collective-permute-done.5.refs_3_), channel_id=1, source_target_pairs={{0,4},{1,5},{2,6},{3,7},{4,8},{5,9},{6,10},{7,11},{8,12},{9,13},{1... | collective-permute-start | bytes 1769480 | tf_op jit(solution)/shard_map/ppermute | solution.py:221
  63.9 21.6 %collective-permute-start.4 = (bf16[256,768]{1,0:T(8,128)(2,1)S(1)}, bf16[256,768]{1,0:T(8,128)(2,1)S(1)}, u32[]{:S(2)}, u32[]{:S(2)}) collective-permute-start(bf16[256,768]{1,0:T(8,128)(2,1)S(1)} %bitcast.22), channel_id=1, source_target_pairs={{0,1},{1,0},{2,3},{3,2},{4,5},{5,4},{6,7},{7,6},{8,9},{9,8},{10,11... | collective-permute-start | bytes 1179656 | tf_op jit(solution)/shard_map/ppermute | solution.py:186
  63.9 14.9 %collective-permute-start.11 = (f32[1,16,4608]{2,1,0:T(8,128)S(1)}, f32[1,16,4608]{2,1,0:T(8,128)S(1)}, u32[]{:S(2)}, u32[]{:S(2)}) collective-permute-start(f32[1,16,4608]{2,1,0:T(8,128)S(1)} %copy-done.2), channel_id=1, source_target_pairs={{32,0},{96,64},{160,128},{224,192},{33,1},{97,65},{161,129},{225,1... | collective-permute-start | bytes 884744 | tf_op jit(solution)/shard_map/ppermute | solution.py:211
  71.9 7.0 %collective-permute-start.10 = (bf16[96,1536]{1,0:T(8,128)(2,1)}, bf16[96,1536]{1,0:T(8,128)(2,1)}, u32[]{:S(2)}, u32[]{:S(2)}) collective-permute-start(bf16[96,1536]{1,0:T(8,128)(2,1)} %slice.23), channel_id=1, source_target_pairs={{0,28},{1,29},{2,30},{3,31},{4,0},{5,1},{6,2},{7,3},{8,4},{9,5},{1... | collective-permute-start | bytes 884744 | tf_op jit(solution)/shard_map/ppermute | solution.py:229
  74.0 7.1 %collective-permute-start.9 = (bf16[96,1536]{1,0:T(8,128)(2,1)}, bf16[96,1536]{1,0:T(8,128)(2,1)}, u32[]{:S(2)}, u32[]{:S(2)}) collective-permute-start(bf16[96,1536]{1,0:T(8,128)(2,1)} %slice.22), channel_id=1, source_target_pairs={{0,4},{1,5},{2,6},{3,7},{4,8},{5,9},{6,10},{7,11},{8,12},{9,13},{1... | collective-permute-start | bytes 884744 | tf_op jit(solution)/shard_map/ppermute | solution.py:228
  74.2 4.7 collective-permute-start.12
  89.7 5.6 %collective-permute-start.13 = (bf16[256,768]{1,0:T(8,128)(2,1)S(1)}, bf16[256,768]{1,0:T(8,128)(2,1)S(1)}, u32[]{:S(2)}, u32[]{:S(2)}) collective-permute-start(bf16[256,768]{1,0:T(8,128)(2,1)S(1)} %front.16.own_ref), channel_id=1, source_target_pairs={{0,1},{1,0},{2,3},{3,2},{4,5},{5,4},{6,7},{7,6},{8,9},{9,8},{10,11... | collective-permute-start | bytes 1179656 | tf_op jit(solution)/shard_map/ppermute | solution.py:186
  96.1 10.5 %collective-permute-start.14 = (bf16[256,768]{1,0:T(8,128)(2,1)S(1)}, bf16[256,768]{1,0:T(8,128)(2,1)S(1)}, u32[]{:S(2)}, u32[]{:S(2)}) collective-permute-start(bf16[256,768]{1,0:T(8,128)(2,1)S(1)} %back.16), channel_id=1, source_target_pairs={{0,32},{1,33},{2,34},{3,35},{4,36},{5,37},{6,38},{7,39},{8,40},{9,... | collective-permute-start | bytes 1179656 | tf_op jit(solution)/shard_map/ppermute | solution.py:315
  106.6 2.5 collective-permute-start.15
  113.3 1.8 collective-permute-start.16
  115.9 0.7 collective-permute-start.17
  116.6 2.2 collective-permute-start.18
  123.0 1.8 collective-permute-start.19
  125.6 0.7 collective-permute-start.20
  126.3 1.8 collective-permute-start.21
  132.3 1.8 collective-permute-start.22
  134.9 3.3 collective-permute-start.23
  135.6 113.2 %collective-permute-start.36 = (bf16[1536,1536]{1,0:T(8,128)(2,1)S(1)}, bf16[1536,1536]{1,0:T(8,128)(2,1)S(1)}, u32[]{:S(2)}, u32[]{:S(2)}) collective-permute-start(bf16[1536,1536]{1,0:T(8,128)(2,1)S(1)} %get-tuple-element.38.kv_ref), channel_id=1, source_target_pairs={{36,0},{37,1},{38,2},{39,3},{44,8},{45,9},{46,10},{47,11},{52,16},... | collective-permute-start | bytes 14155784 | tf_op jit(solution)/shard_map/ppermute | solution.py:306
  136.9 213.4 %collective-permute-start.35 = (bf16[1536,1536]{1,0:T(8,128)(2,1)S(1)}, bf16[1536,1536]{1,0:T(8,128)(2,1)S(1)}, u32[]{:S(2)}, u32[]{:S(2)}) collective-permute-start(bf16[1536,1536]{1,0:T(8,128)(2,1)S(1)} %get-tuple-element.37.sides_ref.weight_ref), channel_id=1, source_target_pairs={{32,0},{33,1},{34,2},{35,3},{40,8},{41,9},{42,10},{43,11},{48,16},... | collective-permute-start | bytes 14155784 | tf_op jit(solution)/shard_map/ppermute | solution.py:305
  138.2 2.0 collective-permute-start.24
  144.4 1.8 collective-permute-start.25
  147.0 0.7 collective-permute-start.26
  147.7 1.8 collective-permute-start.27
  153.6 1.8 collective-permute-start.28
  156.3 0.7 collective-permute-start.29
  157.0 2.0 collective-permute-start.30
  163.2 1.8 collective-permute-start.31
  165.8 0.7 collective-permute-start.32
  166.5 1.8 collective-permute-start.33
  172.4 192.1 %copy-start.4 = (f32[16]{0:T(128)S(1)}, f32[16]{0:T(128)}, u32[]{:S(2)}) copy-start(f32[16]{0:T(128)} %size_ref.3) | copy-start | bytes 196
  172.5 1.8 collective-permute-start.34
  350.3 92.6 %copy-start = (bf16[1536,1536]{1,0:T(8,128)(2,1)}, bf16[1536,1536]{1,0:T(8,128)(2,1)S(1)}, u32[]{:S(2)}) copy-start(bf16[1536,1536]{1,0:T(8,128)(2,1)S(1)} %collective-permute-done.35.sides_ref.weight_ref) | copy-start | bytes 14155780
  350.3 14.2 %collective-permute-start.37 = (bf16[256,768]{1,0:T(8,128)(2,1)S(1)}, bf16[256,768]{1,0:T(8,128)(2,1)S(1)}, u32[]{:S(2)}, u32[]{:S(2)}) collective-permute-start(bf16[256,768]{1,0:T(8,128)(2,1)S(1)} %back.23), channel_id=1, source_target_pairs={{224,0},{225,1},{226,2},{227,3},{228,4},{229,5},{230,6},{231,7},{2... | collective-permute-start | bytes 1179656 | tf_op jit(solution)/shard_map/ppermute | solution.py:315
  365.2 3.1 collective-permute-start.38
  372.6 1.8 collective-permute-start.39
  375.2 1.8 collective-permute-start.40
  381.2 1.8 collective-permute-start.41
  383.8 11.6 %collective-permute-start.42 = (bf16[256,768]{1,0:T(8,128)(2,1)S(1)}, bf16[256,768]{1,0:T(8,128)(2,1)S(1)}, u32[]{:S(2)}, u32[]{:S(2)}) collective-permute-start(bf16[256,768]{1,0:T(8,128)(2,1)S(1)} %back.25), channel_id=1, source_target_pairs={{0,64},{1,65},{2,66},{3,67},{4,68},{5,69},{6,70},{7,71},{8,72},{9,... | collective-permute-start | bytes 1179656 | tf_op jit(solution)/shard_map/ppermute | solution.py:315
  395.3 2.7 collective-permute-start.43
  402.2 1.8 collective-permute-start.44
  404.8 1.8 collective-permute-start.45
  410.8 1.8 collective-permute-start.46
  413.4 0.7 collective-permute-start.47
  414.1 2.0 collective-permute-start.48
  420.3 1.8 collective-permute-start.49
  422.9 1.8 collective-permute-start.50
  428.9 1.8 collective-permute-start.51
  431.5 0.7 collective-permute-start.52
  432.2 2.1 collective-permute-start.53
  438.5 1.8 collective-permute-start.54
  441.1 1.8 collective-permute-start.55
  447.1 1.8 collective-permute-start.56
  (6 other events, 111.4 us)

commit v6 on v4

--- a/solution.py
+++ b/solution.py
@@ -295,13 +295,15 @@
             name="back",
         )(attended, swapped(attended), hidden, mods, weights)
 
-    following = [next_mods, next_gains, to_even(held)]
+    apart = 2
+    held_pairs = [(at + 1, at) for at in range(apart, n_pipe, 2)]
+    following = [next_mods, next_gains, lax.ppermute(held, "pipe", held_pairs)]
 
     holder = 0
     hidden = slot
     for step in range(step_count):
         for section in range(n_pipe):
-            joined = step > 0
+            joined = step > 0 and section >= apart
             place = section - section % 2 if joined else section
             if place != holder:
                 hidden = lax.ppermute(hidden, "pipe", [(holder, place)])

time: 436 us -> 438 us (level)
  blocking collectives: 41.2 us -> 89.4 us
  waiting for transfers between devices: 219 us -> 178 us
  starting transfers between devices: 73.1 us -> 66.9 us
    all_to_all x1, blocking collectives: 30.8 us -> 81.6 us  [shards(): got = lax.all_to_all(sent, 'pipe', 0, 0, tiled=True)]
    ppermute x3 -> x2, waiting for transfers between devices: 40.8 us -> 0.01 us  [to_even(): return lax.ppermute(value, 'pipe', backward)]
    ppermute x11 -> x12, starting transfers between devices: 13.9 us -> 11.4 us  [shards(): hidden = lax.ppermute(hidden, 'pipe', [(holder, place)])]
    ppermute x11 -> x12, waiting for transfers between devices: 95.7 us -> 96 us  [shards(): hidden = lax.ppermute(hidden, 'pipe', [(holder, place)])]
  transfers between devices with their start and end apart: 58 -> 59, of which waited for: 43 -> 42; matrix products, arithmetic and copies ran while one was open for 1% -> 1% of each run, Pallas kernels for 10% -> 10%
where the time goes in v6:
time: 438 us; the launch traced here: 430 us
  waiting for transfers between devices  178 us (41%)
  blocking collectives  89.4 us (20%)
  Pallas kernels  85.2 us (19%)
  starting transfers between devices  66.9 us (15%)
  local copies, waits for them, and re-layouts  8.78 us (2%)
    ppermute x12, waiting for transfers between devices, shards(): hidden = lax.ppermute(hidden, 'pipe', [(holder, place)])  96 us
    all_to_all x1, blocking collectives, shards(): got = lax.all_to_all(sent, 'pipe', 0, 0, tiled=True)  81.6 us
    pallas_call x16, Pallas kernels, layer(): pl.pallas_call(layer_front(head_dim), out_shape=jax.ShapeDtypeStruct((tok...  66.2 us
    ppermute x33, waiting for transfers between devices, swapped(): return lax.ppermute(value, 'seq', core_pairs)  42.9 us
    ppermute x33, starting transfers between devices, swapped(): return lax.ppermute(value, 'seq', core_pairs)  24.4 us
    ppermute x3, waiting for transfers between devices, shards(): falling = lax.ppermute(falling, 'seq', rings[1])  20.8 us
    pallas_call x16, Pallas kernels, layer(): pl.pallas_call(layer_back, out_shape=jax.ShapeDtypeStruct((tokens, half),...  12.7 us
    ppermute x12, starting transfers between devices, shards(): hidden = lax.ppermute(hidden, 'pipe', [(holder, place)])  11.4 us
  transfers between devices with their start and end apart: 59, of which 42 were waited for; matrix products, arithmetic and copies ran while one was open for 1% of the time, Pallas kernels for 10%

profile of v6, /device:TPU:1, one launch (start us, length us, event | category | flops | bytes accessed | tf_op | source)
XLA Modules:
  0.0 429.7 jit_solution(4651612045457581706)
XLA Ops:
  1.1 3.3 collective-permute-start
  8.2 4.1 all-to-all-start
  12.3 3.1 collective-permute-done.1
  15.5 2.0 all-to-all-done
  17.4 5.6 %collective-permute-start.3 = (bf16[192,1536]{1,0:T(8,128)(2,1)S(1)}, bf16[192,1536]{1,0:T(8,128)(2,1)S(1)}, u32[]{:S(2)}, u32[]{:S(2)}) collective-permute-start(bf16[192,1536]{1,0:T(8,128)(2,1)S(1)} %pad_maximum_fusion.refs_0_), channel_id=1, source_target_pairs={{0,28},{1,29},{2,30},{3,31},{4,0},{5,1},{6,2},{7,3},{8,4},{9,5},{1... | collective-permute-start | bytes 1769480 | tf_op jit(solution)/shard_map/ppermute | solution.py:224
  23.0 10.6 %collective-permute-done.3.refs_2_ = bf16[192,1536]{1,0:T(8,128)(2,1)S(1)} collective-permute-done((bf16[192,1536]{1,0:T(8,128)(2,1)S(1)}, bf16[192,1536]{1,0:T(8,128)(2,1)S(1)}, u32[]{:S(2)}, u32[]{:S(2)}) %collective-permute-start.3) | collective-permute-done | bytes 589856 | tf_op jit(solution)/shard_map/ppermute | solution.py:224
  33.6 3.1 collective-permute-done.2.refs_1_
  38.2 10.2 %collective-permute-done.6.refs_4_ = bf16[192,1536]{1,0:T(8,128)(2,1)} collective-permute-done((bf16[192,1536]{1,0:T(8,128)(2,1)S(1)}, bf16[192,1536]{1,0:T(8,128)(2,1)}, u32[]{:S(2)}, u32[]{:S(2)}) %collective-permute-start.6) | collective-permute-done | bytes 589856 | tf_op jit(solution)/shard_map/ppermute | solution.py:224
  48.4 1.8 collective-permute-start.8
  51.2 10.1 %all-to-all-start.1 = ((bf16[32,8,768]{2,1,0:T(8,128)(2,1)}), bf16[32,8,768]{2,1,0:T(8,128)(2,1)S(1)}, u32[]{:S(2)}, u32[]{:S(2)}) async-start(bf16[32,8,768]{2,1,0:T(8,128)(2,1)} %bitcast.10), calls=%async_computation.1 | async-start | bytes 786432 | tf_op jit(solution)/shard_map/all_to_all | solution.py:240
  63.5 2.7 collective-permute-start.10
  68.3 8.6 %all-to-all-done.1 = bf16[32,8,768]{2,1,0:T(8,128)(2,1)S(1)} async-done(((bf16[32,8,768]{2,1,0:T(8,128)(2,1)}), bf16[32,8,768]{2,1,0:T(8,128)(2,1)S(1)}, u32[]{:S(2)}, u32[]{:S(2)}) %all-to-all-start.1) | async-done | bytes 393248 | tf_op jit(solution)/shard_map/all_to_all | solution.py:240
  77.4 1.6 collective-permute-done.10.refs_8_
  79.0 4.5 %load_own.1 = (bf16[1536,3072]{1,0:T(8,128)(2,1)S(1)}, f32[2,128]{1,0:T(2,128)S(1)}, f32[2,128]{1,0:T(2,128)S(1)}, f32[6,768]{1,0:T(8,128)S(1)}, f32[6,768]{1,0:T(8,128)S(1)}, /*index=5*/f32[6,768]{1,0:T(8,128)S(1)}) custom-call(s32[3]{0:T(128)S(1)} %pad_add_fusion.word_ref, bf16[192,1536]{1,0:T(8,128)(2,1)} %copy-done.6, bf16[192,1536]{1,0:T(8,128)(2,1)} %copy-done.10, ...), custom_call_target="tpu_custom_call" | custom-call | tf_op jit(solution)/shard_map/load_own/pallas_call | solution.py:258
  83.5 1.5 collective-permute-start.36
  85.0 4.1 front.16.own_ref
  89.1 3.3 collective-permute-start.13
  92.5 1.3 collective-permute-done.13.other_ref
  94.6 2.6 collective-permute-start.14
  97.3 8.1 %collective-permute-done.14.own_ref.hidden_ref = bf16[256,768]{1,0:T(8,128)(2,1)S(1)} collective-permute-done((bf16[256,768]{1,0:T(8,128)(2,1)S(1)}, bf16[256,768]{1,0:T(8,128)(2,1)S(1)}, u32[]{:S(2)}, u32[]{:S(2)}) %collective-permute-start.14) | collective-permute-done | bytes 393248 | tf_op jit(solution)/shard_map/ppermute | solution.py:309
  106.5 1.3 collective-permute-done.15.other_ref
  107.9 4.1 front.17.own_ref
  117.6 4.1 front.18.own_ref
  122.2 1.4 collective-permute-done.19.other_ref
  125.5 1.4 collective-permute-done.21.other_ref
  126.8 4.1 front.19.own_ref
  131.4 1.4 collective-permute-done.22.other_ref
  134.9 1.4 collective-permute-done.24.other_ref
  136.3 4.1 front.20.own_ref
  140.9 1.4 collective-permute-done.25.other_ref
  144.2 1.4 collective-permute-done.27.other_ref
  145.6 4.1 front.21.own_ref
  150.2 1.4 collective-permute-done.28.other_ref
  153.7 1.4 collective-permute-done.30.other_ref
  155.0 4.1 front.22.own_ref
  159.6 1.4 collective-permute-done.31.other_ref
  163.0 1.4 collective-permute-done.33.other_ref
  164.3 4.1 front.23.own_ref
  168.9 1.4 collective-permute-done.34.other_ref
  172.4 79.5 %collective-permute-done.35.hidden_ref = bf16[256,768]{1,0:T(8,128)(2,1)S(1)} collective-permute-done((bf16[256,768]{1,0:T(8,128)(2,1)S(1)}, bf16[256,768]{1,0:T(8,128)(2,1)S(1)}, u32[]{:S(2)}, u32[]{:S(2)}) %collective-permute-start.35) | collective-permute-done | bytes 393248 | tf_op jit(solution)/shard_map/ppermute | solution.py:309
  252.6 1.4 collective-permute-start.37
  255.3 4.1 front.24.own_ref
  263.4 8.4 %collective-permute-done.39.own_ref.hidden_ref = bf16[256,768]{1,0:T(8,128)(2,1)S(1)} collective-permute-done((bf16[256,768]{1,0:T(8,128)(2,1)S(1)}, bf16[256,768]{1,0:T(8,128)(2,1)S(1)}, u32[]{:S(2)}, u32[]{:S(2)}) %collective-permute-start.39) | collective-permute-done | bytes 393248 | tf_op jit(solution)/shard_map/ppermute | solution.py:309
  274.0 4.1 front.25.own_ref
  283.4 4.1 front.26.own_ref
  288.0 1.4 collective-permute-done.44.other_ref
  290.7 1.4 collective-permute-done.45.other_ref
  292.0 4.1 front.27.own_ref
  296.6 1.4 collective-permute-done.46.other_ref
  300.1 1.4 collective-permute-done.48.other_ref
  301.5 4.1 front.28.own_ref
  306.1 1.4 collective-permute-done.49.other_ref
  308.7 1.4 collective-permute-done.50.other_ref
  310.1 4.1 front.29.own_ref
  314.7 1.4 collective-permute-done.51.other_ref
  318.2 1.4 collective-permute-done.53.other_ref
  319.6 4.1 front.30.own_ref
  324.2 1.4 collective-permute-done.54.other_ref
  326.8 1.4 collective-permute-done.55.other_ref
  328.1 4.1 front.31.own_ref
  332.7 1.4 collective-permute-done.56.other_ref
  334.1 3.7 copy-done.1
  338.6 7.7 %all_to_all.20 = bf16[4,8,768]{2,1,0:T(8,128)(2,1)S(1)} all-to-all(bf16[4,8,768]{2,1,0:T(8,128)(2,1)S(1)} %fusion), channel_id=1, replica_groups={{0,1,2,3},{4,5,6,7},{8,9,10,11},{12,13,14,15},{16,17,18,19},{20,21,22,2..., dimensions={0} | all-to-all | bytes 98304 | tf_op jit(solution)/shard_map/all_to_all | solution.py:327
  346.5 81.6 %all_to_all.21.got_ref = bf16[8,2,8,192]{3,2,1,0:T(8,128)(2,1)S(1)} all-to-all(bf16[8,2,8,192]{3,2,1,0:T(8,128)(2,1)S(1)} %bitcast.28), channel_id=1, replica_groups=mesh['pipe'=8,'seq'=32] {'pipe'}, dimensions={0} | all-to-all | bytes 98304 | tf_op jit(solution)/shard_map/all_to_all | solution.py:332
  (131 shorter events, 60.9 us)
Async XLA Ops:
  0.0 66.9 %copy-start.5 = (f32[1,2,128]{2,1,0:T(2,128)S(1)}, f32[1,2,128]{2,1,0:T(2,128)}, u32[]{:S(2)}) copy-start(f32[1,2,128]{2,1,0:T(2,128)} %refs_11_.1) | copy-start | bytes 3076
  0.0 79.0 %copy-start.3 = (s32[2,2]{1,0:T(2,128)S(1)}, s32[2,2]{1,0:T(2,128)}, u32[]{:S(2)}) copy-start(s32[2,2]{1,0:T(2,128)} %time_ref.3) | copy-start | bytes 52
  1.1 4.3 %collective-permute-start = (bf16[48,1536]{1,0:T(8,128)(2,1)S(1)}, bf16[48,1536]{1,0:T(8,128)(2,1)S(1)}, u32[]{:S(2)}, u32[]{:S(2)}) collective-permute-start(bf16[48,1536]{1,0:T(8,128)(2,1)S(1)} %pad_maximum_fusion.3), channel_id=1, source_target_pairs={{0,1},{1,0},{2,3},{3,2},{4,5},{5,4},{6,7},{7,6},{8,9},{9,8},{10,11... | collective-permute-start | bytes 442376 | tf_op jit(solution)/shard_map/ppermute | solution.py:188
  5.5 9.8 %collective-permute-start.1 = (bf16[96,1536]{1,0:T(8,128)(2,1)S(1)}, bf16[96,1536]{1,0:T(8,128)(2,1)S(1)}, u32[]{:S(2)}, u32[]{:S(2)}) collective-permute-start(bf16[96,1536]{1,0:T(8,128)(2,1)S(1)} %pad_maximum_fusion.1), channel_id=1, source_target_pairs={{0,2},{1,3},{2,0},{3,1},{4,6},{5,7},{6,4},{7,5},{8,10},{9,11},{10,... | collective-permute-start | bytes 884744 | tf_op jit(solution)/shard_map/ppermute | solution.py:203
  8.2 9.3 %all-to-all-start = ((bf16[8,2,8,192]{3,2,1,0:T(8,128)(2,1)}), bf16[8,2,8,192]{3,2,1,0:T(8,128)(2,1)S(1)}, u32[]{:S(2)}, u32[]{:S(2)}) async-start(bf16[8,2,8,192]{3,2,1,0:T(8,128)(2,1)} %broadcast_in_dim.6), calls=%async_computation | async-start | bytes 131072 | tf_op jit(solution)/shard_map/all_to_all | solution.py:206
  15.5 63.5 %copy-start.6 = (bf16[192,1536]{1,0:T(8,128)(2,1)}, bf16[192,1536]{1,0:T(8,128)(2,1)S(1)}, u32[]{:S(2)}) copy-start(bf16[192,1536]{1,0:T(8,128)(2,1)S(1)} %pad_maximum_fusion.refs_0_) | copy-start | bytes 1769476
  17.4 16.2 %collective-permute-start.3 = (bf16[192,1536]{1,0:T(8,128)(2,1)S(1)}, bf16[192,1536]{1,0:T(8,128)(2,1)S(1)}, u32[]{:S(2)}, u32[]{:S(2)}) collective-permute-start(bf16[192,1536]{1,0:T(8,128)(2,1)S(1)} %pad_maximum_fusion.refs_0_), channel_id=1, source_target_pairs={{0,28},{1,29},{2,30},{3,31},{4,0},{5,1},{6,2},{7,3},{8,4},{9,5},{1... | collective-permute-start | bytes 1769480 | tf_op jit(solution)/shard_map/ppermute | solution.py:224
  23.0 13.7 %collective-permute-start.2 = (bf16[192,1536]{1,0:T(8,128)(2,1)S(1)}, bf16[192,1536]{1,0:T(8,128)(2,1)S(1)}, u32[]{:S(2)}, u32[]{:S(2)}) collective-permute-start(bf16[192,1536]{1,0:T(8,128)(2,1)S(1)} %pad_maximum_fusion.refs_0_), channel_id=1, source_target_pairs={{0,4},{1,5},{2,6},{3,7},{4,8},{5,9},{6,10},{7,11},{8,12},{9,13},{1... | collective-permute-start | bytes 1769480 | tf_op jit(solution)/shard_map/ppermute | solution.py:223
  36.7 11.7 %collective-permute-start.6 = (bf16[192,1536]{1,0:T(8,128)(2,1)S(1)}, bf16[192,1536]{1,0:T(8,128)(2,1)}, u32[]{:S(2)}, u32[]{:S(2)}) collective-permute-start(bf16[192,1536]{1,0:T(8,128)(2,1)S(1)} %collective-permute-done.3.refs_2_), channel_id=1, source_target_pairs={{0,28},{1,29},{2,30},{3,31},{4,0},{5,1},{6,2},{7,3},{8,4},{9,5},{1... | collective-permute-start | bytes 1769480 | tf_op jit(solution)/shard_map/ppermute | solution.py:224
  37.1 13.2 %collective-permute-start.5 = (bf16[192,1536]{1,0:T(8,128)(2,1)S(1)}, bf16[192,1536]{1,0:T(8,128)(2,1)}, u32[]{:S(2)}, u32[]{:S(2)}) collective-permute-start(bf16[192,1536]{1,0:T(8,128)(2,1)S(1)} %collective-permute-done.2.refs_1_), channel_id=1, source_target_pairs={{0,4},{1,5},{2,6},{3,7},{4,8},{5,9},{6,10},{7,11},{8,12},{9,13},{1... | collective-permute-start | bytes 1769480 | tf_op jit(solution)/shard_map/ppermute | solution.py:223
  48.4 14.2 %collective-permute-start.8 = (bf16[192,1536]{1,0:T(8,128)(2,1)}, bf16[192,1536]{1,0:T(8,128)(2,1)S(1)}, u32[]{:S(2)}, u32[]{:S(2)}) collective-permute-start(bf16[192,1536]{1,0:T(8,128)(2,1)} %collective-permute-done.6.refs_4_), channel_id=1, source_target_pairs={{0,28},{1,29},{2,30},{3,31},{4,0},{5,1},{6,2},{7,3},{8,4},{9,5},{1... | collective-permute-start | bytes 1769480 | tf_op jit(solution)/shard_map/ppermute | solution.py:224
  50.3 15.9 %collective-permute-start.7 = (bf16[192,1536]{1,0:T(8,128)(2,1)}, bf16[192,1536]{1,0:T(8,128)(2,1)S(1)}, u32[]{:S(2)}, u32[]{:S(2)}) collective-permute-start(bf16[192,1536]{1,0:T(8,128)(2,1)} %collective-permute-done.5.refs_3_), channel_id=1, source_target_pairs={{0,4},{1,5},{2,6},{3,7},{4,8},{5,9},{6,10},{7,11},{8,12},{9,13},{1... | collective-permute-start | bytes 1769480 | tf_op jit(solution)/shard_map/ppermute | solution.py:223
  51.2 25.6 %all-to-all-start.1 = ((bf16[32,8,768]{2,1,0:T(8,128)(2,1)}), bf16[32,8,768]{2,1,0:T(8,128)(2,1)S(1)}, u32[]{:S(2)}, u32[]{:S(2)}) async-start(bf16[32,8,768]{2,1,0:T(8,128)(2,1)} %bitcast.10), calls=%async_computation.1 | async-start | bytes 786432 | tf_op jit(solution)/shard_map/all_to_all | solution.py:240
  61.3 16.0 %collective-permute-start.11 = (f32[1,16,4608]{2,1,0:T(8,128)S(1)}, f32[1,16,4608]{2,1,0:T(8,128)S(1)}, u32[]{:S(2)}, u32[]{:S(2)}) collective-permute-start(f32[1,16,4608]{2,1,0:T(8,128)S(1)} %copy-done.2), channel_id=1, source_target_pairs={{32,0},{96,64},{160,128},{224,192},{33,1},{97,65},{161,129},{225,1... | collective-permute-start | bytes 884744 | tf_op jit(solution)/shard_map/ppermute | solution.py:213
  63.5 15.5 %collective-permute-start.10 = (bf16[96,1536]{1,0:T(8,128)(2,1)}, bf16[96,1536]{1,0:T(8,128)(2,1)}, u32[]{:S(2)}, u32[]{:S(2)}) collective-permute-start(bf16[96,1536]{1,0:T(8,128)(2,1)} %slice.19), channel_id=1, source_target_pairs={{0,28},{1,29},{2,30},{3,31},{4,0},{5,1},{6,2},{7,3},{8,4},{9,5},{1... | collective-permute-start | bytes 884744 | tf_op jit(solution)/shard_map/ppermute | solution.py:231
  66.9 12.0 %collective-permute-start.9 = (bf16[96,1536]{1,0:T(8,128)(2,1)}, bf16[96,1536]{1,0:T(8,128)(2,1)}, u32[]{:S(2)}, u32[]{:S(2)}) collective-permute-start(bf16[96,1536]{1,0:T(8,128)(2,1)} %slice.18), channel_id=1, source_target_pairs={{0,4},{1,5},{2,6},{3,7},{4,8},{5,9},{6,10},{7,11},{8,12},{9,13},{1... | collective-permute-start | bytes 884744 | tf_op jit(solution)/shard_map/ppermute | solution.py:230
  66.9 10.4 %collective-permute-start.12 = (f32[1,2,128]{2,1,0:T(2,128)S(1)}, f32[1,2,128]{2,1,0:T(2,128)S(1)}, u32[]{:S(2)}, u32[]{:S(2)}) collective-permute-start(f32[1,2,128]{2,1,0:T(2,128)S(1)} %copy-done.5), channel_id=1, source_target_pairs={{32,0},{96,64},{160,128},{224,192},{33,1},{97,65},{161,129},{225,1... | collective-permute-start | bytes 3080 | tf_op jit(solution)/shard_map/ppermute | solution.py:213
  76.8 8.2 %collective-permute-start.4 = (bf16[256,768]{1,0:T(8,128)(2,1)S(1)}, bf16[256,768]{1,0:T(8,128)(2,1)S(1)}, u32[]{:S(2)}, u32[]{:S(2)}) collective-permute-start(bf16[256,768]{1,0:T(8,128)(2,1)S(1)} %bitcast.22), channel_id=1, source_target_pairs={{0,1},{1,0},{2,3},{3,2},{4,5},{5,4},{6,7},{7,6},{8,9},{9,8},{10,11... | collective-permute-start | bytes 1179656 | tf_op jit(solution)/shard_map/ppermute | solution.py:188
  83.5 168.4 %collective-permute-start.36 = (bf16[1536,3072]{1,0:T(8,128)(2,1)S(1)}, bf16[1536,3072]{1,0:T(8,128)(2,1)S(1)}, u32[]{:S(2)}, u32[]{:S(2)}) collective-permute-start(bf16[1536,3072]{1,0:T(8,128)(2,1)S(1)} %get-tuple-element.35.weight_ref), channel_id=1, source_target_pairs={{96,64},{160,128},{224,192},{97,65},{161,129},{225,193},{98,66},{1... | collective-permute-start | bytes 28311560 | tf_op jit(solution)/shard_map/ppermute | solution.py:300
  89.1 4.7 %collective-permute-start.13 = (bf16[256,768]{1,0:T(8,128)(2,1)S(1)}, bf16[256,768]{1,0:T(8,128)(2,1)S(1)}, u32[]{:S(2)}, u32[]{:S(2)}) collective-permute-start(bf16[256,768]{1,0:T(8,128)(2,1)S(1)} %front.16.own_ref), channel_id=1, source_target_pairs={{0,1},{1,0},{2,3},{3,2},{4,5},{5,4},{6,7},{7,6},{8,9},{9,8},{10,11... | collective-permute-start | bytes 1179656 | tf_op jit(solution)/shard_map/ppermute | solution.py:188
  94.6 10.7 %collective-permute-start.14 = (bf16[256,768]{1,0:T(8,128)(2,1)S(1)}, bf16[256,768]{1,0:T(8,128)(2,1)S(1)}, u32[]{:S(2)}, u32[]{:S(2)}) collective-permute-start(bf16[256,768]{1,0:T(8,128)(2,1)S(1)} %back.16), channel_id=1, source_target_pairs={{0,32},{1,33},{2,34},{3,35},{4,36},{5,37},{6,38},{7,39},{8,40},{9,... | collective-permute-start | bytes 1179656 | tf_op jit(solution)/shard_map/ppermute | solution.py:309
  105.3 2.5 collective-permute-start.15
  112.0 1.8 collective-permute-start.16
  114.7 0.7 collective-permute-start.17
  115.4 2.2 collective-permute-start.18
  121.7 1.8 collective-permute-start.19
  124.3 0.7 collective-permute-start.20
  125.0 1.8 collective-permute-start.21
  131.0 1.8 collective-permute-start.22
  133.6 0.7 collective-permute-start.23
  134.3 2.0 collective-permute-start.24
  140.4 1.8 collective-permute-start.25
  143.0 0.7 collective-permute-start.26
  143.7 1.8 collective-permute-start.27
  149.7 1.8 collective-permute-start.28
  152.3 0.7 collective-permute-start.29
  153.0 2.0 collective-permute-start.30
  159.2 1.8 collective-permute-start.31
  161.8 0.7 collective-permute-start.32
  162.5 1.8 collective-permute-start.33
  168.4 83.4 %copy-start.4 = (f32[16]{0:T(128)S(1)}, f32[16]{0:T(128)}, u32[]{:S(2)}) copy-start(f32[16]{0:T(128)} %size_ref.3) | copy-start | bytes 196
  168.5 1.8 collective-permute-start.34
  171.1 80.8 %collective-permute-start.35 = (bf16[256,768]{1,0:T(8,128)(2,1)S(1)}, bf16[256,768]{1,0:T(8,128)(2,1)S(1)}, u32[]{:S(2)}, u32[]{:S(2)}) collective-permute-start(bf16[256,768]{1,0:T(8,128)(2,1)S(1)} %back.23), channel_id=1, source_target_pairs={{224,0},{225,1},{226,2},{227,3},{228,4},{229,5},{230,6},{231,7},{2... | collective-permute-start | bytes 1179656 | tf_op jit(solution)/shard_map/ppermute | solution.py:309
  251.9 76.3 %copy-start = (bf16[1536,3072]{1,0:T(8,128)(2,1)}, bf16[1536,3072]{1,0:T(8,128)(2,1)S(1)}, u32[]{:S(2)}) copy-start(bf16[1536,3072]{1,0:T(8,128)(2,1)S(1)} %collective-permute-done.36.weight_ref) | copy-start | bytes 28311556
  252.6 2.7 collective-permute-start.37
  259.4 1.8 collective-permute-start.38
  262.0 9.7 %collective-permute-start.39 = (bf16[256,768]{1,0:T(8,128)(2,1)S(1)}, bf16[256,768]{1,0:T(8,128)(2,1)S(1)}, u32[]{:S(2)}, u32[]{:S(2)}) collective-permute-start(bf16[256,768]{1,0:T(8,128)(2,1)S(1)} %back.24), channel_id=1, source_target_pairs={{0,32},{1,33},{2,34},{3,35},{4,36},{5,37},{6,38},{7,39},{8,40},{9,... | collective-permute-start | bytes 1179656 | tf_op jit(solution)/shard_map/ppermute | solution.py:309
  271.8 2.2 collective-permute-start.40
  278.1 1.8 collective-permute-start.41
  280.8 0.7 collective-permute-start.42
  281.5 2.0 collective-permute-start.43
  287.6 1.8 collective-permute-start.44
  290.2 1.8 collective-permute-start.45
  296.1 1.8 collective-permute-start.46
  298.8 0.7 collective-permute-start.47
  299.5 2.0 collective-permute-start.48
  305.6 1.8 collective-permute-start.49
  308.2 1.8 collective-permute-start.50
  314.2 1.8 collective-permute-start.51
  316.8 0.7 collective-permute-start.52
  317.5 2.1 collective-permute-start.53
  323.7 1.8 collective-permute-start.54
  326.3 1.8 collective-permute-start.55
  332.3 1.8 collective-permute-start.56
  (6 other events, 141.1 us)

commit v7 on v6

--- a/solution.py
+++ b/solution.py
@@ -308,8 +308,9 @@
             if place != holder:
                 hidden = lax.ppermute(hidden, "pipe", [(holder, place)])
                 holder = place
+            if step > 0 and section == 2:
+                hidden, following[2] = lax.optimization_barrier((hidden, following[2]))
             if step > 0 and section == 0:
-                hidden, following[2] = lax.optimization_barrier((hidden, following[2]))
                 slot = pl.pallas_call(
                     advance_slot(step - 1),
                     out_shape=jax.ShapeDtypeStruct((tokens, half), jnp.bfloat16),

time: 438 us -> 449 us (1.025)
  waiting for transfers between devices: 178 us -> 188 us
  blocking collectives: 89.4 us -> 97.6 us
  starting transfers between devices: 66.9 us -> 61.4 us
    all_to_all x1, blocking collectives: 81.6 us -> 88.5 us  [shards(): got = lax.all_to_all(sent, 'pipe', 0, 0, tiled=True)]
    all_to_all x1, waiting for transfers between devices: 8.55 us -> 13.7 us  [shards(): slot = lax.all_to_all(sent, 'seq', 0, 0, tiled=True).reshape(tokens, half)]
  transfers between devices with their start and end apart: 59 -> 59, of which waited for: 42 -> 43; matrix products, arithmetic and copies ran while one was open for 1% -> 1% of each run, Pallas kernels for 10% -> 10%
where the time goes in v7:
time: 449 us; the launch traced here: 442 us
  waiting for transfers between devices  188 us (42%)
  blocking collectives  97.6 us (22%)
  Pallas kernels  85.2 us (19%)
  starting transfers between devices  61.4 us (14%)
  local copies, waits for them, and re-layouts  8.73 us (2%)
    ppermute x12, waiting for transfers between devices, shards(): hidden = lax.ppermute(hidden, 'pipe', [(holder, place)])  99.3 us
    all_to_all x1, blocking collectives, shards(): got = lax.all_to_all(sent, 'pipe', 0, 0, tiled=True)  88.5 us
    pallas_call x16, Pallas kernels, layer(): pl.pallas_call(layer_front(head_dim), out_shape=jax.ShapeDtypeStruct((tok...  66.2 us
    ppermute x33, waiting for transfers between devices, swapped(): return lax.ppermute(value, 'seq', core_pairs)  44.1 us
    ppermute x33, starting transfers between devices, swapped(): return lax.ppermute(value, 'seq', core_pairs)  21.8 us
    ppermute x3, waiting for transfers between devices, shards(): falling = lax.ppermute(falling, 'seq', rings[1])  17.6 us
    all_to_all x1, waiting for transfers between devices, shards(): slot = lax.all_to_all(sent, 'seq', 0, 0, tiled=True).reshape(tokens, half)  13.7 us
    pallas_call x16, Pallas kernels, layer(): pl.pallas_call(layer_back, out_shape=jax.ShapeDtypeStruct((tokens, half),...  12.7 us
  transfers between devices with their start and end apart: 59, of which 43 were waited for; matrix products, arithmetic and copies ran while one was open for 1% of the time, Pallas kernels for 10%

profile of v7, /device:TPU:1, one launch (start us, length us, event | category | flops | bytes accessed | tf_op | source)
XLA Modules:
  0.0 442.3 jit_solution(15378206264881228796)
XLA Ops:
  1.1 3.3 collective-permute-start
  8.1 4.1 all-to-all-start
  12.3 3.1 collective-permute-done.1
  15.5 2.0 all-to-all-done
  17.4 5.6 %collective-permute-start.3 = (bf16[192,1536]{1,0:T(8,128)(2,1)S(1)}, bf16[192,1536]{1,0:T(8,128)(2,1)S(1)}, u32[]{:S(2)}, u32[]{:S(2)}) collective-permute-start(bf16[192,1536]{1,0:T(8,128)(2,1)S(1)} %pad_maximum_fusion.refs_0_), channel_id=1, source_target_pairs={{0,28},{1,29},{2,30},{3,31},{4,0},{5,1},{6,2},{7,3},{8,4},{9,5},{1... | collective-permute-start | bytes 1769480 | tf_op jit(solution)/shard_map/ppermute | solution.py:224
  23.0 10.6 %collective-permute-done.3.refs_2_ = bf16[192,1536]{1,0:T(8,128)(2,1)S(1)} collective-permute-done((bf16[192,1536]{1,0:T(8,128)(2,1)S(1)}, bf16[192,1536]{1,0:T(8,128)(2,1)S(1)}, u32[]{:S(2)}, u32[]{:S(2)}) %collective-permute-start.3) | collective-permute-done | bytes 589856 | tf_op jit(solution)/shard_map/ppermute | solution.py:224
  33.6 3.1 collective-permute-done.2.refs_1_
  39.1 8.1 %all-to-all-start.1 = ((bf16[32,8,768]{2,1,0:T(8,128)(2,1)}), bf16[32,8,768]{2,1,0:T(8,128)(2,1)S(1)}, u32[]{:S(2)}, u32[]{:S(2)}) async-start(bf16[32,8,768]{2,1,0:T(8,128)(2,1)} %bitcast.10), calls=%async_computation.1 | async-start | bytes 786432 | tf_op jit(solution)/shard_map/all_to_all | solution.py:240
  48.4 1.8 collective-permute-start.8
  50.3 13.7 %all-to-all-done.1 = bf16[32,8,768]{2,1,0:T(8,128)(2,1)S(1)} async-done(((bf16[32,8,768]{2,1,0:T(8,128)(2,1)}), bf16[32,8,768]{2,1,0:T(8,128)(2,1)S(1)}, u32[]{:S(2)}, u32[]{:S(2)}) %all-to-all-start.1) | async-done | bytes 393248 | tf_op jit(solution)/shard_map/all_to_all | solution.py:240
  65.2 5.9 %collective-permute-done.8.refs_6_ = bf16[192,1536]{1,0:T(8,128)(2,1)S(1)} collective-permute-done((bf16[192,1536]{1,0:T(8,128)(2,1)}, bf16[192,1536]{1,0:T(8,128)(2,1)S(1)}, u32[]{:S(2)}, u32[]{:S(2)}) %collective-permute-start.8) | collective-permute-done | bytes 589856 | tf_op jit(solution)/shard_map/ppermute | solution.py:224
  74.2 1.5 collective-permute-start.12
  75.7 3.1 collective-permute-done.12.refs_13_
  78.9 2.2 collective-permute-done.9.refs_7_
  81.1 4.4 %load_own.1 = (bf16[1536,3072]{1,0:T(8,128)(2,1)S(1)}, f32[2,128]{1,0:T(2,128)S(1)}, f32[2,128]{1,0:T(2,128)S(1)}, f32[6,768]{1,0:T(8,128)S(1)}, f32[6,768]{1,0:T(8,128)S(1)}, /*index=5*/f32[6,768]{1,0:T(8,128)S(1)}) custom-call(s32[3]{0:T(128)S(1)} %pad_add_fusion.word_ref, bf16[192,1536]{1,0:T(8,128)(2,1)} %copy-done.6, bf16[192,1536]{1,0:T(8,128)(2,1)} %copy-done.10, ...), custom_call_target="tpu_custom_call" | custom-call | tf_op jit(solution)/shard_map/load_own/pallas_call | solution.py:258
  85.6 4.1 front.16.own_ref
  89.7 4.2 collective-permute-start.13
  96.0 2.4 collective-permute-start.14
  98.4 8.1 %collective-permute-done.14.own_ref.hidden_ref = bf16[256,768]{1,0:T(8,128)(2,1)S(1)} collective-permute-done((bf16[256,768]{1,0:T(8,128)(2,1)S(1)}, bf16[256,768]{1,0:T(8,128)(2,1)S(1)}, u32[]{:S(2)}, u32[]{:S(2)}) %collective-permute-start.14) | collective-permute-done | bytes 393248 | tf_op jit(solution)/shard_map/ppermute | solution.py:309
  107.7 1.3 collective-permute-done.15.other_ref
  109.1 4.1 front.17.own_ref
  113.7 1.4 collective-permute-done.16.other_ref
  117.0 1.7 collective-permute-start.42
  118.7 4.1 front.18.own_ref
  123.0 1.6 collective-permute-done.19.other_ref
  126.4 1.6 collective-permute-done.21.other_ref
  127.9 4.1 front.19.own_ref
  132.3 1.6 collective-permute-done.22.other_ref
  135.8 1.6 collective-permute-done.24.other_ref
  137.4 4.1 front.20.own_ref
  141.8 1.6 collective-permute-done.25.other_ref
  145.1 1.6 collective-permute-done.27.other_ref
  146.7 4.1 front.21.own_ref
  151.0 1.6 collective-permute-done.28.other_ref
  154.6 1.6 collective-permute-done.30.other_ref
  156.1 4.1 front.22.own_ref
  160.5 1.6 collective-permute-done.31.other_ref
  163.8 1.6 collective-permute-done.33.other_ref
  165.4 4.1 front.23.own_ref
  169.8 1.6 collective-permute-done.34.other_ref
  173.5 82.7 %collective-permute-done.35.hidden_ref = bf16[256,768]{1,0:T(8,128)(2,1)S(1)} collective-permute-done((bf16[256,768]{1,0:T(8,128)(2,1)S(1)}, bf16[256,768]{1,0:T(8,128)(2,1)S(1)}, u32[]{:S(2)}, u32[]{:S(2)}) %collective-permute-start.35) | collective-permute-done | bytes 393248 | tf_op jit(solution)/shard_map/ppermute | solution.py:309
  256.9 1.4 collective-permute-start.36
  258.3 1.3 collective-permute-done.36.other_ref
  259.6 4.1 front.24.own_ref
  267.7 8.4 %collective-permute-done.38.own_ref.hidden_ref = bf16[256,768]{1,0:T(8,128)(2,1)S(1)} collective-permute-done((bf16[256,768]{1,0:T(8,128)(2,1)S(1)}, bf16[256,768]{1,0:T(8,128)(2,1)S(1)}, u32[]{:S(2)}, u32[]{:S(2)}) %collective-permute-start.38) | collective-permute-done | bytes 393248 | tf_op jit(solution)/shard_map/ppermute | solution.py:309
  278.3 4.1 front.25.own_ref
  287.8 4.1 front.26.own_ref
  296.4 4.1 front.27.own_ref
  301.0 1.4 collective-permute-done.46.other_ref
  304.5 1.4 collective-permute-done.48.other_ref
  305.9 4.1 front.28.own_ref
  310.5 1.4 collective-permute-done.49.other_ref
  313.1 1.4 collective-permute-done.50.other_ref
  314.4 4.1 front.29.own_ref
  319.0 1.4 collective-permute-done.51.other_ref
  322.6 1.4 collective-permute-done.53.other_ref
  323.9 4.1 front.30.own_ref
  328.5 1.4 collective-permute-done.54.other_ref
  331.2 1.4 collective-permute-done.55.other_ref
  332.5 4.1 front.31.own_ref
  337.1 1.4 collective-permute-done.56.other_ref
  338.5 3.7 copy-done.1
  343.0 9.1 %all_to_all.20 = bf16[4,8,768]{2,1,0:T(8,128)(2,1)S(1)} all-to-all(bf16[4,8,768]{2,1,0:T(8,128)(2,1)S(1)} %fusion), channel_id=1, replica_groups={{0,1,2,3},{4,5,6,7},{8,9,10,11},{12,13,14,15},{16,17,18,19},{20,21,22,2..., dimensions={0} | all-to-all | bytes 98304 | tf_op jit(solution)/shard_map/all_to_all | solution.py:328
  352.2 88.5 %all_to_all.21.got_ref = bf16[8,2,8,192]{3,2,1,0:T(8,128)(2,1)S(1)} all-to-all(bf16[8,2,8,192]{3,2,1,0:T(8,128)(2,1)S(1)} %bitcast.28), channel_id=1, replica_groups=mesh['pipe'=8,'seq'=32] {'pipe'}, dimensions={0} | all-to-all | bytes 98304 | tf_op jit(solution)/shard_map/all_to_all | solution.py:333
  (131 shorter events, 58.8 us)
Async XLA Ops:
  0.0 63.9 %copy-start.2 = (f32[1,16,4608]{2,1,0:T(8,128)S(1)}, f32[1,16,4608]{2,1,0:T(8,128)}, u32[]{:S(2)}) copy-start(f32[1,16,4608]{2,1,0:T(8,128)} %refs_10_.1) | copy-start | bytes 884740
  0.0 74.2 %copy-start.5 = (f32[1,2,128]{2,1,0:T(2,128)S(1)}, f32[1,2,128]{2,1,0:T(2,128)}, u32[]{:S(2)}) copy-start(f32[1,2,128]{2,1,0:T(2,128)} %refs_11_.1) | copy-start | bytes 3076
  0.0 81.1 %copy-start.3 = (s32[2,2]{1,0:T(2,128)S(1)}, s32[2,2]{1,0:T(2,128)}, u32[]{:S(2)}) copy-start(s32[2,2]{1,0:T(2,128)} %time_ref.3) | copy-start | bytes 52
  1.1 4.3 collective-permute-start
  5.5 9.8 %collective-permute-start.1 = (bf16[96,1536]{1,0:T(8,128)(2,1)S(1)}, bf16[96,1536]{1,0:T(8,128)(2,1)S(1)}, u32[]{:S(2)}, u32[]{:S(2)}) collective-permute-start(bf16[96,1536]{1,0:T(8,128)(2,1)S(1)} %pad_maximum_fusion.1), channel_id=1, source_target_pairs={{0,2},{1,3},{2,0},{3,1},{4,6},{5,7},{6,4},{7,5},{8,10},{9,11},{10,... | collective-permute-start | bytes 884744 | tf_op jit(solution)/shard_map/ppermute | solution.py:203
  8.1 9.3 %all-to-all-start = ((bf16[8,2,8,192]{3,2,1,0:T(8,128)(2,1)}), bf16[8,2,8,192]{3,2,1,0:T(8,128)(2,1)S(1)}, u32[]{:S(2)}, u32[]{:S(2)}) async-start(bf16[8,2,8,192]{3,2,1,0:T(8,128)(2,1)} %broadcast_in_dim.6), calls=%async_computation | async-start | bytes 131072 | tf_op jit(solution)/shard_map/all_to_all | solution.py:206
  15.5 65.6 %copy-start.6 = (bf16[192,1536]{1,0:T(8,128)(2,1)}, bf16[192,1536]{1,0:T(8,128)(2,1)S(1)}, u32[]{:S(2)}) copy-start(bf16[192,1536]{1,0:T(8,128)(2,1)S(1)} %pad_maximum_fusion.refs_0_) | copy-start | bytes 1769476
  17.4 16.2 %collective-permute-start.3 = (bf16[192,1536]{1,0:T(8,128)(2,1)S(1)}, bf16[192,1536]{1,0:T(8,128)(2,1)S(1)}, u32[]{:S(2)}, u32[]{:S(2)}) collective-permute-start(bf16[192,1536]{1,0:T(8,128)(2,1)S(1)} %pad_maximum_fusion.refs_0_), channel_id=1, source_target_pairs={{0,28},{1,29},{2,30},{3,31},{4,0},{5,1},{6,2},{7,3},{8,4},{9,5},{1... | collective-permute-start | bytes 1769480 | tf_op jit(solution)/shard_map/ppermute | solution.py:224
  23.0 13.7 %collective-permute-start.2 = (bf16[192,1536]{1,0:T(8,128)(2,1)S(1)}, bf16[192,1536]{1,0:T(8,128)(2,1)S(1)}, u32[]{:S(2)}, u32[]{:S(2)}) collective-permute-start(bf16[192,1536]{1,0:T(8,128)(2,1)S(1)} %pad_maximum_fusion.refs_0_), channel_id=1, source_target_pairs={{0,4},{1,5},{2,6},{3,7},{4,8},{5,9},{6,10},{7,11},{8,12},{9,13},{1... | collective-permute-start | bytes 1769480 | tf_op jit(solution)/shard_map/ppermute | solution.py:223
  36.7 11.7 %collective-permute-start.6 = (bf16[192,1536]{1,0:T(8,128)(2,1)S(1)}, bf16[192,1536]{1,0:T(8,128)(2,1)}, u32[]{:S(2)}, u32[]{:S(2)}) collective-permute-start(bf16[192,1536]{1,0:T(8,128)(2,1)S(1)} %collective-permute-done.3.refs_2_), channel_id=1, source_target_pairs={{0,28},{1,29},{2,30},{3,31},{4,0},{5,1},{6,2},{7,3},{8,4},{9,5},{1... | collective-permute-start | bytes 1769480 | tf_op jit(solution)/shard_map/ppermute | solution.py:224
  37.1 13.2 %collective-permute-start.5 = (bf16[192,1536]{1,0:T(8,128)(2,1)S(1)}, bf16[192,1536]{1,0:T(8,128)(2,1)}, u32[]{:S(2)}, u32[]{:S(2)}) collective-permute-start(bf16[192,1536]{1,0:T(8,128)(2,1)S(1)} %collective-permute-done.2.refs_1_), channel_id=1, source_target_pairs={{0,4},{1,5},{2,6},{3,7},{4,8},{5,9},{6,10},{7,11},{8,12},{9,13},{1... | collective-permute-start | bytes 1769480 | tf_op jit(solution)/shard_map/ppermute | solution.py:223
  39.1 24.8 %all-to-all-start.1 = ((bf16[32,8,768]{2,1,0:T(8,128)(2,1)}), bf16[32,8,768]{2,1,0:T(8,128)(2,1)S(1)}, u32[]{:S(2)}, u32[]{:S(2)}) async-start(bf16[32,8,768]{2,1,0:T(8,128)(2,1)} %bitcast.10), calls=%async_computation.1 | async-start | bytes 786432 | tf_op jit(solution)/shard_map/all_to_all | solution.py:240
  48.4 22.7 %collective-permute-start.8 = (bf16[192,1536]{1,0:T(8,128)(2,1)}, bf16[192,1536]{1,0:T(8,128)(2,1)S(1)}, u32[]{:S(2)}, u32[]{:S(2)}) collective-permute-start(bf16[192,1536]{1,0:T(8,128)(2,1)} %collective-permute-done.6.refs_4_), channel_id=1, source_target_pairs={{0,28},{1,29},{2,30},{3,31},{4,0},{5,1},{6,2},{7,3},{8,4},{9,5},{1... | collective-permute-start | bytes 1769480 | tf_op jit(solution)/shard_map/ppermute | solution.py:224
  50.3 22.9 %collective-permute-start.7 = (bf16[192,1536]{1,0:T(8,128)(2,1)}, bf16[192,1536]{1,0:T(8,128)(2,1)S(1)}, u32[]{:S(2)}, u32[]{:S(2)}) collective-permute-start(bf16[192,1536]{1,0:T(8,128)(2,1)} %collective-permute-done.5.refs_3_), channel_id=1, source_target_pairs={{0,4},{1,5},{2,6},{3,7},{4,8},{5,9},{6,10},{7,11},{8,12},{9,13},{1... | collective-permute-start | bytes 1769480 | tf_op jit(solution)/shard_map/ppermute | solution.py:223
  63.9 21.6 %collective-permute-start.4 = (bf16[256,768]{1,0:T(8,128)(2,1)S(1)}, bf16[256,768]{1,0:T(8,128)(2,1)S(1)}, u32[]{:S(2)}, u32[]{:S(2)}) collective-permute-start(bf16[256,768]{1,0:T(8,128)(2,1)S(1)} %bitcast.22), channel_id=1, source_target_pairs={{0,1},{1,0},{2,3},{3,2},{4,5},{5,4},{6,7},{7,6},{8,9},{9,8},{10,11... | collective-permute-start | bytes 1179656 | tf_op jit(solution)/shard_map/ppermute | solution.py:188
  63.9 14.9 %collective-permute-start.11 = (f32[1,16,4608]{2,1,0:T(8,128)S(1)}, f32[1,16,4608]{2,1,0:T(8,128)S(1)}, u32[]{:S(2)}, u32[]{:S(2)}) collective-permute-start(f32[1,16,4608]{2,1,0:T(8,128)S(1)} %copy-done.2), channel_id=1, source_target_pairs={{32,0},{96,64},{160,128},{224,192},{33,1},{97,65},{161,129},{225,1... | collective-permute-start | bytes 884744 | tf_op jit(solution)/shard_map/ppermute | solution.py:213
  71.9 7.0 %collective-permute-start.10 = (bf16[96,1536]{1,0:T(8,128)(2,1)}, bf16[96,1536]{1,0:T(8,128)(2,1)}, u32[]{:S(2)}, u32[]{:S(2)}) collective-permute-start(bf16[96,1536]{1,0:T(8,128)(2,1)} %slice.19), channel_id=1, source_target_pairs={{0,28},{1,29},{2,30},{3,31},{4,0},{5,1},{6,2},{7,3},{8,4},{9,5},{1... | collective-permute-start | bytes 884744 | tf_op jit(solution)/shard_map/ppermute | solution.py:231
  74.0 7.1 %collective-permute-start.9 = (bf16[96,1536]{1,0:T(8,128)(2,1)}, bf16[96,1536]{1,0:T(8,128)(2,1)}, u32[]{:S(2)}, u32[]{:S(2)}) collective-permute-start(bf16[96,1536]{1,0:T(8,128)(2,1)} %slice.18), channel_id=1, source_target_pairs={{0,4},{1,5},{2,6},{3,7},{4,8},{5,9},{6,10},{7,11},{8,12},{9,13},{1... | collective-permute-start | bytes 884744 | tf_op jit(solution)/shard_map/ppermute | solution.py:230
  74.2 4.7 %collective-permute-start.12 = (f32[1,2,128]{2,1,0:T(2,128)S(1)}, f32[1,2,128]{2,1,0:T(2,128)S(1)}, u32[]{:S(2)}, u32[]{:S(2)}) collective-permute-start(f32[1,2,128]{2,1,0:T(2,128)S(1)} %copy-done.5), channel_id=1, source_target_pairs={{32,0},{96,64},{160,128},{224,192},{33,1},{97,65},{161,129},{225,1... | collective-permute-start | bytes 3080 | tf_op jit(solution)/shard_map/ppermute | solution.py:213
  89.7 5.5 %collective-permute-start.13 = (bf16[256,768]{1,0:T(8,128)(2,1)S(1)}, bf16[256,768]{1,0:T(8,128)(2,1)S(1)}, u32[]{:S(2)}, u32[]{:S(2)}) collective-permute-start(bf16[256,768]{1,0:T(8,128)(2,1)S(1)} %front.16.own_ref), channel_id=1, source_target_pairs={{0,1},{1,0},{2,3},{3,2},{4,5},{5,4},{6,7},{7,6},{8,9},{9,8},{10,11... | collective-permute-start | bytes 1179656 | tf_op jit(solution)/shard_map/ppermute | solution.py:188
  96.0 10.5 %collective-permute-start.14 = (bf16[256,768]{1,0:T(8,128)(2,1)S(1)}, bf16[256,768]{1,0:T(8,128)(2,1)S(1)}, u32[]{:S(2)}, u32[]{:S(2)}) collective-permute-start(bf16[256,768]{1,0:T(8,128)(2,1)S(1)} %back.16), channel_id=1, source_target_pairs={{0,32},{1,33},{2,34},{3,35},{4,36},{5,37},{6,38},{7,39},{8,40},{9,... | collective-permute-start | bytes 1179656 | tf_op jit(solution)/shard_map/ppermute | solution.py:309
  106.5 2.5 collective-permute-start.15
  113.2 1.8 collective-permute-start.16
  115.8 0.7 collective-permute-start.17
  116.5 2.1 collective-permute-start.18
  117.0 168.8 %collective-permute-start.42 = (bf16[1536,3072]{1,0:T(8,128)(2,1)S(1)}, bf16[1536,3072]{1,0:T(8,128)(2,1)S(1)}, u32[]{:S(2)}, u32[]{:S(2)}) collective-permute-start(bf16[1536,3072]{1,0:T(8,128)(2,1)S(1)} %get-tuple-element.35.weight_ref), channel_id=1, source_target_pairs={{96,64},{160,128},{224,192},{97,65},{161,129},{225,193},{98,66},{1... | collective-permute-start | bytes 28311560 | tf_op jit(solution)/shard_map/ppermute | solution.py:300
  122.8 1.8 collective-permute-start.19
  125.4 0.7 collective-permute-start.20
  126.1 1.8 collective-permute-start.21
  132.1 1.8 collective-permute-start.22
  134.7 0.7 collective-permute-start.23
  135.4 2.0 collective-permute-start.24
  141.5 1.8 collective-permute-start.25
  144.1 0.7 collective-permute-start.26
  144.8 1.8 collective-permute-start.27
  150.8 1.8 collective-permute-start.28
  153.4 0.7 collective-permute-start.29
  154.1 2.0 collective-permute-start.30
  160.3 1.8 collective-permute-start.31
  162.9 0.7 collective-permute-start.32
  163.6 1.8 collective-permute-start.33
  169.6 86.7 %copy-start.4 = (f32[16]{0:T(128)S(1)}, f32[16]{0:T(128)}, u32[]{:S(2)}) copy-start(f32[16]{0:T(128)} %size_ref.3) | copy-start | bytes 196
  169.6 1.8 collective-permute-start.34
  172.2 84.0 %collective-permute-start.35 = (bf16[256,768]{1,0:T(8,128)(2,1)S(1)}, bf16[256,768]{1,0:T(8,128)(2,1)S(1)}, u32[]{:S(2)}, u32[]{:S(2)}) collective-permute-start(bf16[256,768]{1,0:T(8,128)(2,1)S(1)} %back.23), channel_id=1, source_target_pairs={{224,0},{225,1},{226,2},{227,3},{228,4},{229,5},{230,6},{231,7},{2... | collective-permute-start | bytes 1179656 | tf_op jit(solution)/shard_map/ppermute | solution.py:309
  256.9 2.7 collective-permute-start.36
  263.8 1.8 collective-permute-start.37
  266.4 9.7 %collective-permute-start.38 = (bf16[256,768]{1,0:T(8,128)(2,1)S(1)}, bf16[256,768]{1,0:T(8,128)(2,1)S(1)}, u32[]{:S(2)}, u32[]{:S(2)}) collective-permute-start(bf16[256,768]{1,0:T(8,128)(2,1)S(1)} %back.24), channel_id=1, source_target_pairs={{0,32},{1,33},{2,34},{3,35},{4,36},{5,37},{6,38},{7,39},{8,40},{9,... | collective-permute-start | bytes 1179656 | tf_op jit(solution)/shard_map/ppermute | solution.py:309
  276.1 2.2 collective-permute-start.39
  282.5 1.8 collective-permute-start.40
  285.1 0.7 collective-permute-start.41
  285.8 2.0 collective-permute-start.43
  291.9 1.8 collective-permute-start.44
  294.6 1.8 collective-permute-start.45
  300.5 1.8 collective-permute-start.46
  303.1 0.7 collective-permute-start.47
  303.8 2.0 collective-permute-start.48
  310.0 1.8 collective-permute-start.49
  312.6 1.8 collective-permute-start.50
  318.6 1.8 collective-permute-start.51
  321.2 0.7 collective-permute-start.52
  321.9 2.1 collective-permute-start.53
  328.1 1.8 collective-permute-start.54
  330.7 1.8 collective-permute-start.55
  336.7 1.8 collective-permute-start.56
  (6 other events, 95.5 us)

commit v8 on v6

--- a/solution.py
+++ b/solution.py
@@ -295,7 +295,7 @@
             name="back",
         )(attended, swapped(attended), hidden, mods, weights)
 
-    apart = 2
+    apart = 4
     held_pairs = [(at + 1, at) for at in range(apart, n_pipe, 2)]
     following = [next_mods, next_gains, lax.ppermute(held, "pipe", held_pairs)]
 

time: 438 us -> 428 us (0.977)
  blocking collectives: 89.4 us -> 78.8 us
    all_to_all x1, blocking collectives: 81.6 us -> 71.1 us  [shards(): got = lax.all_to_all(sent, 'pipe', 0, 0, tiled=True)]
    ppermute x12 -> x13, starting transfers between devices: 11.4 us -> 12.1 us  [shards(): hidden = lax.ppermute(hidden, 'pipe', [(holder, place)])]
    ppermute x12 -> x13, waiting for transfers between devices: 96 us -> 95.9 us  [shards(): hidden = lax.ppermute(hidden, 'pipe', [(holder, place)])]
  transfers between devices with their start and end apart: 59 -> 60, of which waited for: 42 -> 42; matrix products, arithmetic and copies ran while one was open for 1% -> 1% of each run, Pallas kernels for 10% -> 10%
where the time goes in v8:
time: 428 us; the launch traced here: 420 us
  waiting for transfers between devices  178 us (42%)
  Pallas kernels  85.2 us (20%)
  blocking collectives  78.8 us (18%)
  starting transfers between devices  67.6 us (16%)
  local copies, waits for them, and re-layouts  8.77 us (2%)
    ppermute x13, waiting for transfers between devices, shards(): hidden = lax.ppermute(hidden, 'pipe', [(holder, place)])  95.9 us
    all_to_all x1, blocking collectives, shards(): got = lax.all_to_all(sent, 'pipe', 0, 0, tiled=True)  71.1 us
    pallas_call x16, Pallas kernels, layer(): pl.pallas_call(layer_front(head_dim), out_shape=jax.ShapeDtypeStruct((tok...  66.2 us
    ppermute x33, waiting for transfers between devices, swapped(): return lax.ppermute(value, 'seq', core_pairs)  42.9 us
    ppermute x33, starting transfers between devices, swapped(): return lax.ppermute(value, 'seq', core_pairs)  24.4 us
    ppermute x3, waiting for transfers between devices, shards(): falling = lax.ppermute(falling, 'seq', rings[1])  20.8 us
    pallas_call x16, Pallas kernels, layer(): pl.pallas_call(layer_back, out_shape=jax.ShapeDtypeStruct((tokens, half),...  12.7 us
    ppermute x13, starting transfers between devices, shards(): hidden = lax.ppermute(hidden, 'pipe', [(holder, place)])  12.1 us
  transfers between devices with their start and end apart: 60, of which 42 were waited for; matrix products, arithmetic and copies ran while one was open for 1% of the time, Pallas kernels for 10%

profile of v8, /device:TPU:1, one launch (start us, length us, event | category | flops | bytes accessed | tf_op | source)
XLA Modules:
  0.0 419.7 jit_solution(12429782151779071326)
XLA Ops:
  1.1 3.3 collective-permute-start
  8.1 4.1 all-to-all-start
  12.3 3.1 collective-permute-done.1
  15.5 2.0 all-to-all-done
  17.4 5.6 %collective-permute-start.3 = (bf16[192,1536]{1,0:T(8,128)(2,1)S(1)}, bf16[192,1536]{1,0:T(8,128)(2,1)S(1)}, u32[]{:S(2)}, u32[]{:S(2)}) collective-permute-start(bf16[192,1536]{1,0:T(8,128)(2,1)S(1)} %pad_maximum_fusion.refs_0_), channel_id=1, source_target_pairs={{0,28},{1,29},{2,30},{3,31},{4,0},{5,1},{6,2},{7,3},{8,4},{9,5},{1... | collective-permute-start | bytes 1769480 | tf_op jit(solution)/shard_map/ppermute | solution.py:224
  23.0 10.6 %collective-permute-done.3.refs_2_ = bf16[192,1536]{1,0:T(8,128)(2,1)S(1)} collective-permute-done((bf16[192,1536]{1,0:T(8,128)(2,1)S(1)}, bf16[192,1536]{1,0:T(8,128)(2,1)S(1)}, u32[]{:S(2)}, u32[]{:S(2)}) %collective-permute-start.3) | collective-permute-done | bytes 589856 | tf_op jit(solution)/shard_map/ppermute | solution.py:224
  33.6 3.1 collective-permute-done.2.refs_1_
  38.2 10.2 %collective-permute-done.6.refs_4_ = bf16[192,1536]{1,0:T(8,128)(2,1)} collective-permute-done((bf16[192,1536]{1,0:T(8,128)(2,1)S(1)}, bf16[192,1536]{1,0:T(8,128)(2,1)}, u32[]{:S(2)}, u32[]{:S(2)}) %collective-permute-start.6) | collective-permute-done | bytes 589856 | tf_op jit(solution)/shard_map/ppermute | solution.py:224
  48.4 1.8 collective-permute-start.8
  51.2 10.1 %all-to-all-start.1 = ((bf16[32,8,768]{2,1,0:T(8,128)(2,1)}), bf16[32,8,768]{2,1,0:T(8,128)(2,1)S(1)}, u32[]{:S(2)}, u32[]{:S(2)}) async-start(bf16[32,8,768]{2,1,0:T(8,128)(2,1)} %bitcast.10), calls=%async_computation.1 | async-start | bytes 786432 | tf_op jit(solution)/shard_map/all_to_all | solution.py:240
  63.4 2.7 collective-permute-start.10
  68.2 8.5 %all-to-all-done.1 = bf16[32,8,768]{2,1,0:T(8,128)(2,1)S(1)} async-done(((bf16[32,8,768]{2,1,0:T(8,128)(2,1)}), bf16[32,8,768]{2,1,0:T(8,128)(2,1)S(1)}, u32[]{:S(2)}, u32[]{:S(2)}) %all-to-all-start.1) | async-done | bytes 393248 | tf_op jit(solution)/shard_map/all_to_all | solution.py:240
  77.4 1.6 collective-permute-done.10.refs_8_
  79.0 4.5 %load_own.1 = (bf16[1536,3072]{1,0:T(8,128)(2,1)S(1)}, f32[2,128]{1,0:T(2,128)S(1)}, f32[2,128]{1,0:T(2,128)S(1)}, f32[6,768]{1,0:T(8,128)S(1)}, f32[6,768]{1,0:T(8,128)S(1)}, /*index=5*/f32[6,768]{1,0:T(8,128)S(1)}) custom-call(s32[3]{0:T(128)S(1)} %pad_add_fusion.word_ref, bf16[192,1536]{1,0:T(8,128)(2,1)} %copy-done.6, bf16[192,1536]{1,0:T(8,128)(2,1)} %copy-done.10, ...), custom_call_target="tpu_custom_call" | custom-call | tf_op jit(solution)/shard_map/load_own/pallas_call | solution.py:258
  83.5 1.5 collective-permute-start.36
  85.0 4.1 front.16.own_ref
  89.1 3.3 collective-permute-start.13
  92.4 1.3 collective-permute-done.13.other_ref
  94.6 2.6 collective-permute-start.14
  97.2 8.1 %collective-permute-done.14.own_ref.hidden_ref = bf16[256,768]{1,0:T(8,128)(2,1)S(1)} collective-permute-done((bf16[256,768]{1,0:T(8,128)(2,1)S(1)}, bf16[256,768]{1,0:T(8,128)(2,1)S(1)}, u32[]{:S(2)}, u32[]{:S(2)}) %collective-permute-start.14) | collective-permute-done | bytes 393248 | tf_op jit(solution)/shard_map/ppermute | solution.py:309
  106.5 1.3 collective-permute-done.15.other_ref
  107.9 4.1 front.17.own_ref
  112.5 1.4 collective-permute-done.16.other_ref
  116.2 1.4 collective-permute-done.18.other_ref
  117.5 4.1 front.18.own_ref
  122.1 1.4 collective-permute-done.19.other_ref
  125.5 1.4 collective-permute-done.21.other_ref
  126.8 4.1 front.19.own_ref
  131.4 1.4 collective-permute-done.22.other_ref
  134.9 1.4 collective-permute-done.24.other_ref
  136.3 4.1 front.20.own_ref
  140.9 1.4 collective-permute-done.25.other_ref
  144.2 1.4 collective-permute-done.27.other_ref
  145.5 4.1 front.21.own_ref
  150.1 1.4 collective-permute-done.28.other_ref
  153.7 1.4 collective-permute-done.30.other_ref
  155.0 4.1 front.22.own_ref
  159.6 1.4 collective-permute-done.31.other_ref
  162.9 1.4 collective-permute-done.33.other_ref
  164.3 4.1 front.23.own_ref
  168.9 1.4 collective-permute-done.34.other_ref
  172.4 79.4 %collective-permute-done.35.hidden_ref = bf16[256,768]{1,0:T(8,128)(2,1)S(1)} collective-permute-done((bf16[256,768]{1,0:T(8,128)(2,1)S(1)}, bf16[256,768]{1,0:T(8,128)(2,1)S(1)}, u32[]{:S(2)}, u32[]{:S(2)}) %collective-permute-start.35) | collective-permute-done | bytes 393248 | tf_op jit(solution)/shard_map/ppermute | solution.py:309
  252.4 1.4 collective-permute-start.37
  253.8 1.3 collective-permute-done.37.other_ref
  255.2 4.1 front.24.own_ref
  259.8 1.4 collective-permute-done.38.other_ref
  263.2 8.4 %collective-permute-done.39.own_ref.hidden_ref = bf16[256,768]{1,0:T(8,128)(2,1)S(1)} collective-permute-done((bf16[256,768]{1,0:T(8,128)(2,1)S(1)}, bf16[256,768]{1,0:T(8,128)(2,1)S(1)}, u32[]{:S(2)}, u32[]{:S(2)}) %collective-permute-start.39) | collective-permute-done | bytes 393248 | tf_op jit(solution)/shard_map/ppermute | solution.py:309
  273.9 4.1 front.25.own_ref
  283.3 4.1 front.26.own_ref
  292.6 4.1 front.27.own_ref
  302.1 4.1 front.28.own_ref
  306.7 1.4 collective-permute-done.50.other_ref
  309.3 1.4 collective-permute-done.51.other_ref
  310.6 4.1 front.29.own_ref
  315.2 1.4 collective-permute-done.52.other_ref
  318.8 1.4 collective-permute-done.54.other_ref
  320.1 4.1 front.30.own_ref
  324.7 1.4 collective-permute-done.55.other_ref
  327.4 1.4 collective-permute-done.56.other_ref
  328.7 4.1 front.31.own_ref
  333.3 1.4 collective-permute-done.57.other_ref
  334.7 3.7 copy-done.1
  339.2 7.7 %all_to_all.20 = bf16[4,8,768]{2,1,0:T(8,128)(2,1)S(1)} all-to-all(bf16[4,8,768]{2,1,0:T(8,128)(2,1)S(1)} %fusion), channel_id=1, replica_groups={{0,1,2,3},{4,5,6,7},{8,9,10,11},{12,13,14,15},{16,17,18,19},{20,21,22,2..., dimensions={0} | all-to-all | bytes 98304 | tf_op jit(solution)/shard_map/all_to_all | solution.py:327
  347.1 71.1 %all_to_all.21.got_ref = bf16[8,2,8,192]{3,2,1,0:T(8,128)(2,1)S(1)} all-to-all(bf16[8,2,8,192]{3,2,1,0:T(8,128)(2,1)S(1)} %bitcast.28), channel_id=1, replica_groups=mesh['pipe'=8,'seq'=32] {'pipe'}, dimensions={0} | all-to-all | bytes 98304 | tf_op jit(solution)/shard_map/all_to_all | solution.py:332
  (133 shorter events, 61.6 us)
Async XLA Ops:
  0.0 66.9 %copy-start.5 = (f32[1,2,128]{2,1,0:T(2,128)S(1)}, f32[1,2,128]{2,1,0:T(2,128)}, u32[]{:S(2)}) copy-start(f32[1,2,128]{2,1,0:T(2,128)} %refs_11_.1) | copy-start | bytes 3076
  0.0 79.0 %copy-start.3 = (s32[2,2]{1,0:T(2,128)S(1)}, s32[2,2]{1,0:T(2,128)}, u32[]{:S(2)}) copy-start(s32[2,2]{1,0:T(2,128)} %time_ref.3) | copy-start | bytes 52
  1.1 4.3 %collective-permute-start = (bf16[48,1536]{1,0:T(8,128)(2,1)S(1)}, bf16[48,1536]{1,0:T(8,128)(2,1)S(1)}, u32[]{:S(2)}, u32[]{:S(2)}) collective-permute-start(bf16[48,1536]{1,0:T(8,128)(2,1)S(1)} %pad_maximum_fusion.3), channel_id=1, source_target_pairs={{0,1},{1,0},{2,3},{3,2},{4,5},{5,4},{6,7},{7,6},{8,9},{9,8},{10,11... | collective-permute-start | bytes 442376 | tf_op jit(solution)/shard_map/ppermute | solution.py:188
  5.5 9.8 %collective-permute-start.1 = (bf16[96,1536]{1,0:T(8,128)(2,1)S(1)}, bf16[96,1536]{1,0:T(8,128)(2,1)S(1)}, u32[]{:S(2)}, u32[]{:S(2)}) collective-permute-start(bf16[96,1536]{1,0:T(8,128)(2,1)S(1)} %pad_maximum_fusion.1), channel_id=1, source_target_pairs={{0,2},{1,3},{2,0},{3,1},{4,6},{5,7},{6,4},{7,5},{8,10},{9,11},{10,... | collective-permute-start | bytes 884744 | tf_op jit(solution)/shard_map/ppermute | solution.py:203
  8.1 9.3 %all-to-all-start = ((bf16[8,2,8,192]{3,2,1,0:T(8,128)(2,1)}), bf16[8,2,8,192]{3,2,1,0:T(8,128)(2,1)S(1)}, u32[]{:S(2)}, u32[]{:S(2)}) async-start(bf16[8,2,8,192]{3,2,1,0:T(8,128)(2,1)} %broadcast_in_dim.6), calls=%async_computation | async-start | bytes 131072 | tf_op jit(solution)/shard_map/all_to_all | solution.py:206
  17.4 16.2 %collective-permute-start.3 = (bf16[192,1536]{1,0:T(8,128)(2,1)S(1)}, bf16[192,1536]{1,0:T(8,128)(2,1)S(1)}, u32[]{:S(2)}, u32[]{:S(2)}) collective-permute-start(bf16[192,1536]{1,0:T(8,128)(2,1)S(1)} %pad_maximum_fusion.refs_0_), channel_id=1, source_target_pairs={{0,28},{1,29},{2,30},{3,31},{4,0},{5,1},{6,2},{7,3},{8,4},{9,5},{1... | collective-permute-start | bytes 1769480 | tf_op jit(solution)/shard_map/ppermute | solution.py:224
  23.0 13.7 %collective-permute-start.2 = (bf16[192,1536]{1,0:T(8,128)(2,1)S(1)}, bf16[192,1536]{1,0:T(8,128)(2,1)S(1)}, u32[]{:S(2)}, u32[]{:S(2)}) collective-permute-start(bf16[192,1536]{1,0:T(8,128)(2,1)S(1)} %pad_maximum_fusion.refs_0_), channel_id=1, source_target_pairs={{0,4},{1,5},{2,6},{3,7},{4,8},{5,9},{6,10},{7,11},{8,12},{9,13},{1... | collective-permute-start | bytes 1769480 | tf_op jit(solution)/shard_map/ppermute | solution.py:223
  36.7 11.7 %collective-permute-start.6 = (bf16[192,1536]{1,0:T(8,128)(2,1)S(1)}, bf16[192,1536]{1,0:T(8,128)(2,1)}, u32[]{:S(2)}, u32[]{:S(2)}) collective-permute-start(bf16[192,1536]{1,0:T(8,128)(2,1)S(1)} %collective-permute-done.3.refs_2_), channel_id=1, source_target_pairs={{0,28},{1,29},{2,30},{3,31},{4,0},{5,1},{6,2},{7,3},{8,4},{9,5},{1... | collective-permute-start | bytes 1769480 | tf_op jit(solution)/shard_map/ppermute | solution.py:224
  37.1 13.2 %collective-permute-start.5 = (bf16[192,1536]{1,0:T(8,128)(2,1)S(1)}, bf16[192,1536]{1,0:T(8,128)(2,1)}, u32[]{:S(2)}, u32[]{:S(2)}) collective-permute-start(bf16[192,1536]{1,0:T(8,128)(2,1)S(1)} %collective-permute-done.2.refs_1_), channel_id=1, source_target_pairs={{0,4},{1,5},{2,6},{3,7},{4,8},{5,9},{6,10},{7,11},{8,12},{9,13},{1... | collective-permute-start | bytes 1769480 | tf_op jit(solution)/shard_map/ppermute | solution.py:223
  48.4 14.3 %collective-permute-start.8 = (bf16[192,1536]{1,0:T(8,128)(2,1)}, bf16[192,1536]{1,0:T(8,128)(2,1)S(1)}, u32[]{:S(2)}, u32[]{:S(2)}) collective-permute-start(bf16[192,1536]{1,0:T(8,128)(2,1)} %collective-permute-done.6.refs_4_), channel_id=1, source_target_pairs={{0,28},{1,29},{2,30},{3,31},{4,0},{5,1},{6,2},{7,3},{8,4},{9,5},{1... | collective-permute-start | bytes 1769480 | tf_op jit(solution)/shard_map/ppermute | solution.py:224
  50.3 15.9 %collective-permute-start.7 = (bf16[192,1536]{1,0:T(8,128)(2,1)}, bf16[192,1536]{1,0:T(8,128)(2,1)S(1)}, u32[]{:S(2)}, u32[]{:S(2)}) collective-permute-start(bf16[192,1536]{1,0:T(8,128)(2,1)} %collective-permute-done.5.refs_3_), channel_id=1, source_target_pairs={{0,4},{1,5},{2,6},{3,7},{4,8},{5,9},{6,10},{7,11},{8,12},{9,13},{1... | collective-permute-start | bytes 1769480 | tf_op jit(solution)/shard_map/ppermute | solution.py:223
  51.2 25.5 %all-to-all-start.1 = ((bf16[32,8,768]{2,1,0:T(8,128)(2,1)}), bf16[32,8,768]{2,1,0:T(8,128)(2,1)S(1)}, u32[]{:S(2)}, u32[]{:S(2)}) async-start(bf16[32,8,768]{2,1,0:T(8,128)(2,1)} %bitcast.10), calls=%async_computation.1 | async-start | bytes 786432 | tf_op jit(solution)/shard_map/all_to_all | solution.py:240
  61.3 16.0 %collective-permute-start.11 = (f32[1,16,4608]{2,1,0:T(8,128)S(1)}, f32[1,16,4608]{2,1,0:T(8,128)S(1)}, u32[]{:S(2)}, u32[]{:S(2)}) collective-permute-start(f32[1,16,4608]{2,1,0:T(8,128)S(1)} %copy-done.2), channel_id=1, source_target_pairs={{32,0},{96,64},{160,128},{224,192},{33,1},{97,65},{161,129},{225,1... | collective-permute-start | bytes 884744 | tf_op jit(solution)/shard_map/ppermute | solution.py:213
  63.4 15.5 %collective-permute-start.10 = (bf16[96,1536]{1,0:T(8,128)(2,1)}, bf16[96,1536]{1,0:T(8,128)(2,1)}, u32[]{:S(2)}, u32[]{:S(2)}) collective-permute-start(bf16[96,1536]{1,0:T(8,128)(2,1)} %slice.19), channel_id=1, source_target_pairs={{0,28},{1,29},{2,30},{3,31},{4,0},{5,1},{6,2},{7,3},{8,4},{9,5},{1... | collective-permute-start | bytes 884744 | tf_op jit(solution)/shard_map/ppermute | solution.py:231
  66.9 12.1 %collective-permute-start.9 = (bf16[96,1536]{1,0:T(8,128)(2,1)}, bf16[96,1536]{1,0:T(8,128)(2,1)}, u32[]{:S(2)}, u32[]{:S(2)}) collective-permute-start(bf16[96,1536]{1,0:T(8,128)(2,1)} %slice.18), channel_id=1, source_target_pairs={{0,4},{1,5},{2,6},{3,7},{4,8},{5,9},{6,10},{7,11},{8,12},{9,13},{1... | collective-permute-start | bytes 884744 | tf_op jit(solution)/shard_map/ppermute | solution.py:230
  66.9 10.4 %collective-permute-start.12 = (f32[1,2,128]{2,1,0:T(2,128)S(1)}, f32[1,2,128]{2,1,0:T(2,128)S(1)}, u32[]{:S(2)}, u32[]{:S(2)}) collective-permute-start(f32[1,2,128]{2,1,0:T(2,128)S(1)} %copy-done.5), channel_id=1, source_target_pairs={{32,0},{96,64},{160,128},{224,192},{33,1},{97,65},{161,129},{225,1... | collective-permute-start | bytes 3080 | tf_op jit(solution)/shard_map/ppermute | solution.py:213
  76.8 8.2 %collective-permute-start.4 = (bf16[256,768]{1,0:T(8,128)(2,1)S(1)}, bf16[256,768]{1,0:T(8,128)(2,1)S(1)}, u32[]{:S(2)}, u32[]{:S(2)}) collective-permute-start(bf16[256,768]{1,0:T(8,128)(2,1)S(1)} %bitcast.22), channel_id=1, source_target_pairs={{0,1},{1,0},{2,3},{3,2},{4,5},{5,4},{6,7},{7,6},{8,9},{9,8},{10,11... | collective-permute-start | bytes 1179656 | tf_op jit(solution)/shard_map/ppermute | solution.py:188
  83.5 168.3 %collective-permute-start.36 = (bf16[1536,3072]{1,0:T(8,128)(2,1)S(1)}, bf16[1536,3072]{1,0:T(8,128)(2,1)S(1)}, u32[]{:S(2)}, u32[]{:S(2)}) collective-permute-start(bf16[1536,3072]{1,0:T(8,128)(2,1)S(1)} %get-tuple-element.35.weight_ref), channel_id=1, source_target_pairs={{160,128},{224,192},{161,129},{225,193},{162,130},{226,194},{163,1... | collective-permute-start | bytes 28311560 | tf_op jit(solution)/shard_map/ppermute | solution.py:300
  89.1 4.7 %collective-permute-start.13 = (bf16[256,768]{1,0:T(8,128)(2,1)S(1)}, bf16[256,768]{1,0:T(8,128)(2,1)S(1)}, u32[]{:S(2)}, u32[]{:S(2)}) collective-permute-start(bf16[256,768]{1,0:T(8,128)(2,1)S(1)} %front.16.own_ref), channel_id=1, source_target_pairs={{0,1},{1,0},{2,3},{3,2},{4,5},{5,4},{6,7},{7,6},{8,9},{9,8},{10,11... | collective-permute-start | bytes 1179656 | tf_op jit(solution)/shard_map/ppermute | solution.py:188
  94.6 10.7 %collective-permute-start.14 = (bf16[256,768]{1,0:T(8,128)(2,1)S(1)}, bf16[256,768]{1,0:T(8,128)(2,1)S(1)}, u32[]{:S(2)}, u32[]{:S(2)}) collective-permute-start(bf16[256,768]{1,0:T(8,128)(2,1)S(1)} %back.16), channel_id=1, source_target_pairs={{0,32},{1,33},{2,34},{3,35},{4,36},{5,37},{6,38},{7,39},{8,40},{9,... | collective-permute-start | bytes 1179656 | tf_op jit(solution)/shard_map/ppermute | solution.py:309
  105.3 2.5 collective-permute-start.15
  112.0 1.8 collective-permute-start.16
  114.6 0.7 collective-permute-start.17
  115.3 2.2 collective-permute-start.18
  121.7 1.8 collective-permute-start.19
  124.3 0.7 collective-permute-start.20
  125.0 1.8 collective-permute-start.21
  131.0 1.8 collective-permute-start.22
  133.6 0.7 collective-permute-start.23
  134.3 2.0 collective-permute-start.24
  140.4 1.8 collective-permute-start.25
  143.0 0.7 collective-permute-start.26
  143.7 1.8 collective-permute-start.27
  149.7 1.8 collective-permute-start.28
  152.3 0.7 collective-permute-start.29
  153.0 2.0 collective-permute-start.30
  159.2 1.8 collective-permute-start.31
  161.8 0.7 collective-permute-start.32
  162.5 1.8 collective-permute-start.33
  168.4 83.3 %copy-start.4 = (f32[16]{0:T(128)S(1)}, f32[16]{0:T(128)}, u32[]{:S(2)}) copy-start(f32[16]{0:T(128)} %size_ref.3) | copy-start | bytes 196
  168.4 1.8 collective-permute-start.34
  171.1 80.7 %collective-permute-start.35 = (bf16[256,768]{1,0:T(8,128)(2,1)S(1)}, bf16[256,768]{1,0:T(8,128)(2,1)S(1)}, u32[]{:S(2)}, u32[]{:S(2)}) collective-permute-start(bf16[256,768]{1,0:T(8,128)(2,1)S(1)} %back.23), channel_id=1, source_target_pairs={{224,0},{225,1},{226,2},{227,3},{228,4},{229,5},{230,6},{231,7},{2... | collective-permute-start | bytes 1179656 | tf_op jit(solution)/shard_map/ppermute | solution.py:309
  251.8 77.0 %copy-start = (bf16[1536,3072]{1,0:T(8,128)(2,1)}, bf16[1536,3072]{1,0:T(8,128)(2,1)S(1)}, u32[]{:S(2)}) copy-start(bf16[1536,3072]{1,0:T(8,128)(2,1)S(1)} %collective-permute-done.36.weight_ref) | copy-start | bytes 28311556
  252.4 2.7 collective-permute-start.37
  259.3 1.8 collective-permute-start.38
  261.9 9.7 %collective-permute-start.39 = (bf16[256,768]{1,0:T(8,128)(2,1)S(1)}, bf16[256,768]{1,0:T(8,128)(2,1)S(1)}, u32[]{:S(2)}, u32[]{:S(2)}) collective-permute-start(bf16[256,768]{1,0:T(8,128)(2,1)S(1)} %back.24), channel_id=1, source_target_pairs={{0,32},{1,33},{2,34},{3,35},{4,36},{5,37},{6,38},{7,39},{8,40},{9,... | collective-permute-start | bytes 1179656 | tf_op jit(solution)/shard_map/ppermute | solution.py:309
  271.6 2.2 collective-permute-start.40
  278.0 1.8 collective-permute-start.41
  280.6 0.7 collective-permute-start.42
  281.3 2.0 collective-permute-start.43
  287.5 1.8 collective-permute-start.44
  290.1 0.7 collective-permute-start.45
  290.8 1.8 collective-permute-start.46
  296.7 1.8 collective-permute-start.47
  299.3 0.7 collective-permute-start.48
  300.0 2.0 collective-permute-start.49
  306.2 1.8 collective-permute-start.50
  308.8 1.8 collective-permute-start.51
  314.8 1.8 collective-permute-start.52
  317.4 0.7 collective-permute-start.53
  318.1 2.1 collective-permute-start.54
  324.3 1.8 collective-permute-start.55
  326.9 1.8 collective-permute-start.56
  332.9 1.8 collective-permute-start.57
  (7 other events, 204.6 us)
